TPU v7x, 256 devices: a whole 4x4x8 slice. The times are simulated.
256 devices in a mesh: blk: 16 (over x, y_lo, core), lane: 16 (over y_hi, z).
Axes of the slice: x: 4, y: 4 (y_hi: 2, y_lo: 2; y = y_hi * 2 + y_lo), z: 8, core: 2. Of those that a mesh axis runs over, the one named last changes fastest.
Arguments:
- recv_pos: float32 [3, 32768], P(None, ('blk', 'lane')), may hold values from 0 to 6
- recv_angles: float32 [2, 32768], P(None, ('blk', 'lane')), may hold values from -3.140625 to 3.140625
- src_pos: float32 [3, 262144], P(None, ('blk', 'lane')), may hold values from 0 to 6
- src_angles: float32 [2, 262144], P(None, ('blk', 'lane')), may hold values from -3.140625 to 3.140625
- src_area: float32 [262144], P(('blk', 'lane')), may hold values from 0.02 to 0.08
- reemission: float32 [262144], P(('blk', 'lane')), may hold values from 0.1 to 0.9
- incident: bfloat16 [262144, 128], P(('blk', 'lane')), may hold values from 0 to 2
- direct: float32 [32768, 128], P(('blk', 'lane')), may hold values from 0.5 to 1.5
- visible_lists: int32 [16, 16, 16, 16, 4], P('blk', 'lane'), may hold values from 0 to 7, as said below
- visible_counts: int32 [16, 16, 16, 16], P('blk', 'lane'), may hold values from 0 to 4, as said below
Outputs:
- incoming: float32 [32768, 128], P(('blk', 'lane'))
Inputs may be any that keep to these rules, and one draw needn't show every extreme that they name: `visible_lists`: each list names 4 different local source blocks of its device; entries at slots at or past the count are valid but unused. `visible_counts`: some list holds exactly 4 used entries in every draw; the loads differ from device to device.
All inputs are finite; a program needn't handle non-finite values.
Results may differ from a plain program's by a relative error of at most 0.0003.
Values sent between devices are 32-bit elements; how exact they have to be, the bound alone decides.
No kernel may reach another device: no remote copies, remote signals or barrier semaphores. Data moves between devices by JAX's collectives and lax.ppermute only.
A program may use at most 64 MiB of HBM per device.

v0:
```python
import jax
import jax.numpy as jnp
from jax import lax
from jax.sharding import PartitionSpec as P


def shifted(block, axis, distance):
    devices = range(lax.axis_size(axis))
    route = [((i - distance) % len(devices), i) for i in devices]
    return lax.ppermute(block, axis, route)


def normals(angle_rows):
    polar = angle_rows[0]
    azimuth = angle_rows[1]
    return jnp.stack(
        [jnp.sin(polar) * jnp.cos(azimuth), jnp.sin(polar) * jnp.sin(azimuth), jnp.cos(polar)]
    )


def factors(receiver_pos, receiver_dir, source_pos, source_dir, source_area, source_keep):
    offsets = [source_pos[component] - receiver_pos[component] for component in range(3)]
    distance = offsets[0] * offsets[0] + offsets[1] * offsets[1] + offsets[2] * offsets[2]
    facing = jnp.maximum(
        receiver_dir[0] * offsets[0] + receiver_dir[1] * offsets[1] + receiver_dir[2] * offsets[2],
        0.0,
    )
    seen = jnp.maximum(
        -(source_dir[0] * offsets[0] + source_dir[1] * offsets[1] + source_dir[2] * offsets[2]), 0.0
    )
    spread = distance + source_area
    value = source_keep * source_area * facing * seen / (jnp.pi * spread * spread)
    return value.astype(jnp.bfloat16)


def shards(
    recv_pos,
    recv_angles,
    src_pos,
    src_angles,
    src_area,
    reemission,
    incident,
    direct,
    visible_lists,
    visible_counts,
):
    group_count = lax.axis_size("blk")
    lane_count = lax.axis_size("lane")
    block_rows = recv_pos.shape[1]
    bin_count = incident.shape[1]
    source_blocks = src_area.shape[0] // block_rows
    slot_count = visible_lists.shape[-1]
    every_pos, every_angles = (
        lax.all_gather(recv_pos, ("blk", "lane"), axis=1, tiled=True),
        lax.all_gather(recv_angles, ("blk", "lane"), axis=1, tiled=True),
    )
    receiver_pos = every_pos.reshape(3, group_count * lane_count, block_rows)
    receiver_dir = normals(every_angles).reshape(3, group_count * lane_count, block_rows)
    source_pos = src_pos.reshape(3, source_blocks, block_rows)
    source_dir = normals(src_angles).reshape(3, source_blocks, block_rows)
    source_area = src_area.reshape(source_blocks, block_rows)
    source_keep = reemission.reshape(source_blocks, block_rows)
    emission = incident.reshape(source_blocks, block_rows, bin_count)
    my_lists = visible_lists[0, 0]
    my_counts = visible_counts[0, 0]
    group_index = lax.axis_index("blk")
    lane_range = jnp.arange(lane_count, dtype=jnp.int32)
    slot_range = jnp.arange(slot_count, dtype=jnp.int32)

    def slab_of(cycle_step):
        ahead = (group_index - cycle_step - 1) % group_count
        return ahead + 0 * lane_range

    def contribution(cycle_step):
        slabs = slab_of(cycle_step)
        targets = slabs * lane_count + lane_range
        near_pos = jnp.take(receiver_pos, targets, axis=1)
        near_dir = jnp.take(receiver_dir, targets, axis=1)
        chosen = my_lists[slabs, lane_range]
        counts_here = my_counts[slabs, lane_range]
        picked_pos = source_pos[:, chosen]
        picked_dir = source_dir[:, chosen]
        picked_area = source_area[chosen]
        picked_keep = source_keep[chosen]
        picked_flux = emission[chosen]
        values = factors(
            near_pos[:, :, :, None, None],
            near_dir[:, :, :, None, None],
            picked_pos[:, :, None, :, :],
            picked_dir[:, :, None, :, :],
            picked_area[:, None, :, :],
            picked_keep[:, None, :, :],
        )
        live_mask = (slot_range[None, :] < counts_here[:, None])[:, None, :, None]
        values = jnp.where(live_mask, values, jnp.zeros((), jnp.bfloat16))
        return jnp.einsum("jrcs,jcsb->jrb", values, picked_flux, preferred_element_type=jnp.float32)

    def pass_on(running):
        return shifted(running, "blk", 1)

    def cycle_turn(cycle_step, running):
        return pass_on(running + contribution(cycle_step))

    start = jnp.zeros((lane_count, block_rows, bin_count), jnp.float32)
    running = lax.fori_loop(0, group_count - 1, cycle_turn, start)
    running = running + contribution(group_count - 1)
    owned = lax.psum_scatter(
        running.reshape(lane_count * block_rows, bin_count), "lane", scatter_dimension=0, tiled=True
    )
    return direct + owned


def solution(mesh):
    return jax.shard_map(
        shards,
        mesh=mesh,
        in_specs=(
            P(None, ("blk", "lane")),
            P(None, ("blk", "lane")),
            P(None, ("blk", "lane")),
            P(None, ("blk", "lane")),
            P(("blk", "lane")),
            P(("blk", "lane")),
            P(("blk", "lane"), None),
            P(("blk", "lane"), None),
            P("blk", "lane", None, None, None),
            P("blk", "lane", None, None),
        ),
        out_specs=P(("blk", "lane"), None),
        check_vma=False,
    )
```

profile of v0, /device:TPU:6, one launch (start us, length us, event | category | flops | bytes accessed | tf_op | source)
XLA Modules:
  0.0 2028.7 jit_solution(4897555335530008646)
XLA Ops:
  7.5 562.4 %all_gather.6 = f32[2,32768]{1,0:T(2,128)S(1)} all-gather(f32[2,128]{1,0:T(2,128)} %param.15), channel_id=1, replica_groups=mesh['blk'=16,'lane'=16] {'blk','lane'}, dimensions={1}, use_global_device_ids=true | all-gather | bytes 263168 | tf_op jit(solution)/shard_map/all_gather | solution.py:56
  577.4 600.4 %all_gather.7 = f32[3,32768]{1,0:T(4,128)} all-gather(f32[3,128]{1,0:T(4,128)} %param.14), channel_id=1, replica_groups=mesh['blk'=16,'lane'=16] {'blk','lane'}, dimensions={1}, use_global_device_ids=true | all-gather | bytes 394752 | tf_op jit(solution)/shard_map/all_gather | solution.py:55
  1191.7 594.5 %while.17 = (s32[]{:T(128)}, f32[16,128,128]{2,1,0:T(8,128)}, s32[]{:T(128)}, s32[16,16]{1,0:T(8,128)S(1)}, s32[16,16,4]{2,1,0:T(8,128)S(1)}, /*index=5*/f32[8,1...) while((s32[]{:T(128)}, f32[16,128,128]{2,1,0:T(8,128)}, ...), condition=%wide.region_1.3_spmd.clone.clone, body=%wide.region_0.2_spmd.clone.clone.sunk | while | flops 299129344 | bytes 18412892 | solution.py:106
  1199.4 8.1 fusion.118
  1213.8 9.1 collective-permute-done
  1231.6 8.1 fusion.118
  1239.7 50.0 %collective-permute-start = (f32[16,128,128]{2,1,0:T(8,128)}, f32[16,128,128]{2,1,0:T(8,128)S(1)}, u32[]{:S(2)}, u32[]{:S(2)}) collective-permute-start(f32[16,128,128]{2,1,0:T(8,128)} %fusion.118), channel_id=1, source_target_pairs={{240,0},{0,16},{16,32},{32,48},{48,64},{64,80},{80,96},{96,112},{1... | collective-permute-start | bytes 3145736 | tf_op jit(solution)/shard_map/while/body/eval_jaxpr/ppermute | solution.py:10
  1300.9 8.1 fusion.118
  1309.0 31.3 %collective-permute-start = (f32[16,128,128]{2,1,0:T(8,128)}, f32[16,128,128]{2,1,0:T(8,128)S(1)}, u32[]{:S(2)}, u32[]{:S(2)}) collective-permute-start(f32[16,128,128]{2,1,0:T(8,128)} %fusion.118), channel_id=1, source_target_pairs={{240,0},{0,16},{16,32},{32,48},{48,64},{64,80},{80,96},{96,112},{1... | collective-permute-start | bytes 3145736 | tf_op jit(solution)/shard_map/while/body/eval_jaxpr/ppermute | solution.py:10
  1351.4 8.1 fusion.118
  1359.5 56.5 %collective-permute-start = (f32[16,128,128]{2,1,0:T(8,128)}, f32[16,128,128]{2,1,0:T(8,128)S(1)}, u32[]{:S(2)}, u32[]{:S(2)}) collective-permute-start(f32[16,128,128]{2,1,0:T(8,128)} %fusion.118), channel_id=1, source_target_pairs={{240,0},{0,16},{16,32},{32,48},{48,64},{64,80},{80,96},{96,112},{1... | collective-permute-start | bytes 3145736 | tf_op jit(solution)/shard_map/while/body/eval_jaxpr/ppermute | solution.py:10
  1427.2 8.1 fusion.118
  1435.3 14.1 collective-permute-start
  1460.5 8.1 fusion.118
  1468.6 14.0 collective-permute-start
  1493.9 8.1 fusion.118
  1502.0 14.1 collective-permute-start
  1527.2 8.1 fusion.118
  1535.3 14.0 collective-permute-start
  1560.5 8.1 fusion.118
  1568.6 14.0 collective-permute-start
  1593.9 8.1 fusion.118
  1602.0 14.0 collective-permute-start
  1635.3 14.0 collective-permute-start
  1668.6 14.0 collective-permute-start
  1693.9 8.1 fusion.118
  1702.0 14.0 collective-permute-start
  1727.2 8.1 fusion.118
  1735.3 14.0 collective-permute-start
  1760.5 8.1 fusion.118
  1768.6 14.0 collective-permute-start
  1793.5 226.9 %reduce-scatter.2.cloned.1.call-done = f32[128,128]{1,0:T(8,128)} async-done(((f32[2048,128]{1,0:T(8,128)}), f32[128,128]{1,0:T(8,128)}) %reduce-scatter.2.cloned.1.call-update) | async-done | bytes 65552 | tf_op jit(solution)/shard_map/reduce_scatter | solution.py:108
  (455 shorter events, 217.4 us)
Async XLA Ops:
  6.5 1173.2 %copy-start.1 = (bf16[1024,128]{1,0:T(8,128)(2,1)S(1)}, bf16[1024,128]{1,0:T(8,128)(2,1)}, u32[]{:S(2)}) copy-start(bf16[1024,128]{1,0:T(8,128)(2,1)} %param.20) | copy-start | bytes 786436
  6.5 2013.9 %reduce-scatter.2.cloned.1.call-start = ((), (), s32[]{:S(2)}) async-start(), calls=%async_computation.1 | async-start | bytes 1114112 | tf_op jit(solution)/shard_map/reduce_scatter | solution.py:108
  1179.8 2.2 copy-start.3
  1179.8 6.7 copy-start.4
  1181.9 5.9 copy-start.2
  1181.9 6.5 copy-start
  1182.5 9.1 copy-start.6
  1207.5 15.4 collective-permute-start
  1222.9 1.0 copy-start.5
  1239.7 52.5 %collective-permute-start = (f32[16,128,128]{2,1,0:T(8,128)}, f32[16,128,128]{2,1,0:T(8,128)S(1)}, u32[]{:S(2)}, u32[]{:S(2)}) collective-permute-start(f32[16,128,128]{2,1,0:T(8,128)} %fusion.118), channel_id=1, source_target_pairs={{240,0},{0,16},{16,32},{32,48},{48,64},{64,80},{80,96},{96,112},{1... | collective-permute-start | bytes 3145736 | tf_op jit(solution)/shard_map/while/body/eval_jaxpr/ppermute | solution.py:10
  1292.2 1.0 copy-start.5
  1309.0 33.8 %collective-permute-start = (f32[16,128,128]{2,1,0:T(8,128)}, f32[16,128,128]{2,1,0:T(8,128)S(1)}, u32[]{:S(2)}, u32[]{:S(2)}) collective-permute-start(f32[16,128,128]{2,1,0:T(8,128)} %fusion.118), channel_id=1, source_target_pairs={{240,0},{0,16},{16,32},{32,48},{48,64},{64,80},{80,96},{96,112},{1... | collective-permute-start | bytes 3145736 | tf_op jit(solution)/shard_map/while/body/eval_jaxpr/ppermute | solution.py:10
  1342.8 1.0 copy-start.5
  1359.5 59.0 %collective-permute-start = (f32[16,128,128]{2,1,0:T(8,128)}, f32[16,128,128]{2,1,0:T(8,128)S(1)}, u32[]{:S(2)}, u32[]{:S(2)}) collective-permute-start(f32[16,128,128]{2,1,0:T(8,128)} %fusion.118), channel_id=1, source_target_pairs={{240,0},{0,16},{16,32},{32,48},{48,64},{64,80},{80,96},{96,112},{1... | collective-permute-start | bytes 3145736 | tf_op jit(solution)/shard_map/while/body/eval_jaxpr/ppermute | solution.py:10
  1418.5 1.0 copy-start.5
  1435.3 16.6 collective-permute-start
  1451.9 1.0 copy-start.5
  1468.6 16.5 collective-permute-start
  1485.2 1.0 copy-start.5
  1502.0 16.5 collective-permute-start
  1518.5 1.0 copy-start.5
  1535.3 16.5 collective-permute-start
  1551.9 1.0 copy-start.5
  1568.6 16.5 collective-permute-start
  1585.2 1.0 copy-start.5
  1602.0 16.5 collective-permute-start
  1635.3 16.5 collective-permute-start
  1668.6 16.5 collective-permute-start
  1702.0 16.5 collective-permute-start
  1735.3 16.5 collective-permute-start
  1768.6 16.5 collective-permute-start
  1786.2 234.2 %copy-start.7 = (f32[128,128]{1,0:T(8,128)S(1)}, f32[128,128]{1,0:T(8,128)}, u32[]{:S(2)}) copy-start(f32[128,128]{1,0:T(8,128)} %param.21) | copy-start | bytes 196612
  (6 other events, 6.0 us)
Sparse Core Ops, SparseCore 0:
  1793.6 226.7 reduce-scatter.1
where the time goes:
time: 2030 us
  blocking collectives  1160 us (57%)
  starting transfers between devices  299 us (15%)
  waiting for transfers between devices  271 us (13%)
  local copies, waits for them, and re-layouts  138 us (7%)
  matrix products  129 us (6%)
    all_gather x1, blocking collectives, shards(): lax.all_gather(recv_pos, ('blk', 'lane'), axis=1, tiled=True)  600 us
    all_gather x1, blocking collectives, shards(): lax.all_gather(recv_angles, ('blk', 'lane'), axis=1, tiled=True)  562 us
    ppermute x15, starting transfers between devices, shifted(): return lax.ppermute(block, axis, route)  299 us
    reduce_scatter x1, waiting for transfers between devices, shards(): lax.psum_scatter(running.reshape(lane_count * block_rows, bin_count), 'la...  227 us
    dot_general x16, matrix products, contribution(): jnp.einsum('jrcs,jcsb->jrb', values, picked_flux, preferred_element_type=...  129 us
    ppermute x15, waiting for transfers between devices, shifted(): return lax.ppermute(block, axis, route)  44.1 us
  transfers between devices with their start and end apart: 16, of which 16 were waited for; matrix products, arithmetic and copies ran while one was open for 0% of the time, Pallas kernels for 0%

commit v1 on v0

v1 whole, which is shorter than its diff:
```python
import functools

import jax
import jax.numpy as jnp
import numpy as np
from jax import lax
from jax.experimental import pallas as pl
from jax.experimental.pallas import tpu as pltpu
from jax.sharding import Mesh
from jax.sharding import PartitionSpec as P

NX, NYL, NC, NYH, NZ = 4, 2, 2, 2, 8
NY = NYL * NYH
BS = 128
SB = 8
CAP = 4
GROUP = NX * NC
NJ = NY * NZ
NULL = GROUP * SB
CENTRE = 3.0
ROWS = 16
POS, NRM, DOT, SQA, SQB, ONE, LST = 0, 3, 6, 7, 8, 9, 10
KF, KS, KD = 32, 32, 48
UNROLL = 8


def selection_matrices():
    pieces = [(i, j) for i in range(3) for j in range(3) if i + j < 4]

    def build(depth, terms):
        recv = np.zeros((depth, 3 * ROWS), np.float32)
        src = np.zeros((depth, 3 * ROWS), np.float32)
        for at, (scale, ri, rrow, si, srow) in enumerate(terms):
            recv[at, ri * ROWS + rrow] = scale
            src[at, si * ROWS + srow] = 1.0
        return recv, src

    def product(scale, rrow, srow):
        return [(scale, i, rrow + a, j, srow + a) for i, j in pieces for a in range(3)]

    def from_recv(row, count):
        return [(1.0, i, row, 0, ONE) for i in range(count)]

    def from_src(row, count):
        return [(1.0, 0, ONE, i, row) for i in range(count)]

    facing = product(1.0, NRM, POS) + from_recv(DOT, 3)
    seen = product(1.0, POS, NRM) + from_src(DOT, 3)
    cross = product(-2.0, POS, POS)
    spread = (
        from_recv(SQA, 2) + from_src(SQA, 2) + cross + from_recv(SQB, 3) + from_src(SQB, 3)
    )
    return [build(KF, facing), build(KS, seen), build(KD, spread)]


def null_spread():
    column = np.zeros((KD, BS), np.float32)
    column[2, :] = 1.0
    return column


def split_pieces(tile):
    row = lax.broadcasted_iota(jnp.int32, tile.shape, 0)
    fixed = row < NRM
    high = jnp.where(fixed, jnp.round(tile * 32.0) * (1.0 / 32.0), tile).astype(jnp.bfloat16)
    rest = tile - high.astype(jnp.float32)
    mid = jnp.where(fixed, jnp.round(rest * 8192.0) * (1.0 / 8192.0), rest).astype(jnp.bfloat16)
    low = (rest - mid.astype(jnp.float32)).astype(jnp.bfloat16)
    return jnp.concatenate([high, mid, low], axis=0)


def dot(a, b):
    return jnp.dot(a, b, preferred_element_type=jnp.float32)


def recv_prep_kernel(tiles, mf, ms, md, rf, rs, rd):
    def one(j, carry):
        y, z = j // NZ, j % NZ
        at = (y % NYL) * (NYH * NZ) + (y // NYL) * NZ + z
        q = split_pieces(tiles[at])
        for m, out in ((mf, rf), (ms, rs), (md, rd)):
            out[j] = lax.dot_general(
                q, m[...], (((0,), (1,)), ((), ())), preferred_element_type=jnp.float32
            ).astype(jnp.bfloat16)
        return carry

    lax.fori_loop(0, NJ, one, 0)


def src_prep_kernel(*refs):
    packed = refs[:GROUP]
    mf, ms, md, nul, sf, ss, sd, em = refs[GROUP:]
    for d in range(GROUP):
        ref = packed[d]

        def one(k, carry, ref=ref, d=d):
            start = pl.multiple_of(k * BS, BS)
            em[d * SB + k] = ref[pl.ds(start, BS), :].astype(jnp.bfloat16)
            tile_at = pl.multiple_of(SB * BS + k * ROWS, ROWS)
            q = split_pieces(ref[pl.ds(tile_at, ROWS), :])
            for m, out in ((mf, sf), (ms, ss), (md, sd)):
                out[d * SB + k] = dot(m[...], q).astype(jnp.bfloat16)
            return carry

        lax.fori_loop(0, SB, one, 0)
    em[NULL] = jnp.zeros((BS, BS), jnp.bfloat16)
    sf[NULL] = jnp.zeros((KF, BS), jnp.bfloat16)
    ss[NULL] = jnp.zeros((KS, BS), jnp.bfloat16)
    sd[NULL] = nul[...]


def sweep_kernel(first, lists, rf, rs, rd, sf, ss, sd, em, out, ids, owner):
    base = first[0]
    out[...] = jnp.zeros(out.shape, out.dtype)

    def one_block(j, n):
        def one_entry(t, n):
            value = lists[(t // CAP) * BS + (base + j) * CAP + t % CAP]
            ids[n] = (t // CAP) * SB + value
            owner[n // 2] = j
            return n + (value >= 0).astype(jnp.int32)

        n = lax.fori_loop(0, GROUP * CAP, one_entry, n, unroll=8)
        ids[n] = NULL
        return n + n % 2

    n = lax.fori_loop(0, NZ, one_block, 0)

    def pad(t, carry):
        ids[n + t] = NULL
        owner[(n + t) // 2] = 0
        return carry

    lax.fori_loop(0, 2 * UNROLL, pad, 0, unroll=True)

    def front(u):
        a, b = ids[2 * u], ids[2 * u + 1]
        j = base + owner[u]

        def pair(ref):
            return jnp.concatenate([ref[a], ref[b]], axis=1)

        facing = jnp.maximum(dot(rf[j], pair(sf)), 0.0)
        seen = jnp.maximum(dot(rs[j], pair(ss)), 0.0)
        spread = dot(rd[j], pair(sd))
        return (facing * seen / (spread * spread)).astype(jnp.bfloat16)

    def back(u, values):
        a, b = ids[2 * u], ids[2 * u + 1]
        j = owner[u]
        out[j] = out[j] + dot(values, jnp.concatenate([em[a], em[b]], axis=0))

    def step(i, carry):
        values = [front(i * UNROLL + r) for r in range(UNROLL)]
        for r in range(UNROLL):
            back(i * UNROLL + r, values[r])
        return carry

    lax.fori_loop(0, pl.cdiv(n // 2, UNROLL), step, 0)


VMEM_SPEC = pl.BlockSpec(memory_space=pltpu.VMEM)
SMEM_SPEC = pl.BlockSpec(memory_space=pltpu.SMEM)
BF16 = jnp.bfloat16


def bf16_shape(*shape):
    return jax.ShapeDtypeStruct(shape, BF16)


def recv_prep(tiles, mats):
    return pl.pallas_call(
        recv_prep_kernel,
        out_shape=[bf16_shape(NJ, BS, KF), bf16_shape(NJ, BS, KS), bf16_shape(NJ, BS, KD)],
        in_specs=[VMEM_SPEC] * 4,
        out_specs=[VMEM_SPEC] * 3,
        name="recv_prep",
        cost_estimate=pl.CostEstimate(flops=10**7, bytes_accessed=4 * 10**6, transcendentals=0),
    )(tiles, *mats)


def src_prep(packed, mats, nul):
    return pl.pallas_call(
        src_prep_kernel,
        out_shape=[
            bf16_shape(NULL + 1, KF, BS),
            bf16_shape(NULL + 1, KS, BS),
            bf16_shape(NULL + 1, KD, BS),
            bf16_shape(NULL + 1, BS, BS),
        ],
        in_specs=[VMEM_SPEC] * (GROUP + 4),
        out_specs=[VMEM_SPEC] * 4,
        name="src_prep",
        cost_estimate=pl.CostEstimate(flops=10**7, bytes_accessed=9 * 10**6, transcendentals=0),
    )(*packed, *mats, nul)


def sweep(first, lists, recv, src):
    return pl.pallas_call(
        sweep_kernel,
        out_shape=jax.ShapeDtypeStruct((NZ, BS, BS), jnp.float32),
        in_specs=[SMEM_SPEC] * 2 + [VMEM_SPEC] * 7,
        out_specs=VMEM_SPEC,
        scratch_shapes=[
            pltpu.SMEM((NZ * GROUP * CAP + 4 * UNROLL,), jnp.int32),
            pltpu.SMEM((NZ * GROUP * CAP // 2 + 2 * UNROLL,), jnp.int32),
        ],
        name="sweep",
        cost_estimate=pl.CostEstimate(
            flops=4 * 10**9, bytes_accessed=8 * 10**6, transcendentals=2 * 10**6
        ),
    )(first, lists, *recv, *src)


def normals(angle_rows):
    polar = angle_rows[0]
    azimuth = angle_rows[1]
    return jnp.stack(
        [jnp.sin(polar) * jnp.cos(azimuth), jnp.sin(polar) * jnp.sin(azimuth), jnp.cos(polar)]
    )


def base_rows(pos, direction, extra):
    centred = pos - CENTRE
    coarse = jnp.round(centred * 32.0) * (1.0 / 32.0)
    fine = centred - coarse
    square_a = coarse[0] * coarse[0] + coarse[1] * coarse[1] + coarse[2] * coarse[2]
    square_b = (
        fine[0] * (2.0 * coarse[0] + fine[0])
        + fine[1] * (2.0 * coarse[1] + fine[1])
        + fine[2] * (2.0 * coarse[2] + fine[2])
    ) + extra
    along = -(
        direction[0] * centred[0] + direction[1] * centred[1] + direction[2] * centred[2]
    )
    rows = [centred, direction, along[None], square_a[None], square_b[None]]
    return jnp.concatenate(rows + [jnp.ones_like(along)[None]], axis=0)


def y_route(distance):
    def linear(y):
        return (y % NYL) * NYH + y // NYL

    return [(linear(y), linear((y + distance) % NY)) for y in range(NY)]


def shards(
    recv_pos,
    recv_angles,
    src_pos,
    src_angles,
    src_area,
    reemission,
    incident,
    direct,
    visible_lists,
    visible_counts,
):
    mats = selection_matrices()
    recv_mats = [jnp.asarray(r, BF16) for r, _ in mats]
    src_mats = [jnp.asarray(s, BF16) for _, s in mats]
    nul = jnp.asarray(null_spread(), BF16)

    scale = reemission * src_area * (1.0 / np.pi)
    rows = base_rows(src_pos, normals(src_angles) * scale, src_area)
    rows = rows.reshape(LST, SB, BS).transpose(1, 0, 2)
    slots = jnp.arange(CAP, dtype=jnp.int32)
    live = slots < visible_counts[0, 0][:, :, None]
    marked = jnp.where(live, visible_lists[0, 0], -1)
    marked = marked.reshape(NX, NYL, NC, NYH, NZ, CAP).transpose(0, 2, 3, 1, 4, 5)
    marked = marked.reshape(GROUP, 1, NJ * CAP).astype(jnp.float32)
    rest = jnp.zeros((SB, ROWS - LST - 1, BS), jnp.float32)
    tiles = jnp.concatenate([rows, marked, rest], axis=1).reshape(SB * ROWS, BS)
    mine = jnp.concatenate([incident.astype(jnp.float32), tiles], axis=0)

    def along_x(block, distance):
        return lax.ppermute(block, "x", [(i, (i + distance) % NX) for i in range(NX)])

    def other_core(block):
        return lax.ppermute(block, "c", [(0, 1), (1, 0)])

    gathered = [mine] + [along_x(mine, d) for d in (1, 3, 2)]
    gathered = gathered + [other_core(block) for block in gathered]

    recv_rows = base_rows(recv_pos, normals(recv_angles), jnp.zeros((BS,), jnp.float32))
    recv_tile = jnp.concatenate([recv_rows, jnp.zeros((ROWS - LST, BS), jnp.float32)], axis=0)
    recv_tiles = lax.all_to_all(
        jnp.broadcast_to(recv_tile, (NJ, ROWS, BS)), ("yl", "yh", "z"), 0, 0, tiled=True
    )
    recv = recv_prep(recv_tiles, recv_mats)

    src = src_prep(gathered, src_mats, nul)
    me = lax.axis_index("x") * NC + lax.axis_index("c")
    at = SB * BS + me * ROWS + LST
    lists = jnp.concatenate(
        [lax.dynamic_slice(block, (at, 0), (1, BS)) for block in gathered], axis=0
    )
    lists = lists.astype(jnp.int32).reshape(GROUP * BS)

    y = lax.axis_index("yh") * NYL + lax.axis_index("yl")

    def chunk(distance):
        target = (y + distance) % NY
        return sweep((target * NZ).astype(jnp.int32).reshape(1), lists, recv, src)

    def along_y(block, distance):
        return lax.ppermute(block, ("yl", "yh"), y_route(distance))

    arrived = [along_y(chunk(d), d) for d in (2, 1, 3)]
    total = chunk(0) + arrived[0] + arrived[1] + arrived[2]
    pieces = lax.all_to_all(total, "z", 0, 0, tiled=True)
    return direct + jnp.sum(pieces, axis=0)


def solution(mesh):
    fine = Mesh(mesh.devices.reshape(NX, NYL, NC, NYH, NZ), ("x", "yl", "c", "yh", "z"))
    blk, lane = ("x", "yl", "c"), ("yh", "z")
    both = blk + lane
    return jax.shard_map(
        shards,
        mesh=fine,
        in_specs=(
            P(None, both),
            P(None, both),
            P(None, both),
            P(None, both),
            P(both),
            P(both),
            P(both, None),
            P(both, None),
            P(blk, lane, None, None, None),
            P(blk, lane, None, None),
        ),
        out_specs=P(both, None),
        check_vma=False,
    )
```

time: 2030 us -> 163 us (0.08)
  blocking collectives: 1160 us -> 25.4 us
  starting transfers between devices: 299 us -> 21.7 us
  waiting for transfers between devices: 271 us -> 19.6 us
  local copies, waits for them, and re-layouts: 138 us -> 6.77 us
  matrix products: 129 us -> 0 us
  Pallas kernels: 0 us -> 81.5 us
    all_gather x2 -> x0, blocking collectives: 1160 us -> none  [the longest x1 600 us: shards(): lax.all_gather(recv_pos, ('blk', 'lane'), axis=1, tiled=True)]
    ppermute x15 -> x10, starting transfers between devices: 299 us -> 10.2 us  [the longest x3 4.98 us: along_y(): return lax.ppermute(block, ('yl', 'yh'), y_route(distance))]
    reduce_scatter x1 -> x0, waiting for transfers between devices: 227 us -> none  [shards(): lax.psum_scatter(running.reshape(lane_count * block_rows, bin_count), 'la...]
    dot_general x16 -> x0, matrix products: 129 us -> none  [contribution(): jnp.einsum('jrcs,jcsb->jrb', values, picked_flux, preferred_element_type=...]
    gather x160 -> x0, local copies, waits for them, and re-layouts: 114 us -> none  [the longest x16 26 us: contribution(): near_pos = jnp.take(receiver_pos, targets, axis=1)]
    pallas_call x0 -> x6, Pallas kernels: none -> 81.5 us  [the longest x4 58.2 us: sweep(): pl.pallas_call(sweep_kernel, out_shape=jax.ShapeDtypeStruct((NZ, BS, BS),...]
    all_to_all x0 -> x1, blocking collectives: none -> 25.4 us  [shards(): pieces = lax.all_to_all(total, 'z', 0, 0, tiled=True)]
    ppermute x15 -> x10, waiting for transfers between devices: 44.1 us -> 19.6 us  [the longest x3 12.1 us: along_x(): lax.ppermute(block, 'x', [(i, (i + distance) % NX) for i in range(NX)])]
  transfers between devices with their start and end apart: 16 -> 11, of which waited for: 16 -> 3; matrix products, arithmetic and copies ran while one was open for 0% -> 2% of each run, Pallas kernels for 0% -> 15%
where the time goes in v1:
time: 163 us; the launch traced here: 161 us
  Pallas kernels  81.5 us (50%)
  blocking collectives  25.4 us (16%)
  starting transfers between devices  21.7 us (13%)
  waiting for transfers between devices  19.6 us (12%)
  local copies, waits for them, and re-layouts  6.77 us (4%)
  other arithmetic  6.24 us (4%)
    pallas_call x4, Pallas kernels, sweep(): pl.pallas_call(sweep_kernel, out_shape=jax.ShapeDtypeStruct((NZ, BS, BS),...  58.2 us
    all_to_all x1, blocking collectives, shards(): pieces = lax.all_to_all(total, 'z', 0, 0, tiled=True)  25.4 us
    pallas_call x1, Pallas kernels, src_prep(): pl.pallas_call(src_prep_kernel, out_shape=[bf16_shape(NULL + 1, KF, BS),...  13.4 us
    ppermute x3, waiting for transfers between devices, along_x(): lax.ppermute(block, 'x', [(i, (i + distance) % NX) for i in range(NX)])  12.1 us
    all_to_all x1, starting transfers between devices, shards(): lax.all_to_all(jnp.broadcast_to(recv_tile, (NJ, ROWS, BS)), ('yl', 'yh',...  11.5 us
    pallas_call x1, Pallas kernels, recv_prep(): pl.pallas_call(recv_prep_kernel, out_shape=[bf16_shape(NJ, BS, KF), bf16_...  9.86 us
    ppermute x3, waiting for transfers between devices, along_y(): return lax.ppermute(block, ('yl', 'yh'), y_route(distance))  7.51 us
    ppermute x3, starting transfers between devices, along_y(): return lax.ppermute(block, ('yl', 'yh'), y_route(distance))  4.98 us
  transfers between devices with their start and end apart: 11, of which 3 were waited for; matrix products, arithmetic and copies ran while one was open for 2% of the time, Pallas kernels for 15%

profile of v1, /device:TPU:6, one launch (start us, length us, event | category | flops | bytes accessed | tf_op | source)
XLA Modules:
  0.0 161.5 jit_solution(9765104958020599192)
XLA Ops:
  0.0 0.8 lt.46
  0.8 1.0 slice_cosine_fusion
  1.8 0.9 squeeze.11
  3.2 0.7 fusion.5
  3.9 1.0 convert_element_type.27
  5.0 0.7 fusion.2
  6.0 1.5 collective-permute-start.2
  7.5 1.7 %collective-permute-start.1 = (f32[1152,128]{1,0:T(8,128)S(1)}, f32[1152,128]{1,0:T(8,128)S(1)}, u32[]{:S(2)}, u32[]{:S(2)}) collective-permute-start(f32[1152,128]{1,0:T(8,128)S(1)} %pad_maximum_fusion.refs_0_), channel_id=1, source_target_pairs={{0,192},{64,0},{128,64},{192,128},{1,193},{65,1},{129,65},{193,129... | collective-permute-start | bytes 1769480 | tf_op jit(solution)/shard_map/ppermute | solution.py:277
  9.2 1.6 collective-permute-start
  10.9 0.7 broadcast_in_dim.24
  11.6 11.5 %all-to-all-start = ((f32[32,16,128]{2,1,0:T(8,128)}), f32[32,16,128]{2,1,0:T(8,128)S(1)}, u32[]{:S(2)}, u32[]{:S(2)}) async-start(f32[32,16,128]{2,1,0:T(8,128)} %broadcast_in_dim.24), calls=%async_computation | async-start | bytes 524288 | tf_op jit(solution)/shard_map/all_to_all | solution.py:287
  23.2 0.6 collective-permute-done.2.refs_3_
  23.9 11.4 %collective-permute-done.1.refs_2_ = f32[1152,128]{1,0:T(8,128)S(1)} collective-permute-done((f32[1152,128]{1,0:T(8,128)S(1)}, f32[1152,128]{1,0:T(8,128)S(1)}, u32[]{:S(2)}, u32[]{:S(2)}) %collective-permute-start.1) | collective-permute-done | bytes 589856 | tf_op jit(solution)/shard_map/ppermute | solution.py:277
  35.4 0.8 copy-done.1
  36.2 9.9 %recv_prep.1 = (bf16[32,128,32]{2,1,0:T(8,128)(2,1)}, bf16[32,128,32]{2,1,0:T(8,128)(2,1)}, bf16[32,128,48]{2,1,0:T(8,128)(2,1)}) custom-call(f32[32,16,128]{2,1,0:T(8,128)} %copy-done.1, bf16[32,48]{1,0:T(8,128)(2,1)} %constant.100.clone.mf, bf16[32,48]{1,0:T(8,128)(2,1)} %constant.101.clone.ms, bf16[48,48]{1,0:T(8,128)(2,1)} %constant.102.clone.md), custom_call_target="tpu_custom_call" | custom-call | flops 10000000 | bytes 4000000 | tf_op jit(solution)/shard_map/recv_prep/pallas_call | solution.py:172
  46.1 0.4 collective-permute-start.4
  46.5 0.7 constant_dynamic-slice_fusion.3
  47.2 0.7 constant_dynamic-slice_fusion
  47.9 0.7 constant_dynamic-slice_fusion.1
  48.6 0.8 copy-done.5
  49.4 0.6 convert_bitcast_fusion.1.lists
  50.0 13.4 %src_prep.1 = (bf16[65,32,128]{2,1,0:T(8,128)(2,1)}, bf16[65,32,128]{2,1,0:T(8,128)(2,1)}, bf16[65,48,128]{2,1,0:T(8,128)(2,1)}, bf16[65,128,128]{2,1,0:T(8,128)(2,1)}) custom-call(f32[1152,128]{1,0:T(8,128)} %copy-done, f32[1152,128]{1,0:T(8,128)} %copy-done.4, f32[1152,128]{1,0:T(8,128)} %copy-done.3, f32[1152,128]{1,0:T(8,128)} %copy-done.2, ...), custom_call_target="tpu_custom_call" | custom-call | flops 10000000 | bytes 9000000 | tf_op jit(solution)/shard_map/src_prep/pallas_call | solution.py:183
  63.5 14.7 %sweep.7 = f32[8,128,128]{2,1,0:T(8,128)} custom-call(s32[1]{0:T(128)} %bitcast.27.first, s32[1024]{0:T(1024)} %convert_bitcast_fusion.1.lists, bf16[32,128,32]{2,1,0:T(8,128)(2,1)} %get-tuple-element.12.rf, bf16[32,128,32]{2,1,0:T(8,128)(2,1)} %get-tuple-element.13.rs, bf16[32,128,48]{2,1,0:T(8,128)(2,1)} %get-tuple-element.14.rd, ...), custom_call_target="tpu_custom_call" | custom-call | flops 4000000000 | bytes 8000000 | tf_op jit(solution)/shard_map/sweep/pallas_call | solution.py:199
  78.2 14.7 %sweep.6 = f32[8,128,128]{2,1,0:T(8,128)} custom-call(s32[1]{0:T(128)} %bitcast.26.first, s32[1024]{0:T(1024)} %convert_bitcast_fusion.1.lists, bf16[32,128,32]{2,1,0:T(8,128)(2,1)} %get-tuple-element.12.rf, bf16[32,128,32]{2,1,0:T(8,128)(2,1)} %get-tuple-element.13.rs, bf16[32,128,48]{2,1,0:T(8,128)(2,1)} %get-tuple-element.14.rd, ...), custom_call_target="tpu_custom_call" | custom-call | flops 4000000000 | bytes 8000000 | tf_op jit(solution)/shard_map/sweep/pallas_call | solution.py:199
  92.9 14.1 %sweep.5 = f32[8,128,128]{2,1,0:T(8,128)} custom-call(s32[1]{0:T(128)} %bitcast.25.first, s32[1024]{0:T(1024)} %convert_bitcast_fusion.1.lists, bf16[32,128,32]{2,1,0:T(8,128)(2,1)} %get-tuple-element.12.rf, bf16[32,128,32]{2,1,0:T(8,128)(2,1)} %get-tuple-element.13.rs, bf16[32,128,48]{2,1,0:T(8,128)(2,1)} %get-tuple-element.14.rd, ...), custom_call_target="tpu_custom_call" | custom-call | flops 4000000000 | bytes 8000000 | tf_op jit(solution)/shard_map/sweep/pallas_call | solution.py:199
  107.0 1.7 %collective-permute-start.7 = (f32[8,128,128]{2,1,0:T(8,128)}, f32[8,128,128]{2,1,0:T(8,128)S(1)}, u32[]{:S(2)}, u32[]{:S(2)}) collective-permute-start(f32[8,128,128]{2,1,0:T(8,128)} %sweep.5), channel_id=1, source_target_pairs={{0,8},{32,40},{8,0},{40,32},{1,9},{33,41},{9,1},{41,33},{2,10},{34... | collective-permute-start | bytes 1572872 | tf_op jit(solution)/shard_map/ppermute | solution.py:307
  108.7 3.2 %collective-permute-start.9 = (f32[8,128,128]{2,1,0:T(8,128)S(1)}, f32[8,128,128]{2,1,0:T(8,128)S(1)}, u32[]{:S(2)}, u32[]{:S(2)}) collective-permute-start(f32[8,128,128]{2,1,0:T(8,128)S(1)} %copy-done.9), channel_id=1, source_target_pairs={{0,40},{32,0},{8,32},{40,8},{1,41},{33,1},{9,33},{41,9},{2,42},{34... | collective-permute-start | bytes 1572872 | tf_op jit(solution)/shard_map/ppermute | solution.py:307
  112.0 14.7 %sweep.4 = f32[8,128,128]{2,1,0:T(8,128)} custom-call(s32[1]{0:T(128)} %bitcast.first, s32[1024]{0:T(1024)} %convert_bitcast_fusion.1.lists, bf16[32,128,32]{2,1,0:T(8,128)(2,1)} %get-tuple-element.12.rf, bf16[32,128,32]{2,1,0:T(8,128)(2,1)} %get-tuple-element.13.rs, bf16[32,128,48]{2,1,0:T(8,128)(2,1)} %get-tuple-element.14.rd, ...), custom_call_target="tpu_custom_call" | custom-call | flops 4000000000 | bytes 8000000 | tf_op jit(solution)/shard_map/sweep/pallas_call | solution.py:199
  126.7 7.5 %collective-permute-done.8 = f32[8,128,128]{2,1,0:T(8,128)S(1)} collective-permute-done((f32[8,128,128]{2,1,0:T(8,128)S(1)}, f32[8,128,128]{2,1,0:T(8,128)S(1)}, u32[]{:S(2)}, u32[]{:S(2)}) %collective-permute-start.8) | collective-permute-done | bytes 524320 | tf_op jit(solution)/shard_map/ppermute | solution.py:307
  134.2 1.1 add_add_fusion
  135.3 25.4 %all_to_all.10 = f32[8,128,128]{2,1,0:T(8,128)S(1)} all-to-all(f32[8,128,128]{2,1,0:T(8,128)S(1)} %add_add_fusion), channel_id=1, replica_groups=mesh['x'=4,'yl'=2,'c'=2,'yh'=2,'z'=8] {'z'}, dimensions={0} | all-to-all | bytes 1048576 | tf_op jit(solution)/shard_map/all_to_all | solution.py:311
  160.8 0.6 add.162
  (58 shorter events, 1.2 us)
Async XLA Ops:
  0.0 10.8 %copy-start.7 = (f32[3,128]{1,0:T(4,128)S(1)}, f32[3,128]{1,0:T(4,128)}, u32[]{:S(2)}) copy-start(f32[3,128]{1,0:T(4,128)} %param.17) | copy-start | bytes 4612
  0.0 10.8 %copy-start.8 = (f32[2,128]{1,0:T(2,128)S(1)}, f32[2,128]{1,0:T(2,128)}, u32[]{:S(2)}) copy-start(f32[2,128]{1,0:T(2,128)} %param.18) | copy-start | bytes 3076
  6.0 44.0 %copy-start = (f32[1152,128]{1,0:T(8,128)}, f32[1152,128]{1,0:T(8,128)S(1)}, u32[]{:S(2)}) copy-start(f32[1152,128]{1,0:T(8,128)S(1)} %pad_maximum_fusion.refs_0_) | copy-start | bytes 1769476
  6.0 17.8 %collective-permute-start.2 = (f32[1152,128]{1,0:T(8,128)S(1)}, f32[1152,128]{1,0:T(8,128)S(1)}, u32[]{:S(2)}, u32[]{:S(2)}) collective-permute-start(f32[1152,128]{1,0:T(8,128)S(1)} %pad_maximum_fusion.refs_0_), channel_id=1, source_target_pairs={{0,128},{64,192},{128,0},{192,64},{1,129},{65,193},{129,1},{193,65... | collective-permute-start | bytes 1769480 | tf_op jit(solution)/shard_map/ppermute | solution.py:277
  7.5 27.8 %collective-permute-start.1 = (f32[1152,128]{1,0:T(8,128)S(1)}, f32[1152,128]{1,0:T(8,128)S(1)}, u32[]{:S(2)}, u32[]{:S(2)}) collective-permute-start(f32[1152,128]{1,0:T(8,128)S(1)} %pad_maximum_fusion.refs_0_), channel_id=1, source_target_pairs={{0,192},{64,0},{128,64},{192,128},{1,193},{65,1},{129,65},{193,129... | collective-permute-start | bytes 1769480 | tf_op jit(solution)/shard_map/ppermute | solution.py:277
  9.2 36.9 %collective-permute-start = (f32[1152,128]{1,0:T(8,128)S(1)}, f32[1152,128]{1,0:T(8,128)S(1)}, u32[]{:S(2)}, u32[]{:S(2)}) collective-permute-start(f32[1152,128]{1,0:T(8,128)S(1)} %pad_maximum_fusion.refs_0_), channel_id=1, source_target_pairs={{0,64},{64,128},{128,192},{192,0},{1,65},{65,129},{129,193},{193,1... | collective-permute-start | bytes 1769480 | tf_op jit(solution)/shard_map/ppermute | solution.py:277
  11.6 23.8 %all-to-all-start = ((f32[32,16,128]{2,1,0:T(8,128)}), f32[32,16,128]{2,1,0:T(8,128)S(1)}, u32[]{:S(2)}, u32[]{:S(2)}) async-start(f32[32,16,128]{2,1,0:T(8,128)} %broadcast_in_dim.24), calls=%async_computation | async-start | bytes 524288 | tf_op jit(solution)/shard_map/all_to_all | solution.py:287
  23.1 23.3 %collective-permute-start.3 = (f32[1152,128]{1,0:T(8,128)S(1)}, f32[1152,128]{1,0:T(8,128)}, u32[]{:S(2)}, u32[]{:S(2)}) collective-permute-start(f32[1152,128]{1,0:T(8,128)S(1)} %pad_maximum_fusion.refs_0_), channel_id=1, source_target_pairs={{0,16},{16,0},{1,17},{17,1},{2,18},{18,2},{3,19},{19,3},{4,20},{20... | collective-permute-start | bytes 1769480 | tf_op jit(solution)/shard_map/ppermute | solution.py:280
  23.9 26.1 %copy-start.2 = (f32[1152,128]{1,0:T(8,128)}, f32[1152,128]{1,0:T(8,128)S(1)}, u32[]{:S(2)}) copy-start(f32[1152,128]{1,0:T(8,128)S(1)} %collective-permute-done.2.refs_3_) | copy-start | bytes 1769476
  23.9 23.3 %collective-permute-start.6 = (f32[1152,128]{1,0:T(8,128)S(1)}, f32[1152,128]{1,0:T(8,128)}, u32[]{:S(2)}, u32[]{:S(2)}) collective-permute-start(f32[1152,128]{1,0:T(8,128)S(1)} %collective-permute-done.2.refs_3_), channel_id=1, source_target_pairs={{0,16},{16,0},{1,17},{17,1},{2,18},{18,2},{3,19},{19,3},{4,20},{20... | collective-permute-start | bytes 1769480 | tf_op jit(solution)/shard_map/ppermute | solution.py:280
  35.3 14.7 %copy-start.3 = (f32[1152,128]{1,0:T(8,128)}, f32[1152,128]{1,0:T(8,128)S(1)}, u32[]{:S(2)}) copy-start(f32[1152,128]{1,0:T(8,128)S(1)} %collective-permute-done.1.refs_2_) | copy-start | bytes 1769476
  35.3 12.5 %collective-permute-start.5 = (f32[1152,128]{1,0:T(8,128)S(1)}, f32[1152,128]{1,0:T(8,128)}, u32[]{:S(2)}, u32[]{:S(2)}) collective-permute-start(f32[1152,128]{1,0:T(8,128)S(1)} %collective-permute-done.1.refs_2_), channel_id=1, source_target_pairs={{0,16},{16,0},{1,17},{17,1},{2,18},{18,2},{3,19},{19,3},{4,20},{20... | collective-permute-start | bytes 1769480 | tf_op jit(solution)/shard_map/ppermute | solution.py:280
  35.4 0.8 copy-start.1
  46.1 3.9 %copy-start.4 = (f32[1152,128]{1,0:T(8,128)}, f32[1152,128]{1,0:T(8,128)S(1)}, u32[]{:S(2)}) copy-start(f32[1152,128]{1,0:T(8,128)S(1)} %collective-permute-done.refs_1_) | copy-start | bytes 1769476
  46.1 2.5 %collective-permute-start.4 = (f32[1152,128]{1,0:T(8,128)S(1)}, f32[1152,128]{1,0:T(8,128)S(1)}, u32[]{:S(2)}, u32[]{:S(2)}) collective-permute-start(f32[1152,128]{1,0:T(8,128)S(1)} %collective-permute-done.refs_1_), channel_id=1, source_target_pairs={{0,16},{16,0},{1,17},{17,1},{2,18},{18,2},{3,19},{19,3},{4,20},{20... | collective-permute-start | bytes 1769480 | tf_op jit(solution)/shard_map/ppermute | solution.py:280
  48.6 0.8 copy-start.5
  92.9 15.8 %copy-start.10 = (f32[8,128,128]{2,1,0:T(8,128)S(1)}, f32[8,128,128]{2,1,0:T(8,128)}, u32[]{:S(2)}) copy-start(f32[8,128,128]{2,1,0:T(8,128)} %sweep.6) | copy-start | bytes 1572868
  92.9 15.8 %copy-start.9 = (f32[8,128,128]{2,1,0:T(8,128)S(1)}, f32[8,128,128]{2,1,0:T(8,128)}, u32[]{:S(2)}) copy-start(f32[8,128,128]{2,1,0:T(8,128)} %sweep.7) | copy-start | bytes 1572868
  107.0 19.7 %collective-permute-start.7 = (f32[8,128,128]{2,1,0:T(8,128)}, f32[8,128,128]{2,1,0:T(8,128)S(1)}, u32[]{:S(2)}, u32[]{:S(2)}) collective-permute-start(f32[8,128,128]{2,1,0:T(8,128)} %sweep.5), channel_id=1, source_target_pairs={{0,8},{32,40},{8,0},{40,32},{1,9},{33,41},{9,1},{41,33},{2,10},{34... | collective-permute-start | bytes 1572872 | tf_op jit(solution)/shard_map/ppermute | solution.py:307
  108.7 25.5 %collective-permute-start.8 = (f32[8,128,128]{2,1,0:T(8,128)S(1)}, f32[8,128,128]{2,1,0:T(8,128)S(1)}, u32[]{:S(2)}, u32[]{:S(2)}) collective-permute-start(f32[8,128,128]{2,1,0:T(8,128)S(1)} %copy-done.10), channel_id=1, source_target_pairs={{0,32},{32,8},{8,40},{40,0},{1,33},{33,9},{9,41},{41,1},{2,34},{34... | collective-permute-start | bytes 1572872 | tf_op jit(solution)/shard_map/ppermute | solution.py:307
  108.7 25.5 %collective-permute-start.9 = (f32[8,128,128]{2,1,0:T(8,128)S(1)}, f32[8,128,128]{2,1,0:T(8,128)S(1)}, u32[]{:S(2)}, u32[]{:S(2)}) collective-permute-start(f32[8,128,128]{2,1,0:T(8,128)S(1)} %copy-done.9), channel_id=1, source_target_pairs={{0,40},{32,0},{8,32},{40,8},{1,41},{33,1},{9,33},{41,9},{2,42},{34... | collective-permute-start | bytes 1572872 | tf_op jit(solution)/shard_map/ppermute | solution.py:307
  126.7 34.1 %copy-start.6 = (f32[128,128]{1,0:T(8,128)S(1)}, f32[128,128]{1,0:T(8,128)}, u32[]{:S(2)}) copy-start(f32[128,128]{1,0:T(8,128)} %param.24) | copy-start | bytes 196612

commit v2 on v1

--- a/solution.py
+++ b/solution.py
@@ -16,11 +16,11 @@
 CAP = 4
 GROUP = NX * NC
 NJ = NY * NZ
-NULL = GROUP * SB
 CENTRE = 3.0
 ROWS = 16
 POS, NRM, DOT, SQA, SQB, ONE, LST = 0, 3, 6, 7, 8, 9, 10
 KF, KS, KD = 32, 32, 48
+VMEM_LIMIT = 24 << 20
 UNROLL = 8
 
 
@@ -73,69 +73,68 @@
     return jnp.dot(a, b, preferred_element_type=jnp.float32)
 
 
-def recv_prep_kernel(tiles, mf, ms, md, rf, rs, rd):
-    def one(j, carry):
-        y, z = j // NZ, j % NZ
-        at = (y % NYL) * (NYH * NZ) + (y // NYL) * NZ + z
-        q = split_pieces(tiles[at])
-        for m, out in ((mf, rf), (ms, rs), (md, rd)):
-            out[j] = lax.dot_general(
+def src_prep_kernel(count, me, *refs):
+    packed = refs[:count]
+    mf, ms, md, nul, sf, ss, sd, em, lists = refs[count:]
+    list_at = SB * BS + me[0] * ROWS + LST
+    for d in range(count):
+        ref = packed[d]
+        for k in range(SB):
+            em[d * SB + k] = ref[k * BS : (k + 1) * BS, :].astype(jnp.bfloat16)
+        tiles = [ref[SB * BS + k * ROWS : SB * BS + (k + 1) * ROWS, :] for k in range(SB)]
+        q = split_pieces(jnp.concatenate(tiles, axis=1))
+        lists[d : d + 1, :] = ref[pl.ds(list_at, 1), :].astype(jnp.int32)
+        for m, out in ((mf, sf), (ms, ss), (md, sd)):
+            values = dot(m[...], q).astype(jnp.bfloat16)
+            for k in range(SB):
+                out[d * SB + k] = values[:, k * BS : (k + 1) * BS]
+    null = count * SB
+    em[null] = jnp.zeros((BS, BS), jnp.bfloat16)
+    sf[null] = jnp.zeros((KF, BS), jnp.bfloat16)
+    ss[null] = jnp.zeros((KS, BS), jnp.bfloat16)
+    sd[null] = nul[...]
+
+
+def sweep_kernel(count, blocks, added, distance, my_y, lists, tiles, mf, ms, md, sf, ss, sd, em, *refs):
+    if added:
+        before, out, rf, rs, rd, ids, owner = refs
+    else:
+        out, rf, rs, rd, ids, owner = refs
+    target = (my_y[0] + distance) & (NY - 1)
+    base = ((target & (NYL - 1)) * NYH + (target >> 1)) * NZ if added else 0
+    null = count * SB
+    slots = count * CAP // 2
+
+    for j in range(blocks):
+        q = split_pieces(tiles[base + j])
+        for m, ref in ((mf, rf), (ms, rs), (md, rd)):
+            ref[j] = lax.dot_general(
                 q, m[...], (((0,), (1,)), ((), ())), preferred_element_type=jnp.float32
             ).astype(jnp.bfloat16)
-        return carry
-
-    lax.fori_loop(0, NJ, one, 0)
-
-
-def src_prep_kernel(*refs):
-    packed = refs[:GROUP]
-    mf, ms, md, nul, sf, ss, sd, em = refs[GROUP:]
-    for d in range(GROUP):
-        ref = packed[d]
-
-        def one(k, carry, ref=ref, d=d):
-            start = pl.multiple_of(k * BS, BS)
-            em[d * SB + k] = ref[pl.ds(start, BS), :].astype(jnp.bfloat16)
-            tile_at = pl.multiple_of(SB * BS + k * ROWS, ROWS)
-            q = split_pieces(ref[pl.ds(tile_at, ROWS), :])
-            for m, out in ((mf, sf), (ms, ss), (md, sd)):
-                out[d * SB + k] = dot(m[...], q).astype(jnp.bfloat16)
-            return carry
-
-        lax.fori_loop(0, SB, one, 0)
-    em[NULL] = jnp.zeros((BS, BS), jnp.bfloat16)
-    sf[NULL] = jnp.zeros((KF, BS), jnp.bfloat16)
-    ss[NULL] = jnp.zeros((KS, BS), jnp.bfloat16)
-    sd[NULL] = nul[...]
-
-
-def sweep_kernel(first, lists, rf, rs, rd, sf, ss, sd, em, out, ids, owner):
-    base = first[0]
-    out[...] = jnp.zeros(out.shape, out.dtype)
+        out[j] = before[base + j] if added else jnp.zeros((BS, BS), jnp.float32)
 
     def one_block(j, n):
-        def one_entry(t, n):
-            value = lists[(t // CAP) * BS + (base + j) * CAP + t % CAP]
-            ids[n] = (t // CAP) * SB + value
-            owner[n // 2] = j
-            return n + (value >= 0).astype(jnp.int32)
-
-        n = lax.fori_loop(0, GROUP * CAP, one_entry, n, unroll=8)
-        ids[n] = NULL
+        for t in range(slots):
+            owner[n // 2 + t] = j
+        for d in range(count):
+            used = []
+            for c in range(CAP):
+                value = lists[d, (base + j) * CAP + c]
+                ids[n + c] = d * SB + value
+                used.append((value >= 0).astype(jnp.int32))
+            n = n + ((used[0] + used[1]) + (used[2] + used[3]))
+        ids[n] = null
         return n + n % 2
 
-    n = lax.fori_loop(0, NZ, one_block, 0)
-
-    def pad(t, carry):
-        ids[n + t] = NULL
-        owner[(n + t) // 2] = 0
-        return carry
-
-    lax.fori_loop(0, 2 * UNROLL, pad, 0, unroll=True)
+    n = lax.fori_loop(0, blocks, one_block, 0)
+    for t in range(2 * UNROLL):
+        ids[n + t] = null
+    for t in range(UNROLL):
+        owner[n // 2 + t] = 0
 
     def front(u):
         a, b = ids[2 * u], ids[2 * u + 1]
-        j = base + owner[u]
+        j = owner[u]
 
         def pair(ref):
             return jnp.concatenate([ref[a], ref[b]], axis=1)
@@ -162,54 +161,53 @@
 VMEM_SPEC = pl.BlockSpec(memory_space=pltpu.VMEM)
 SMEM_SPEC = pl.BlockSpec(memory_space=pltpu.SMEM)
 BF16 = jnp.bfloat16
+PARAMS = pltpu.CompilerParams(vmem_limit_bytes=VMEM_LIMIT)
 
 
 def bf16_shape(*shape):
     return jax.ShapeDtypeStruct(shape, BF16)
 
 
-def recv_prep(tiles, mats):
+def src_prep(me, packed, mats, nul):
+    count = len(packed)
+    rows = count * SB + 1
     return pl.pallas_call(
-        recv_prep_kernel,
-        out_shape=[bf16_shape(NJ, BS, KF), bf16_shape(NJ, BS, KS), bf16_shape(NJ, BS, KD)],
-        in_specs=[VMEM_SPEC] * 4,
-        out_specs=[VMEM_SPEC] * 3,
-        name="recv_prep",
-        cost_estimate=pl.CostEstimate(flops=10**7, bytes_accessed=4 * 10**6, transcendentals=0),
-    )(tiles, *mats)
-
-
-def src_prep(packed, mats, nul):
+        functools.partial(src_prep_kernel, count),
+        out_shape=[
+            bf16_shape(rows, KF, BS),
+            bf16_shape(rows, KS, BS),
+            bf16_shape(rows, KD, BS),
+            bf16_shape(rows, BS, BS),
+            jax.ShapeDtypeStruct((count, BS), jnp.int32),
+        ],
+        in_specs=[SMEM_SPEC] + [VMEM_SPEC] * (count + 4),
+        out_specs=[VMEM_SPEC] * 5,
+        name="src_prep",
+        compiler_params=PARAMS,
+        cost_estimate=pl.CostEstimate(flops=10**6, bytes_accessed=10**6, transcendentals=0),
+    )(me, *packed, *mats, nul)
+
+
+def sweep(my_y, distance, tiles, mats, src, blocks, before=None):
+    *src, lists = src
+    count = lists.shape[0]
+    extra = () if before is None else (before,)
     return pl.pallas_call(
-        src_prep_kernel,
-        out_shape=[
-            bf16_shape(NULL + 1, KF, BS),
-            bf16_shape(NULL + 1, KS, BS),
-            bf16_shape(NULL + 1, KD, BS),
-            bf16_shape(NULL + 1, BS, BS),
-        ],
-        in_specs=[VMEM_SPEC] * (GROUP + 4),
-        out_specs=[VMEM_SPEC] * 4,
-        name="src_prep",
-        cost_estimate=pl.CostEstimate(flops=10**7, bytes_accessed=9 * 10**6, transcendentals=0),
-    )(*packed, *mats, nul)
-
-
-def sweep(first, lists, recv, src):
-    return pl.pallas_call(
-        sweep_kernel,
-        out_shape=jax.ShapeDtypeStruct((NZ, BS, BS), jnp.float32),
-        in_specs=[SMEM_SPEC] * 2 + [VMEM_SPEC] * 7,
+        functools.partial(sweep_kernel, count, blocks, before is not None, distance),
+        out_shape=jax.ShapeDtypeStruct((blocks, BS, BS), jnp.float32),
+        in_specs=[SMEM_SPEC] * 2 + [VMEM_SPEC] * (8 + len(extra)),
         out_specs=VMEM_SPEC,
         scratch_shapes=[
-            pltpu.SMEM((NZ * GROUP * CAP + 4 * UNROLL,), jnp.int32),
-            pltpu.SMEM((NZ * GROUP * CAP // 2 + 2 * UNROLL,), jnp.int32),
+            pltpu.VMEM((blocks, BS, KF), BF16),
+            pltpu.VMEM((blocks, BS, KS), BF16),
+            pltpu.VMEM((blocks, BS, KD), BF16),
+            pltpu.SMEM((blocks * count * CAP + 4 * UNROLL,), jnp.int32),
+            pltpu.SMEM((blocks * count * CAP // 2 + count * CAP + 2 * UNROLL,), jnp.int32),
         ],
         name="sweep",
-        cost_estimate=pl.CostEstimate(
-            flops=4 * 10**9, bytes_accessed=8 * 10**6, transcendentals=2 * 10**6
-        ),
-    )(first, lists, *recv, *src)
+        compiler_params=PARAMS,
+        cost_estimate=pl.CostEstimate(flops=10**6, bytes_accessed=10**6, transcendentals=0),
+    )(my_y, lists, tiles, *mats, *src, *extra)
 
 
 def normals(angle_rows):
@@ -267,7 +265,7 @@
     slots = jnp.arange(CAP, dtype=jnp.int32)
     live = slots < visible_counts[0, 0][:, :, None]
     marked = jnp.where(live, visible_lists[0, 0], -1)
-    marked = marked.reshape(NX, NYL, NC, NYH, NZ, CAP).transpose(0, 2, 3, 1, 4, 5)
+    marked = marked.reshape(NX, NYL, NC, NYH, NZ, CAP).transpose(0, 2, 1, 3, 4, 5)
     marked = marked.reshape(GROUP, 1, NJ * CAP).astype(jnp.float32)
     rest = jnp.zeros((SB, ROWS - LST - 1, BS), jnp.float32)
     tiles = jnp.concatenate([rows, marked, rest], axis=1).reshape(SB * ROWS, BS)
@@ -279,29 +277,25 @@
     def other_core(block):
         return lax.ppermute(block, "c", [(0, 1), (1, 0)])
 
-    gathered = [mine] + [along_x(mine, d) for d in (1, 3, 2)]
-    gathered = gathered + [other_core(block) for block in gathered]
+    me = (lax.axis_index("x") * NC + lax.axis_index("c")).astype(jnp.int32).reshape(1)
+    my_y = (lax.axis_index("yh") * NYL + lax.axis_index("yl")).astype(jnp.int32).reshape(1)
+    far = [along_x(mine, d) for d in (1, 3, 2)]
+    near = [mine, other_core(mine)]
 
     recv_rows = base_rows(recv_pos, normals(recv_angles), jnp.zeros((BS,), jnp.float32))
     recv_tile = jnp.concatenate([recv_rows, jnp.zeros((ROWS - LST, BS), jnp.float32)], axis=0)
-    recv_tiles = lax.all_to_all(
+    tiles = lax.all_to_all(
         jnp.broadcast_to(recv_tile, (NJ, ROWS, BS)), ("yl", "yh", "z"), 0, 0, tiled=True
     )
-    recv = recv_prep(recv_tiles, recv_mats)
-
-    src = src_prep(gathered, src_mats, nul)
-    me = lax.axis_index("x") * NC + lax.axis_index("c")
-    at = SB * BS + me * ROWS + LST
-    lists = jnp.concatenate(
-        [lax.dynamic_slice(block, (at, 0), (1, BS)) for block in gathered], axis=0
-    )
-    lists = lists.astype(jnp.int32).reshape(GROUP * BS)
-
-    y = lax.axis_index("yh") * NYL + lax.axis_index("yl")
+
+    begun = sweep(my_y, 0, tiles, recv_mats, src_prep(me, near, src_mats, nul), NJ)
+    far = lax.optimization_barrier((*far, begun))
+    far, begun = list(far[:3]), far[3]
+    far = far + [other_core(block) for block in far]
+    src = src_prep(me, far, src_mats, nul)
 
     def chunk(distance):
-        target = (y + distance) % NY
-        return sweep((target * NZ).astype(jnp.int32).reshape(1), lists, recv, src)
+        return sweep(my_y, distance, tiles, recv_mats, src, NZ, begun)
 
     def along_y(block, distance):
         return lax.ppermute(block, ("yl", "yh"), y_route(distance))

time: 163 us -> 115 us (0.71)
  Pallas kernels: 81.5 us -> 34.9 us
  other arithmetic: 6.24 us -> 4.6 us
    pallas_call x6 -> x7, Pallas kernels: 81.5 us -> 34.9 us  [the longest x5 34 us: sweep(): pl.pallas_call(functools.partial(sweep_kernel, count, blocks, before is n...]
    ppermute x3, waiting for transfers between devices: 12.1 us -> 0.01 us  [along_x(): lax.ppermute(block, 'x', [(i, (i + distance) % NX) for i in range(NX)])]
    all_to_all x1, waiting for transfers between devices: 0.01 us -> 9.84 us  [shards(): lax.all_to_all(jnp.broadcast_to(recv_tile, (NJ, ROWS, BS)), ('yl', 'yh',...]
    unnamed x22 -> x32, local copies, waits for them, and re-layouts: 1.66 us -> 5.02 us
    ppermute x4, waiting for transfers between devices: 0.01 us -> 3.08 us  [other_core(): return lax.ppermute(block, 'c', [(0, 1), (1, 0)])]
    dynamic_slice x7 -> x0, local copies, waits for them, and re-layouts: 2.09 us -> none  [shards(): lax.dynamic_slice(block, (at, 0), (1, BS))]
  transfers between devices with their start and end apart: 11 -> 11, of which waited for: 3 -> 6; matrix products, arithmetic and copies ran while one was open for 2% -> 1% of each run, Pallas kernels for 15% -> 26%
where the time goes in v2:
time: 115 us; the launch traced here: 113 us
  Pallas kernels  34.9 us (30%)
  blocking collectives  24.6 us (21%)
  starting transfers between devices  20.6 us (18%)
  waiting for transfers between devices  20.2 us (18%)
  local copies, waits for them, and re-layouts  8.01 us (7%)
  other arithmetic  4.6 us (4%)
    pallas_call x5, Pallas kernels, sweep(): pl.pallas_call(functools.partial(sweep_kernel, count, blocks, before is n...  34 us
    all_to_all x1, blocking collectives, shards(): pieces = lax.all_to_all(total, 'z', 0, 0, tiled=True)  24.6 us
    all_to_all x1, starting transfers between devices, shards(): lax.all_to_all(jnp.broadcast_to(recv_tile, (NJ, ROWS, BS)), ('yl', 'yh',...  11.5 us
    all_to_all x1, waiting for transfers between devices, shards(): lax.all_to_all(jnp.broadcast_to(recv_tile, (NJ, ROWS, BS)), ('yl', 'yh',...  9.84 us
    ppermute x3, waiting for transfers between devices, along_y(): return lax.ppermute(block, ('yl', 'yh'), y_route(distance))  7.3 us
    unnamed x32, local copies, waits for them, and re-layouts  5.02 us
    ppermute x3, starting transfers between devices, along_x(): lax.ppermute(block, 'x', [(i, (i + distance) % NX) for i in range(NX)])  4.73 us
    ppermute x3, starting transfers between devices, along_y(): return lax.ppermute(block, ('yl', 'yh'), y_route(distance))  3.65 us
  transfers between devices with their start and end apart: 11, of which 6 were waited for; matrix products, arithmetic and copies ran while one was open for 1% of the time, Pallas kernels for 26%

profile of v2, /device:TPU:6, one launch (start us, length us, event | category | flops | bytes accessed | tf_op | source)
XLA Modules:
  0.0 113.3 jit_solution(18155006703159782999)
XLA Ops:
  0.0 0.8 lt.17
  0.9 1.0 slice_cosine_fusion
  1.9 0.9 squeeze.11
  3.3 0.7 fusion.5
  4.0 1.0 convert_element_type.20
  5.1 0.7 fusion.2
  6.2 1.5 %collective-permute-start.2 = (f32[1152,128]{1,0:T(8,128)S(1)}, f32[1152,128]{1,0:T(8,128)S(1)}, u32[]{:S(2)}, u32[]{:S(2)}) collective-permute-start(f32[1152,128]{1,0:T(8,128)S(1)} %pad_maximum_fusion.refs_0_), channel_id=1, source_target_pairs={{0,128},{64,192},{128,0},{192,64},{1,129},{65,193},{129,1},{193,65... | collective-permute-start | bytes 1769480 | tf_op jit(solution)/shard_map/ppermute | solution.py:275
  7.7 1.7 %collective-permute-start.1 = (f32[1152,128]{1,0:T(8,128)S(1)}, f32[1152,128]{1,0:T(8,128)S(1)}, u32[]{:S(2)}, u32[]{:S(2)}) collective-permute-start(f32[1152,128]{1,0:T(8,128)S(1)} %pad_maximum_fusion.refs_0_), channel_id=1, source_target_pairs={{0,192},{64,0},{128,64},{192,128},{1,193},{65,1},{129,65},{193,129... | collective-permute-start | bytes 1769480 | tf_op jit(solution)/shard_map/ppermute | solution.py:275
  9.4 1.6 %collective-permute-start = (f32[1152,128]{1,0:T(8,128)S(1)}, f32[1152,128]{1,0:T(8,128)S(1)}, u32[]{:S(2)}, u32[]{:S(2)}) collective-permute-start(f32[1152,128]{1,0:T(8,128)S(1)} %pad_maximum_fusion.refs_0_), channel_id=1, source_target_pairs={{0,64},{64,128},{128,192},{192,0},{1,65},{65,129},{129,193},{193,1... | collective-permute-start | bytes 1769480 | tf_op jit(solution)/shard_map/ppermute | solution.py:275
  11.1 0.7 broadcast_in_dim.24
  11.8 11.5 %all-to-all-start = ((f32[32,16,128]{2,1,0:T(8,128)}), f32[32,16,128]{2,1,0:T(8,128)S(1)}, u32[]{:S(2)}, u32[]{:S(2)}) async-start(f32[32,16,128]{2,1,0:T(8,128)} %broadcast_in_dim.24), calls=%async_computation | async-start | bytes 524288 | tf_op jit(solution)/shard_map/all_to_all | solution.py:287
  23.7 0.8 copy-done
  24.5 0.7 copy-done.5
  25.2 0.6 copy-done.7
  25.8 9.8 %all-to-all-done.tiles = f32[32,16,128]{2,1,0:T(8,128)S(1)} async-done(((f32[32,16,128]{2,1,0:T(8,128)}), f32[32,16,128]{2,1,0:T(8,128)S(1)}, u32[]{:S(2)}, u32[]{:S(2)}) %all-to-all-start) | async-done | bytes 262176 | tf_op jit(solution)/shard_map/all_to_all | solution.py:287
  35.7 1.0 copy-done.1
  36.7 0.9 copy-done.6
  37.6 0.9 copy-done.8
  38.5 12.8 %sweep.5.refs_0_ = f32[32,128,128]{2,1,0:T(8,128)S(1)} custom-call(s32[1]{0:T(128)} %bitcast.my_y, s32[2,128]{1,0:T(2,128)S(1)} %get-tuple-element.19.lists, f32[32,16,128]{2,1,0:T(8,128)S(1)} %all-to-all-done.tiles, bf16[32,48]{1,0:T(8,128)(2,1)S(1)} %copy-done.4, bf16[32,48]{1,0:T(8,128)(2,1)S(1)} %copy-done.3, bf16[48,48]{1,0:T(8,128)(2,1)S(1)} %copy-done.2, ...), custom_call_target="tpu_custom_call" | custom-call | flops 1000000 | bytes 1000000 | tf_op jit(solution)/shard_map/sweep/pallas_call | solution.py:195
  52.1 1.4 %collective-permute-done.4.refs_3_ = f32[1152,128]{1,0:T(8,128)S(1)} collective-permute-done((f32[1152,128]{1,0:T(8,128)S(1)}, f32[1152,128]{1,0:T(8,128)S(1)}, u32[]{:S(2)}, u32[]{:S(2)}) %collective-permute-start.4) | collective-permute-done | bytes 589856 | tf_op jit(solution)/shard_map/ppermute | solution.py:278
  53.5 0.8 collective-permute-done.5.refs_4_
  54.3 0.8 collective-permute-done.6.refs_5_
  55.2 0.6 src_prep.3
  55.7 5.3 %sweep.7 = f32[8,128,128]{2,1,0:T(8,128)S(1)} custom-call(s32[1]{0:T(128)} %bitcast.my_y, s32[6,128]{1,0:T(8,128)S(1)} %get-tuple-element.27.lists, f32[32,16,128]{2,1,0:T(8,128)S(1)} %all-to-all-done.tiles, bf16[32,48]{1,0:T(8,128)(2,1)S(1)} %copy-done.4, bf16[32,48]{1,0:T(8,128)(2,1)S(1)} %copy-done.3, bf16[48,48]{1,0:T(8,128)(2,1)S(1)} %copy-done.2, ...), custom_call_target="tpu_custom_call" | custom-call | flops 1000000 | bytes 1000000 | tf_op jit(solution)/shard_map/sweep/pallas_call | solution.py:195
  61.1 5.3 %sweep.8 = f32[8,128,128]{2,1,0:T(8,128)S(1)} custom-call(s32[1]{0:T(128)} %bitcast.my_y, s32[6,128]{1,0:T(8,128)S(1)} %get-tuple-element.27.lists, f32[32,16,128]{2,1,0:T(8,128)S(1)} %all-to-all-done.tiles, bf16[32,48]{1,0:T(8,128)(2,1)S(1)} %copy-done.4, bf16[32,48]{1,0:T(8,128)(2,1)S(1)} %copy-done.3, bf16[48,48]{1,0:T(8,128)(2,1)S(1)} %copy-done.2, ...), custom_call_target="tpu_custom_call" | custom-call | flops 1000000 | bytes 1000000 | tf_op jit(solution)/shard_map/sweep/pallas_call | solution.py:195
  66.4 1.4 %collective-permute-start.8 = (f32[8,128,128]{2,1,0:T(8,128)S(1)}, f32[8,128,128]{2,1,0:T(8,128)S(1)}, u32[]{:S(2)}, u32[]{:S(2)}) collective-permute-start(f32[8,128,128]{2,1,0:T(8,128)S(1)} %sweep.8), channel_id=1, source_target_pairs={{0,32},{32,8},{8,40},{40,0},{1,33},{33,9},{9,41},{41,1},{2,34},{34... | collective-permute-start | bytes 1572872 | tf_op jit(solution)/shard_map/ppermute | solution.py:301
  67.8 5.3 %sweep.9 = f32[8,128,128]{2,1,0:T(8,128)S(1)} custom-call(s32[1]{0:T(128)} %bitcast.my_y, s32[6,128]{1,0:T(8,128)S(1)} %get-tuple-element.27.lists, f32[32,16,128]{2,1,0:T(8,128)S(1)} %all-to-all-done.tiles, bf16[32,48]{1,0:T(8,128)(2,1)S(1)} %copy-done.4, bf16[32,48]{1,0:T(8,128)(2,1)S(1)} %copy-done.3, bf16[48,48]{1,0:T(8,128)(2,1)S(1)} %copy-done.2, ...), custom_call_target="tpu_custom_call" | custom-call | flops 1000000 | bytes 1000000 | tf_op jit(solution)/shard_map/sweep/pallas_call | solution.py:195
  73.1 2.2 %collective-permute-start.9 = (f32[8,128,128]{2,1,0:T(8,128)S(1)}, f32[8,128,128]{2,1,0:T(8,128)S(1)}, u32[]{:S(2)}, u32[]{:S(2)}) collective-permute-start(f32[8,128,128]{2,1,0:T(8,128)S(1)} %sweep.9), channel_id=1, source_target_pairs={{0,40},{32,0},{8,32},{40,8},{1,41},{33,1},{9,33},{41,9},{2,42},{34... | collective-permute-start | bytes 1572872 | tf_op jit(solution)/shard_map/ppermute | solution.py:301
  75.3 5.3 %sweep.6 = f32[8,128,128]{2,1,0:T(8,128)S(1)} custom-call(s32[1]{0:T(128)} %bitcast.my_y, s32[6,128]{1,0:T(8,128)S(1)} %get-tuple-element.27.lists, f32[32,16,128]{2,1,0:T(8,128)S(1)} %all-to-all-done.tiles, bf16[32,48]{1,0:T(8,128)(2,1)S(1)} %copy-done.4, bf16[32,48]{1,0:T(8,128)(2,1)S(1)} %copy-done.3, bf16[48,48]{1,0:T(8,128)(2,1)S(1)} %copy-done.2, ...), custom_call_target="tpu_custom_call" | custom-call | flops 1000000 | bytes 1000000 | tf_op jit(solution)/shard_map/sweep/pallas_call | solution.py:195
  80.6 7.2 %collective-permute-done.8 = f32[8,128,128]{2,1,0:T(8,128)S(1)} collective-permute-done((f32[8,128,128]{2,1,0:T(8,128)S(1)}, f32[8,128,128]{2,1,0:T(8,128)S(1)}, u32[]{:S(2)}, u32[]{:S(2)}) %collective-permute-start.8) | collective-permute-done | bytes 524320 | tf_op jit(solution)/shard_map/ppermute | solution.py:301
  88.0 24.6 %all_to_all.10 = f32[8,128,128]{2,1,0:T(8,128)S(1)} all-to-all(f32[8,128,128]{2,1,0:T(8,128)S(1)} %add_add_fusion), channel_id=1, replica_groups=mesh['x'=4,'yl'=2,'c'=2,'yh'=2,'z'=8] {'z'}, dimensions={0} | all-to-all | bytes 1048576 | tf_op jit(solution)/shard_map/all_to_all | solution.py:305
  112.6 0.6 add.114
  (58 shorter events, 2.4 us)
Async XLA Ops:
  0.0 23.3 %copy-start.9 = (bf16[48,128]{1,0:T(8,128)(2,1)S(1)}, bf16[48,128]{1,0:T(8,128)(2,1)}, u32[]{:S(2)}) copy-start(bf16[48,128]{1,0:T(8,128)(2,1)} %constant.66.clone.refs_5_.refs_9_) | copy-start | bytes 36868
  0.0 23.3 %copy-start.10 = (bf16[48,48]{1,0:T(8,128)(2,1)S(1)}, bf16[48,48]{1,0:T(8,128)(2,1)}, u32[]{:S(2)}) copy-start(bf16[48,48]{1,0:T(8,128)(2,1)} %constant.65.clone.refs_4_.refs_8_) | copy-start | bytes 13828
  0.0 23.3 %copy-start.11 = (bf16[32,48]{1,0:T(8,128)(2,1)S(1)}, bf16[32,48]{1,0:T(8,128)(2,1)}, u32[]{:S(2)}) copy-start(bf16[32,48]{1,0:T(8,128)(2,1)} %constant.64.clone.refs_3_.refs_7_) | copy-start | bytes 9220
  0.0 23.3 %copy-start.12 = (bf16[32,48]{1,0:T(8,128)(2,1)S(1)}, bf16[32,48]{1,0:T(8,128)(2,1)}, u32[]{:S(2)}) copy-start(bf16[32,48]{1,0:T(8,128)(2,1)} %constant.63.clone.refs_2_.refs_6_) | copy-start | bytes 9220
  0.0 10.9 %copy-start.14 = (f32[3,128]{1,0:T(4,128)S(1)}, f32[3,128]{1,0:T(4,128)}, u32[]{:S(2)}) copy-start(f32[3,128]{1,0:T(4,128)} %param.17) | copy-start | bytes 4612
  0.0 10.9 %copy-start.15 = (f32[2,128]{1,0:T(2,128)S(1)}, f32[2,128]{1,0:T(2,128)}, u32[]{:S(2)}) copy-start(f32[2,128]{1,0:T(2,128)} %param.18) | copy-start | bytes 3076
  5.0 30.7 %copy-start.2 = (bf16[48,48]{1,0:T(8,128)(2,1)S(1)}, bf16[48,48]{1,0:T(8,128)(2,1)}, u32[]{:S(2)}) copy-start(bf16[48,48]{1,0:T(8,128)(2,1)} %constant.62.clone.md) | copy-start | bytes 13828
  5.0 30.7 %copy-start.3 = (bf16[32,48]{1,0:T(8,128)(2,1)S(1)}, bf16[32,48]{1,0:T(8,128)(2,1)}, u32[]{:S(2)}) copy-start(bf16[32,48]{1,0:T(8,128)(2,1)} %constant.61.clone.ms) | copy-start | bytes 9220
  5.0 30.7 %copy-start.4 = (bf16[32,48]{1,0:T(8,128)(2,1)S(1)}, bf16[32,48]{1,0:T(8,128)(2,1)}, u32[]{:S(2)}) copy-start(bf16[32,48]{1,0:T(8,128)(2,1)} %constant.60.clone.mf) | copy-start | bytes 9220
  6.1 17.2 %collective-permute-start.3 = (f32[1152,128]{1,0:T(8,128)S(1)}, f32[1152,128]{1,0:T(8,128)S(1)}, u32[]{:S(2)}, u32[]{:S(2)}) collective-permute-start(f32[1152,128]{1,0:T(8,128)S(1)} %pad_maximum_fusion.refs_0_), channel_id=1, source_target_pairs={{0,16},{16,0},{1,17},{17,1},{2,18},{18,2},{3,19},{19,3},{4,20},{20... | collective-permute-start | bytes 1769480 | tf_op jit(solution)/shard_map/ppermute | solution.py:278
  6.2 45.1 %collective-permute-start.2 = (f32[1152,128]{1,0:T(8,128)S(1)}, f32[1152,128]{1,0:T(8,128)S(1)}, u32[]{:S(2)}, u32[]{:S(2)}) collective-permute-start(f32[1152,128]{1,0:T(8,128)S(1)} %pad_maximum_fusion.refs_0_), channel_id=1, source_target_pairs={{0,128},{64,192},{128,0},{192,64},{1,129},{65,193},{129,1},{193,65... | collective-permute-start | bytes 1769480 | tf_op jit(solution)/shard_map/ppermute | solution.py:275
  7.7 43.6 %collective-permute-start.1 = (f32[1152,128]{1,0:T(8,128)S(1)}, f32[1152,128]{1,0:T(8,128)S(1)}, u32[]{:S(2)}, u32[]{:S(2)}) collective-permute-start(f32[1152,128]{1,0:T(8,128)S(1)} %pad_maximum_fusion.refs_0_), channel_id=1, source_target_pairs={{0,192},{64,0},{128,64},{192,128},{1,193},{65,1},{129,65},{193,129... | collective-permute-start | bytes 1769480 | tf_op jit(solution)/shard_map/ppermute | solution.py:275
  9.4 42.0 %collective-permute-start = (f32[1152,128]{1,0:T(8,128)S(1)}, f32[1152,128]{1,0:T(8,128)S(1)}, u32[]{:S(2)}, u32[]{:S(2)}) collective-permute-start(f32[1152,128]{1,0:T(8,128)S(1)} %pad_maximum_fusion.refs_0_), channel_id=1, source_target_pairs={{0,64},{64,128},{128,192},{192,0},{1,65},{65,129},{129,193},{193,1... | collective-permute-start | bytes 1769480 | tf_op jit(solution)/shard_map/ppermute | solution.py:275
  11.8 23.8 %all-to-all-start = ((f32[32,16,128]{2,1,0:T(8,128)}), f32[32,16,128]{2,1,0:T(8,128)S(1)}, u32[]{:S(2)}, u32[]{:S(2)}) async-start(f32[32,16,128]{2,1,0:T(8,128)} %broadcast_in_dim.24), calls=%async_computation | async-start | bytes 524288 | tf_op jit(solution)/shard_map/all_to_all | solution.py:287
  23.7 0.8 copy-start
  24.5 0.7 copy-start.5
  25.2 0.6 copy-start.7
  35.7 1.1 copy-start.1
  36.7 0.9 copy-start.6
  37.6 0.9 copy-start.8
  51.4 2.1 %collective-permute-start.4 = (f32[1152,128]{1,0:T(8,128)S(1)}, f32[1152,128]{1,0:T(8,128)S(1)}, u32[]{:S(2)}, u32[]{:S(2)}) collective-permute-start(f32[1152,128]{1,0:T(8,128)S(1)} %collective-permute-done.refs_0_), channel_id=1, source_target_pairs={{0,16},{16,0},{1,17},{17,1},{2,18},{18,2},{3,19},{19,3},{4,20},{20... | collective-permute-start | bytes 1769480 | tf_op jit(solution)/shard_map/ppermute | solution.py:278
  51.5 2.8 %collective-permute-start.5 = (f32[1152,128]{1,0:T(8,128)S(1)}, f32[1152,128]{1,0:T(8,128)S(1)}, u32[]{:S(2)}, u32[]{:S(2)}) collective-permute-start(f32[1152,128]{1,0:T(8,128)S(1)} %collective-permute-done.1.refs_1_), channel_id=1, source_target_pairs={{0,16},{16,0},{1,17},{17,1},{2,18},{18,2},{3,19},{19,3},{4,20},{20... | collective-permute-start | bytes 1769480 | tf_op jit(solution)/shard_map/ppermute | solution.py:278
  52.0 3.2 %collective-permute-start.6 = (f32[1152,128]{1,0:T(8,128)S(1)}, f32[1152,128]{1,0:T(8,128)S(1)}, u32[]{:S(2)}, u32[]{:S(2)}) collective-permute-start(f32[1152,128]{1,0:T(8,128)S(1)} %collective-permute-done.2.refs_2_), channel_id=1, source_target_pairs={{0,16},{16,0},{1,17},{17,1},{2,18},{18,2},{3,19},{19,3},{4,20},{20... | collective-permute-start | bytes 1769480 | tf_op jit(solution)/shard_map/ppermute | solution.py:278
  61.0 19.6 %collective-permute-start.7 = (f32[8,128,128]{2,1,0:T(8,128)S(1)}, f32[8,128,128]{2,1,0:T(8,128)S(1)}, u32[]{:S(2)}, u32[]{:S(2)}) collective-permute-start(f32[8,128,128]{2,1,0:T(8,128)S(1)} %sweep.7), channel_id=1, source_target_pairs={{0,8},{32,40},{8,0},{40,32},{1,9},{33,41},{9,1},{41,33},{2,10},{34... | collective-permute-start | bytes 1572872 | tf_op jit(solution)/shard_map/ppermute | solution.py:301
  66.4 21.4 %collective-permute-start.8 = (f32[8,128,128]{2,1,0:T(8,128)S(1)}, f32[8,128,128]{2,1,0:T(8,128)S(1)}, u32[]{:S(2)}, u32[]{:S(2)}) collective-permute-start(f32[8,128,128]{2,1,0:T(8,128)S(1)} %sweep.8), channel_id=1, source_target_pairs={{0,32},{32,8},{8,40},{40,0},{1,33},{33,9},{9,41},{41,1},{2,34},{34... | collective-permute-start | bytes 1572872 | tf_op jit(solution)/shard_map/ppermute | solution.py:301
  73.1 14.8 %collective-permute-start.9 = (f32[8,128,128]{2,1,0:T(8,128)S(1)}, f32[8,128,128]{2,1,0:T(8,128)S(1)}, u32[]{:S(2)}, u32[]{:S(2)}) collective-permute-start(f32[8,128,128]{2,1,0:T(8,128)S(1)} %sweep.9), channel_id=1, source_target_pairs={{0,40},{32,0},{8,32},{40,8},{1,41},{33,1},{9,33},{41,9},{2,42},{34... | collective-permute-start | bytes 1572872 | tf_op jit(solution)/shard_map/ppermute | solution.py:301
  80.6 32.0 %copy-start.13 = (f32[128,128]{1,0:T(8,128)S(1)}, f32[128,128]{1,0:T(8,128)}, u32[]{:S(2)}) copy-start(f32[128,128]{1,0:T(8,128)} %param.24) | copy-start | bytes 196612

commit v3 on v2

--- a/solution.py
+++ b/solution.py
@@ -17,10 +17,11 @@
 GROUP = NX * NC
 NJ = NY * NZ
 CENTRE = 3.0
-ROWS = 16
-POS, NRM, DOT, SQA, SQB, ONE, LST = 0, 3, 6, 7, 8, 9, 10
+TILE = 16
+POS, NRM, AREA = 0, 3, 6
+ROWS, DOT, SQA, SQB, ONE = 16, 8, 9, 10, 11
 KF, KS, KD = 32, 32, 48
-VMEM_LIMIT = 24 << 20
+VMEM_LIMIT = 16 << 20
 UNROLL = 8
 
 
@@ -62,28 +63,84 @@
 def split_pieces(tile):
     row = lax.broadcasted_iota(jnp.int32, tile.shape, 0)
     fixed = row < NRM
-    high = jnp.where(fixed, jnp.round(tile * 32.0) * (1.0 / 32.0), tile).astype(jnp.bfloat16)
-    rest = tile - high.astype(jnp.float32)
-    mid = jnp.where(fixed, jnp.round(rest * 8192.0) * (1.0 / 8192.0), rest).astype(jnp.bfloat16)
+    coarse = jnp.where(fixed, jnp.round(tile * 32.0) * (1.0 / 32.0), tile)
+    along = -(
+        tile[NRM : NRM + 1] * tile[POS : POS + 1]
+        + tile[NRM + 1 : NRM + 2] * tile[POS + 1 : POS + 2]
+        + tile[NRM + 2 : NRM + 3] * tile[POS + 2 : POS + 3]
+    )
+    grid = [coarse[a : a + 1] for a in range(3)]
+    fine = [tile[a : a + 1] - grid[a] for a in range(3)]
+    square_a = grid[0] * grid[0] + grid[1] * grid[1] + grid[2] * grid[2]
+    square_b = (
+        fine[0] * (2.0 * grid[0] + fine[0])
+        + fine[1] * (2.0 * grid[1] + fine[1])
+        + fine[2] * (2.0 * grid[2] + fine[2])
+    ) + tile[AREA : AREA + 1]
+    derived = jnp.where(
+        row == 0,
+        along,
+        jnp.where(
+            row == 1, square_a, jnp.where(row == 2, square_b, jnp.where(row == 3, 1.0, 0.0))
+        ),
+    )
+    values = jnp.concatenate([tile, derived], axis=0)
+    high = jnp.concatenate([coarse, derived], axis=0).astype(jnp.bfloat16)
+    rest = values - high.astype(jnp.float32)
+    cut = lax.broadcasted_iota(jnp.int32, values.shape, 0) < NRM
+    mid = jnp.where(cut, jnp.round(rest * 8192.0) * (1.0 / 8192.0), rest).astype(jnp.bfloat16)
     low = (rest - mid.astype(jnp.float32)).astype(jnp.bfloat16)
     return jnp.concatenate([high, mid, low], axis=0)
 
 
 def dot(a, b):
     return jnp.dot(a, b, preferred_element_type=jnp.float32)
+
+
+def direction(angles):
+    polar, azimuth = angles[0:1], angles[1:2]
+    across = jnp.sin(polar)
+    return [across * jnp.cos(azimuth), across * jnp.sin(azimuth), jnp.cos(polar)]
+
+
+def pack_kernel(
+    incident, pos, angles, area, keep, lists, counts, recv_pos, recv_angles, packed, recv_tile
+):
+    packed[: SB * BS, :] = incident[...].astype(jnp.float32)
+    packed[SB * BS :, :] = jnp.zeros((SB * TILE, BS), jnp.float32)
+    scale = keep[...] * area[...] * (1.0 / np.pi)
+    rows = [pos[a : a + 1, :] - CENTRE for a in range(3)]
+    rows += [component * scale for component in direction(angles[...])]
+    rows += [area[...], jnp.zeros_like(scale)]
+    tile = jnp.concatenate(rows, axis=0)
+    slot = lax.broadcasted_iota(jnp.int32, (CAP, NYH * NZ), 0)
+    for k in range(SB):
+        at = SB * BS + k * TILE
+        packed[at : at + 8, :] = tile[:, k * BS : (k + 1) * BS]
+        for yl in range(NYL):
+            slab = ((k // NC) * NYL + yl) * NC + k % NC
+            live = slot < counts[slab : slab + 1, :]
+            marked = jnp.where(live, lists[slab], -1).astype(jnp.float32)
+            packed[at + 8 + yl * CAP : at + 8 + (yl + 1) * CAP, : NYH * NZ] = marked
+    rows = [recv_pos[a : a + 1, :] - CENTRE for a in range(3)]
+    rows += direction(recv_angles[...])
+    rows += [jnp.zeros((2, BS), jnp.float32)]
+    tile = jnp.concatenate(rows, axis=0)
+    for j in range(NJ):
+        recv_tile[j] = tile
 
 
 def src_prep_kernel(count, me, *refs):
     packed = refs[:count]
     mf, ms, md, nul, sf, ss, sd, em, lists = refs[count:]
-    list_at = SB * BS + me[0] * ROWS + LST
+    list_at = SB * BS + me[0] * TILE + 8
     for d in range(count):
         ref = packed[d]
         for k in range(SB):
             em[d * SB + k] = ref[k * BS : (k + 1) * BS, :].astype(jnp.bfloat16)
-        tiles = [ref[SB * BS + k * ROWS : SB * BS + (k + 1) * ROWS, :] for k in range(SB)]
+        tiles = [ref[SB * BS + k * TILE : SB * BS + k * TILE + 8, :] for k in range(SB)]
         q = split_pieces(jnp.concatenate(tiles, axis=1))
-        lists[d : d + 1, :] = ref[pl.ds(list_at, 1), :].astype(jnp.int32)
+        lists[d] = ref[pl.ds(pl.multiple_of(list_at, 8), 8), :].astype(jnp.int32)
         for m, out in ((mf, sf), (ms, ss), (md, sd)):
             values = dot(m[...], q).astype(jnp.bfloat16)
             for k in range(SB):
@@ -114,12 +171,14 @@
         out[j] = before[base + j] if added else jnp.zeros((BS, BS), jnp.float32)
 
     def one_block(j, n):
+        row = (((base + j) >> 4)) * CAP
+        lane = (base + j) & (NYH * NZ - 1)
         for t in range(slots):
             owner[n // 2 + t] = j
         for d in range(count):
             used = []
             for c in range(CAP):
-                value = lists[d, (base + j) * CAP + c]
+                value = lists[d, row + c, lane]
                 ids[n + c] = d * SB + value
                 used.append((value >= 0).astype(jnp.int32))
             n = n + ((used[0] + used[1]) + (used[2] + used[3]))
@@ -178,7 +237,7 @@
             bf16_shape(rows, KS, BS),
             bf16_shape(rows, KD, BS),
             bf16_shape(rows, BS, BS),
-            jax.ShapeDtypeStruct((count, BS), jnp.int32),
+            jax.ShapeDtypeStruct((count, 8, BS), jnp.int32),
         ],
         in_specs=[SMEM_SPEC] + [VMEM_SPEC] * (count + 4),
         out_specs=[VMEM_SPEC] * 5,
@@ -210,29 +269,19 @@
     )(my_y, lists, tiles, *mats, *src, *extra)
 
 
-def normals(angle_rows):
-    polar = angle_rows[0]
-    azimuth = angle_rows[1]
-    return jnp.stack(
-        [jnp.sin(polar) * jnp.cos(azimuth), jnp.sin(polar) * jnp.sin(azimuth), jnp.cos(polar)]
-    )
-
-
-def base_rows(pos, direction, extra):
-    centred = pos - CENTRE
-    coarse = jnp.round(centred * 32.0) * (1.0 / 32.0)
-    fine = centred - coarse
-    square_a = coarse[0] * coarse[0] + coarse[1] * coarse[1] + coarse[2] * coarse[2]
-    square_b = (
-        fine[0] * (2.0 * coarse[0] + fine[0])
-        + fine[1] * (2.0 * coarse[1] + fine[1])
-        + fine[2] * (2.0 * coarse[2] + fine[2])
-    ) + extra
-    along = -(
-        direction[0] * centred[0] + direction[1] * centred[1] + direction[2] * centred[2]
-    )
-    rows = [centred, direction, along[None], square_a[None], square_b[None]]
-    return jnp.concatenate(rows + [jnp.ones_like(along)[None]], axis=0)
+def pack(*operands):
+    return pl.pallas_call(
+        pack_kernel,
+        out_shape=[
+            jax.ShapeDtypeStruct((SB * (BS + TILE), BS), jnp.float32),
+            jax.ShapeDtypeStruct((NJ, 8, BS), jnp.float32),
+        ],
+        in_specs=[VMEM_SPEC] * 9,
+        out_specs=[VMEM_SPEC] * 2,
+        name="pack",
+        compiler_params=PARAMS,
+        cost_estimate=pl.CostEstimate(flops=10**6, bytes_accessed=10**6, transcendentals=0),
+    )(*operands)
 
 
 def y_route(distance):
@@ -259,17 +308,17 @@
     src_mats = [jnp.asarray(s, BF16) for _, s in mats]
     nul = jnp.asarray(null_spread(), BF16)
 
-    scale = reemission * src_area * (1.0 / np.pi)
-    rows = base_rows(src_pos, normals(src_angles) * scale, src_area)
-    rows = rows.reshape(LST, SB, BS).transpose(1, 0, 2)
-    slots = jnp.arange(CAP, dtype=jnp.int32)
-    live = slots < visible_counts[0, 0][:, :, None]
-    marked = jnp.where(live, visible_lists[0, 0], -1)
-    marked = marked.reshape(NX, NYL, NC, NYH, NZ, CAP).transpose(0, 2, 1, 3, 4, 5)
-    marked = marked.reshape(GROUP, 1, NJ * CAP).astype(jnp.float32)
-    rest = jnp.zeros((SB, ROWS - LST - 1, BS), jnp.float32)
-    tiles = jnp.concatenate([rows, marked, rest], axis=1).reshape(SB * ROWS, BS)
-    mine = jnp.concatenate([incident.astype(jnp.float32), tiles], axis=0)
+    mine, recv_tile = pack(
+        incident,
+        src_pos,
+        src_angles,
+        src_area.reshape(1, SB * BS),
+        reemission.reshape(1, SB * BS),
+        visible_lists[0, 0].transpose(0, 2, 1),
+        visible_counts[0, 0],
+        recv_pos,
+        recv_angles,
+    )
 
     def along_x(block, distance):
         return lax.ppermute(block, "x", [(i, (i + distance) % NX) for i in range(NX)])
@@ -282,15 +331,12 @@
     far = [along_x(mine, d) for d in (1, 3, 2)]
     near = [mine, other_core(mine)]
 
-    recv_rows = base_rows(recv_pos, normals(recv_angles), jnp.zeros((BS,), jnp.float32))
-    recv_tile = jnp.concatenate([recv_rows, jnp.zeros((ROWS - LST, BS), jnp.float32)], axis=0)
-    tiles = lax.all_to_all(
-        jnp.broadcast_to(recv_tile, (NJ, ROWS, BS)), ("yl", "yh", "z"), 0, 0, tiled=True
-    )
-
-    begun = sweep(my_y, 0, tiles, recv_mats, src_prep(me, near, src_mats, nul), NJ)
-    far = lax.optimization_barrier((*far, begun))
-    far, begun = list(far[:3]), far[3]
+    tiles = lax.all_to_all(recv_tile, ("yl", "yh", "z"), 0, 0, tiled=True)
+
+    near = src_prep(me, near, src_mats, nul)
+    begun = sweep(my_y, 0, tiles, recv_mats, near, NJ)
+    far = lax.optimization_barrier((*far, tiles, near[0]))
+    far = list(far[:3])
     far = far + [other_core(block) for block in far]
     src = src_prep(me, far, src_mats, nul)
 

time: 115 us -> 124 us (1.078)
  local copies, waits for them, and re-layouts: 8.01 us -> 14.9 us
  waiting for transfers between devices: 20.2 us -> 13.4 us
  starting transfers between devices: 20.6 us -> 25.7 us
  blocking collectives: 24.6 us -> 28.8 us
  Pallas kernels: 34.9 us -> 38.8 us
  other arithmetic: 4.6 us -> 0.8 us
    unnamed x32 -> x52, local copies, waits for them, and re-layouts: 5.02 us -> 14.9 us
    ppermute x3, starting transfers between devices: 3.65 us -> 8.97 us  [along_y(): return lax.ppermute(block, ('yl', 'yh'), y_route(distance))]
    all_to_all x1, blocking collectives: 24.6 us -> 28.8 us  [shards(): pieces = lax.all_to_all(total, 'z', 0, 0, tiled=True)]
    all_to_all x1, waiting for transfers between devices: 9.84 us -> 5.8 us  [shards(): tiles = lax.all_to_all(recv_tile, ('yl', 'yh', 'z'), 0, 0, tiled=True)]
    ppermute x3, waiting for transfers between devices: 0.01 us -> 3.26 us  [along_x(): lax.ppermute(block, 'x', [(i, (i + distance) % NX) for i in range(NX)])]
    ppermute x4, waiting for transfers between devices: 3.08 us -> 0.01 us  [other_core(): return lax.ppermute(block, 'c', [(0, 1), (1, 0)])]
    ppermute x3, waiting for transfers between devices: 7.3 us -> 4.28 us  [along_y(): return lax.ppermute(block, ('yl', 'yh'), y_route(distance))]
    pallas_call x5, Pallas kernels: 34 us -> 35.9 us  [sweep(): pl.pallas_call(functools.partial(sweep_kernel, count, blocks, before is n...]
  transfers between devices with their start and end apart: 11 -> 11, of which waited for: 6 -> 4; matrix products, arithmetic and copies ran while one was open for 1% -> 0% of each run, Pallas kernels for 26% -> 24%
where the time goes in v3:
time: 124 us; the launch traced here: 122 us
  Pallas kernels  38.8 us (31%)
  blocking collectives  28.8 us (23%)
  starting transfers between devices  25.7 us (21%)
  local copies, waits for them, and re-layouts  14.9 us (12%)
  waiting for transfers between devices  13.4 us (11%)
    pallas_call x5, Pallas kernels, sweep(): pl.pallas_call(functools.partial(sweep_kernel, count, blocks, before is n...  35.9 us
    all_to_all x1, blocking collectives, shards(): pieces = lax.all_to_all(total, 'z', 0, 0, tiled=True)  28.8 us
    unnamed x52, local copies, waits for them, and re-layouts  14.9 us
    all_to_all x1, starting transfers between devices, shards(): tiles = lax.all_to_all(recv_tile, ('yl', 'yh', 'z'), 0, 0, tiled=True)  11.5 us
    ppermute x3, starting transfers between devices, along_y(): return lax.ppermute(block, ('yl', 'yh'), y_route(distance))  8.97 us
    all_to_all x1, waiting for transfers between devices, shards(): tiles = lax.all_to_all(recv_tile, ('yl', 'yh', 'z'), 0, 0, tiled=True)  5.8 us
    ppermute x3, starting transfers between devices, along_x(): lax.ppermute(block, 'x', [(i, (i + distance) % NX) for i in range(NX)])  4.64 us
    ppermute x3, waiting for transfers between devices, along_y(): return lax.ppermute(block, ('yl', 'yh'), y_route(distance))  4.28 us
  transfers between devices with their start and end apart: 11, of which 4 were waited for; matrix products, arithmetic and copies ran while one was open for 0% of the time, Pallas kernels for 24%

profile of v3, /device:TPU:6, one launch (start us, length us, event | category | flops | bytes accessed | tf_op | source)
XLA Modules:
  0.0 122.5 jit_solution(15380323294524946194)
XLA Ops:
  0.0 0.9 copy-done.3
  1.0 0.8 copy-done.17
  1.7 0.7 copy-done.18
  2.4 0.7 copy-done.19
  3.1 0.7 copy-done.20
  6.6 0.7 pack.1
  7.3 1.4 %collective-permute-start.2 = (f32[1152,128]{1,0:T(8,128)S(1)}, f32[1152,128]{1,0:T(8,128)S(1)}, u32[]{:S(2)}, u32[]{:S(2)}) collective-permute-start(f32[1152,128]{1,0:T(8,128)S(1)} %get-tuple-element.20.refs_0_), channel_id=1, source_target_pairs={{0,128},{64,192},{128,0},{192,64},{1,129},{65,193},{129,1},{193,65... | collective-permute-start | bytes 1769480 | tf_op jit(solution)/shard_map/ppermute | solution.py:324
  8.7 1.7 %collective-permute-start.1 = (f32[1152,128]{1,0:T(8,128)S(1)}, f32[1152,128]{1,0:T(8,128)S(1)}, u32[]{:S(2)}, u32[]{:S(2)}) collective-permute-start(f32[1152,128]{1,0:T(8,128)S(1)} %get-tuple-element.20.refs_0_), channel_id=1, source_target_pairs={{0,192},{64,0},{128,64},{192,128},{1,193},{65,1},{129,65},{193,129... | collective-permute-start | bytes 1769480 | tf_op jit(solution)/shard_map/ppermute | solution.py:324
  10.3 1.6 %collective-permute-start = (f32[1152,128]{1,0:T(8,128)S(1)}, f32[1152,128]{1,0:T(8,128)S(1)}, u32[]{:S(2)}, u32[]{:S(2)}) collective-permute-start(f32[1152,128]{1,0:T(8,128)S(1)} %get-tuple-element.20.refs_0_), channel_id=1, source_target_pairs={{0,64},{64,128},{128,192},{192,0},{1,65},{65,129},{129,193},{193,1... | collective-permute-start | bytes 1769480 | tf_op jit(solution)/shard_map/ppermute | solution.py:324
  11.9 11.5 %all-to-all-start = ((f32[32,8,128]{2,1,0:T(8,128)}), f32[32,8,128]{2,1,0:T(8,128)S(1)}, u32[]{:S(2)}, u32[]{:S(2)}) async-start(f32[32,8,128]{2,1,0:T(8,128)} %get-tuple-element.21), calls=%async_computation | async-start | bytes 262144 | tf_op jit(solution)/shard_map/all_to_all | solution.py:334
  23.4 0.7 copy-done.9
  24.1 0.7 copy-done.11
  24.8 0.7 copy-done.13
  25.5 0.7 copy-done.15
  26.6 0.8 copy-done
  28.1 5.8 %all-to-all-done.tiles = f32[32,8,128]{2,1,0:T(8,128)S(1)} async-done(((f32[32,8,128]{2,1,0:T(8,128)}), f32[32,8,128]{2,1,0:T(8,128)S(1)}, u32[]{:S(2)}, u32[]{:S(2)}) %all-to-all-start) | async-done | bytes 131104 | tf_op jit(solution)/shard_map/all_to_all | solution.py:334
  33.9 3.3 %collective-permute-done.1.refs_1_ = f32[1152,128]{1,0:T(8,128)S(1)} collective-permute-done((f32[1152,128]{1,0:T(8,128)S(1)}, f32[1152,128]{1,0:T(8,128)S(1)}, u32[]{:S(2)}, u32[]{:S(2)}) %collective-permute-start.1) | collective-permute-done | bytes 589856 | tf_op jit(solution)/shard_map/ppermute | solution.py:324
  37.7 1.1 copy-done.1
  38.8 0.7 copy-done.2
  40.2 0.7 copy-done.5
  40.9 0.9 copy-done.8
  41.8 8.7 %sweep.5.refs_0_ = f32[32,128,128]{2,1,0:T(8,128)S(1)} custom-call(s32[1]{0:T(128)} %bitcast.my_y, s32[2,8,128]{2,1,0:T(8,128)S(1)} %get-tuple-element.31.lists, f32[32,8,128]{2,1,0:T(8,128)S(1)} %all-to-all-done.tiles, bf16[32,48]{1,0:T(8,128)(2,1)S(1)} %copy-done.5, bf16[32,48]{1,0:T(8,128)(2,1)S(1)} %copy-done.4, bf16[48,48]{1,0:T(8,128)(2,1)S(1)} %copy-done.2, ...), custom_call_target="tpu_custom_call" | custom-call | flops 1000000 | bytes 1000000 | tf_op jit(solution)/shard_map/sweep/pallas_call | solution.py:254
  50.6 1.8 %src_prep.3 = (bf16[49,32,128]{2,1,0:T(8,128)(2,1)S(1)}, bf16[49,32,128]{2,1,0:T(8,128)(2,1)S(1)}, bf16[49,48,128]{2,1,0:T(8,128)(2,1)S(1)}, bf16[49,128,128]{2,1,0:T(8,128)(2,1)S(1)}, s32[6,8,128]{2,1,0:T(8,128)S(1)}) custom-call(s32[1]{0:T(128)} %bitcast.1.me, f32[1152,128]{1,0:T(8,128)S(1)} %collective-permute-done.refs_0_, ...), custom_call_target="tpu_custom_call" | custom-call | flops 1000000 | bytes 1000000 | tf_op jit(solution)/shard_map/src_prep/pallas_call | solution.py:233
  52.4 7.0 %sweep.7 = f32[8,128,128]{2,1,0:T(8,128)S(1)} custom-call(s32[1]{0:T(128)} %bitcast.my_y, s32[6,8,128]{2,1,0:T(8,128)S(1)} %get-tuple-element.26.lists, f32[32,8,128]{2,1,0:T(8,128)S(1)} %all-to-all-done.tiles, bf16[32,48]{1,0:T(8,128)(2,1)S(1)} %copy-done.6, bf16[32,48]{1,0:T(8,128)(2,1)S(1)} %copy-done.4, bf16[48,48]{1,0:T(8,128)(2,1)S(1)} %copy-done.2, ...), custom_call_target="tpu_custom_call" | custom-call | flops 1000000 | bytes 1000000 | tf_op jit(solution)/shard_map/sweep/pallas_call | solution.py:254
  59.4 6.1 %collective-permute-start.7 = (f32[8,128,128]{2,1,0:T(8,128)S(1)}, f32[8,128,128]{2,1,0:T(8,128)S(1)}, u32[]{:S(2)}, u32[]{:S(2)}) collective-permute-start(f32[8,128,128]{2,1,0:T(8,128)S(1)} %sweep.7), channel_id=1, source_target_pairs={{0,8},{32,40},{8,0},{40,32},{1,9},{33,41},{9,1},{41,33},{2,10},{34... | collective-permute-start | bytes 1572872 | tf_op jit(solution)/shard_map/ppermute | solution.py:347
  65.5 6.3 %sweep.8 = f32[8,128,128]{2,1,0:T(8,128)S(1)} custom-call(s32[1]{0:T(128)} %bitcast.my_y, s32[6,8,128]{2,1,0:T(8,128)S(1)} %get-tuple-element.26.lists, f32[32,8,128]{2,1,0:T(8,128)S(1)} %all-to-all-done.tiles, bf16[32,48]{1,0:T(8,128)(2,1)S(1)} %copy-done.6, bf16[32,48]{1,0:T(8,128)(2,1)S(1)} %copy-done.4, bf16[48,48]{1,0:T(8,128)(2,1)S(1)} %copy-done.2, ...), custom_call_target="tpu_custom_call" | custom-call | flops 1000000 | bytes 1000000 | tf_op jit(solution)/shard_map/sweep/pallas_call | solution.py:254
  72.0 7.0 %sweep.9 = f32[8,128,128]{2,1,0:T(8,128)S(1)} custom-call(s32[1]{0:T(128)} %bitcast.my_y, s32[6,8,128]{2,1,0:T(8,128)S(1)} %get-tuple-element.26.lists, f32[32,8,128]{2,1,0:T(8,128)S(1)} %all-to-all-done.tiles, bf16[32,48]{1,0:T(8,128)(2,1)S(1)} %copy-done.6, bf16[32,48]{1,0:T(8,128)(2,1)S(1)} %copy-done.4, bf16[48,48]{1,0:T(8,128)(2,1)S(1)} %copy-done.2, ...), custom_call_target="tpu_custom_call" | custom-call | flops 1000000 | bytes 1000000 | tf_op jit(solution)/shard_map/sweep/pallas_call | solution.py:254
  79.0 2.6 %collective-permute-start.9 = (f32[8,128,128]{2,1,0:T(8,128)S(1)}, f32[8,128,128]{2,1,0:T(8,128)S(1)}, u32[]{:S(2)}, u32[]{:S(2)}) collective-permute-start(f32[8,128,128]{2,1,0:T(8,128)S(1)} %sweep.9), channel_id=1, source_target_pairs={{0,40},{32,0},{8,32},{40,8},{1,41},{33,1},{9,33},{41,9},{2,42},{34... | collective-permute-start | bytes 1572872 | tf_op jit(solution)/shard_map/ppermute | solution.py:347
  81.6 7.0 %sweep.6 = f32[8,128,128]{2,1,0:T(8,128)S(1)} custom-call(s32[1]{0:T(128)} %bitcast.my_y, s32[6,8,128]{2,1,0:T(8,128)S(1)} %get-tuple-element.26.lists, f32[32,8,128]{2,1,0:T(8,128)S(1)} %all-to-all-done.tiles, bf16[32,48]{1,0:T(8,128)(2,1)S(1)} %copy-done.6, bf16[32,48]{1,0:T(8,128)(2,1)S(1)} %copy-done.4, bf16[48,48]{1,0:T(8,128)(2,1)S(1)} %copy-done.2, ...), custom_call_target="tpu_custom_call" | custom-call | flops 1000000 | bytes 1000000 | tf_op jit(solution)/shard_map/sweep/pallas_call | solution.py:254
  88.6 0.7 collective-permute-done.8
  89.3 3.6 %collective-permute-done.9 = f32[8,128,128]{2,1,0:T(8,128)S(1)} collective-permute-done((f32[8,128,128]{2,1,0:T(8,128)S(1)}, f32[8,128,128]{2,1,0:T(8,128)S(1)}, u32[]{:S(2)}, u32[]{:S(2)}) %collective-permute-start.9) | collective-permute-done | bytes 524320 | tf_op jit(solution)/shard_map/ppermute | solution.py:347
  93.0 28.8 %all_to_all.10 = f32[8,128,128]{2,1,0:T(8,128)S(1)} all-to-all(f32[8,128,128]{2,1,0:T(8,128)S(1)} %add_add_fusion), channel_id=1, replica_groups=mesh['x'=4,'yl'=2,'c'=2,'yh'=2,'z'=8] {'z'}, dimensions={0} | all-to-all | bytes 1048576 | tf_op jit(solution)/shard_map/all_to_all | solution.py:351
  (54 shorter events, 6.1 us)
Async XLA Ops:
  0.0 0.9 copy-start.3
  1.0 0.8 copy-start.17
  1.7 0.7 copy-start.18
  2.4 0.7 copy-start.19
  3.1 0.7 copy-start.20
  7.3 16.2 %collective-permute-start.3 = (f32[1152,128]{1,0:T(8,128)S(1)}, f32[1152,128]{1,0:T(8,128)S(1)}, u32[]{:S(2)}, u32[]{:S(2)}) collective-permute-start(f32[1152,128]{1,0:T(8,128)S(1)} %get-tuple-element.20.refs_0_), channel_id=1, source_target_pairs={{0,16},{16,0},{1,17},{17,1},{2,18},{18,2},{3,19},{19,3},{4,20},{20... | collective-permute-start | bytes 1769480 | tf_op jit(solution)/shard_map/ppermute | solution.py:327
  7.3 26.6 %collective-permute-start.2 = (f32[1152,128]{1,0:T(8,128)S(1)}, f32[1152,128]{1,0:T(8,128)S(1)}, u32[]{:S(2)}, u32[]{:S(2)}) collective-permute-start(f32[1152,128]{1,0:T(8,128)S(1)} %get-tuple-element.20.refs_0_), channel_id=1, source_target_pairs={{0,128},{64,192},{128,0},{192,64},{1,129},{65,193},{129,1},{193,65... | collective-permute-start | bytes 1769480 | tf_op jit(solution)/shard_map/ppermute | solution.py:324
  8.7 28.5 %collective-permute-start.1 = (f32[1152,128]{1,0:T(8,128)S(1)}, f32[1152,128]{1,0:T(8,128)S(1)}, u32[]{:S(2)}, u32[]{:S(2)}) collective-permute-start(f32[1152,128]{1,0:T(8,128)S(1)} %get-tuple-element.20.refs_0_), channel_id=1, source_target_pairs={{0,192},{64,0},{128,64},{192,128},{1,193},{65,1},{129,65},{193,129... | collective-permute-start | bytes 1769480 | tf_op jit(solution)/shard_map/ppermute | solution.py:324
  10.3 26.8 %collective-permute-start = (f32[1152,128]{1,0:T(8,128)S(1)}, f32[1152,128]{1,0:T(8,128)S(1)}, u32[]{:S(2)}, u32[]{:S(2)}) collective-permute-start(f32[1152,128]{1,0:T(8,128)S(1)} %get-tuple-element.20.refs_0_), channel_id=1, source_target_pairs={{0,64},{64,128},{128,192},{192,0},{1,65},{65,129},{129,193},{193,1... | collective-permute-start | bytes 1769480 | tf_op jit(solution)/shard_map/ppermute | solution.py:324
  11.9 22.0 %all-to-all-start = ((f32[32,8,128]{2,1,0:T(8,128)}), f32[32,8,128]{2,1,0:T(8,128)S(1)}, u32[]{:S(2)}, u32[]{:S(2)}) async-start(f32[32,8,128]{2,1,0:T(8,128)} %get-tuple-element.21), calls=%async_computation | async-start | bytes 262144 | tf_op jit(solution)/shard_map/all_to_all | solution.py:334
  23.4 0.7 copy-start.9
  24.1 0.7 copy-start.11
  24.8 0.7 copy-start.13
  25.5 0.7 copy-start.15
  26.2 24.3 %copy-start.10 = (bf16[48,128]{1,0:T(8,128)(2,1)S(1)}, bf16[48,128]{1,0:T(8,128)(2,1)}, u32[]{:S(2)}) copy-start(bf16[48,128]{1,0:T(8,128)(2,1)} %constant.43.clone.refs_5_.refs_9_) | copy-start | bytes 36868
  26.2 24.3 %copy-start.12 = (bf16[48,48]{1,0:T(8,128)(2,1)S(1)}, bf16[48,48]{1,0:T(8,128)(2,1)}, u32[]{:S(2)}) copy-start(bf16[48,48]{1,0:T(8,128)(2,1)} %constant.42.clone.refs_4_.refs_8_) | copy-start | bytes 13828
  26.2 24.3 %copy-start.14 = (bf16[32,48]{1,0:T(8,128)(2,1)S(1)}, bf16[32,48]{1,0:T(8,128)(2,1)}, u32[]{:S(2)}) copy-start(bf16[32,48]{1,0:T(8,128)(2,1)} %constant.41.clone.refs_3_.refs_7_) | copy-start | bytes 9220
  26.2 24.3 %copy-start.16 = (bf16[32,48]{1,0:T(8,128)(2,1)S(1)}, bf16[32,48]{1,0:T(8,128)(2,1)}, u32[]{:S(2)}) copy-start(bf16[32,48]{1,0:T(8,128)(2,1)} %constant.40.clone.refs_2_.refs_6_) | copy-start | bytes 9220
  26.6 0.8 copy-start
  37.2 13.4 %collective-permute-start.4 = (f32[1152,128]{1,0:T(8,128)S(1)}, f32[1152,128]{1,0:T(8,128)S(1)}, u32[]{:S(2)}, u32[]{:S(2)}) collective-permute-start(f32[1152,128]{1,0:T(8,128)S(1)} %collective-permute-done.refs_0_), channel_id=1, source_target_pairs={{0,16},{16,0},{1,17},{17,1},{2,18},{18,2},{3,19},{19,3},{4,20},{20... | collective-permute-start | bytes 1769480 | tf_op jit(solution)/shard_map/ppermute | solution.py:327
  37.2 13.3 %collective-permute-start.5 = (f32[1152,128]{1,0:T(8,128)S(1)}, f32[1152,128]{1,0:T(8,128)S(1)}, u32[]{:S(2)}, u32[]{:S(2)}) collective-permute-start(f32[1152,128]{1,0:T(8,128)S(1)} %collective-permute-done.1.refs_1_), channel_id=1, source_target_pairs={{0,16},{16,0},{1,17},{17,1},{2,18},{18,2},{3,19},{19,3},{4,20},{20... | collective-permute-start | bytes 1769480 | tf_op jit(solution)/shard_map/ppermute | solution.py:327
  37.7 12.9 %collective-permute-start.6 = (f32[1152,128]{1,0:T(8,128)S(1)}, f32[1152,128]{1,0:T(8,128)}, u32[]{:S(2)}, u32[]{:S(2)}) collective-permute-start(f32[1152,128]{1,0:T(8,128)S(1)} %collective-permute-done.2.refs_2_), channel_id=1, source_target_pairs={{0,16},{16,0},{1,17},{17,1},{2,18},{18,2},{3,19},{19,3},{4,20},{20... | collective-permute-start | bytes 1769480 | tf_op jit(solution)/shard_map/ppermute | solution.py:327
  37.7 1.1 copy-start.1
  38.8 0.7 copy-start.2
  39.5 0.7 copy-start.4
  40.2 0.7 copy-start.5
  40.9 0.9 copy-start.8
  50.5 1.9 %copy-start.6 = (bf16[32,48]{1,0:T(8,128)(2,1)S(1)}, bf16[32,48]{1,0:T(8,128)(2,1)}, u32[]{:S(2)}) copy-start(bf16[32,48]{1,0:T(8,128)(2,1)} %constant.37.clone.mf) | copy-start | bytes 9220
  59.4 29.2 %collective-permute-start.7 = (f32[8,128,128]{2,1,0:T(8,128)S(1)}, f32[8,128,128]{2,1,0:T(8,128)S(1)}, u32[]{:S(2)}, u32[]{:S(2)}) collective-permute-start(f32[8,128,128]{2,1,0:T(8,128)S(1)} %sweep.7), channel_id=1, source_target_pairs={{0,8},{32,40},{8,0},{40,32},{1,9},{33,41},{9,1},{41,33},{2,10},{34... | collective-permute-start | bytes 1572872 | tf_op jit(solution)/shard_map/ppermute | solution.py:347
  71.7 17.6 %collective-permute-start.8 = (f32[8,128,128]{2,1,0:T(8,128)S(1)}, f32[8,128,128]{2,1,0:T(8,128)S(1)}, u32[]{:S(2)}, u32[]{:S(2)}) collective-permute-start(f32[8,128,128]{2,1,0:T(8,128)S(1)} %sweep.8), channel_id=1, source_target_pairs={{0,32},{32,8},{8,40},{40,0},{1,33},{33,9},{9,41},{41,1},{2,34},{34... | collective-permute-start | bytes 1572872 | tf_op jit(solution)/shard_map/ppermute | solution.py:347
  79.0 13.9 %collective-permute-start.9 = (f32[8,128,128]{2,1,0:T(8,128)S(1)}, f32[8,128,128]{2,1,0:T(8,128)S(1)}, u32[]{:S(2)}, u32[]{:S(2)}) collective-permute-start(f32[8,128,128]{2,1,0:T(8,128)S(1)} %sweep.9), channel_id=1, source_target_pairs={{0,40},{32,0},{8,32},{40,8},{1,41},{33,1},{9,33},{41,9},{2,42},{34... | collective-permute-start | bytes 1572872 | tf_op jit(solution)/shard_map/ppermute | solution.py:347
  88.6 33.3 %copy-start.25 = (f32[128,128]{1,0:T(8,128)S(1)}, f32[128,128]{1,0:T(8,128)}, u32[]{:S(2)}) copy-start(f32[128,128]{1,0:T(8,128)} %param.24) | copy-start | bytes 196612
  (5 other events, 3.4 us)

commit v4 on v3

--- a/solution.py
+++ b/solution.py
@@ -22,42 +22,49 @@
 ROWS, DOT, SQA, SQB, ONE = 16, 8, 9, 10, 11
 KF, KS, KD = 32, 32, 48
 VMEM_LIMIT = 16 << 20
-UNROLL = 8
-
-
-def selection_matrices():
+UNROLL, TAIL = 16, 4
+HALF = NZ // 2
+FIRST = 4 * BS
+
+
+def contraction_terms():
     pieces = [(i, j) for i in range(3) for j in range(3) if i + j < 4]
 
-    def build(depth, terms):
-        recv = np.zeros((depth, 3 * ROWS), np.float32)
-        src = np.zeros((depth, 3 * ROWS), np.float32)
-        for at, (scale, ri, rrow, si, srow) in enumerate(terms):
-            recv[at, ri * ROWS + rrow] = scale
-            src[at, si * ROWS + srow] = 1.0
-        return recv, src
-
     def product(scale, rrow, srow):
-        return [(scale, i, rrow + a, j, srow + a) for i, j in pieces for a in range(3)]
+        return [
+            (scale, i * ROWS + rrow + a, j * ROWS + srow + a) for i, j in pieces for a in range(3)
+        ]
 
     def from_recv(row, count):
-        return [(1.0, i, row, 0, ONE) for i in range(count)]
+        return [(1.0, i * ROWS + row, ONE) for i in range(count)]
 
     def from_src(row, count):
-        return [(1.0, 0, ONE, i, row) for i in range(count)]
+        return [(1.0, ONE, i * ROWS + row) for i in range(count)]
 
     facing = product(1.0, NRM, POS) + from_recv(DOT, 3)
     seen = product(1.0, POS, NRM) + from_src(DOT, 3)
     cross = product(-2.0, POS, POS)
     spread = (
-        from_recv(SQA, 2) + from_src(SQA, 2) + cross + from_recv(SQB, 3) + from_src(SQB, 3)
+        from_src(SQA, 2) + from_recv(SQA, 2) + cross + from_recv(SQB, 3) + from_src(SQB, 3)
     )
-    return [build(KF, facing), build(KS, seen), build(KD, spread)]
-
-
-def null_spread():
-    column = np.zeros((KD, BS), np.float32)
-    column[2, :] = 1.0
-    return column
+    return (KF, facing), (KS, seen), (KD, spread)
+
+
+def selections(side):
+    made = []
+    for depth, terms in contraction_terms():
+        groups = []
+        for start in range(0, depth, 8):
+            row = lax.broadcasted_iota(jnp.int32, (8, 3 * ROWS), 0)
+            column = lax.broadcasted_iota(jnp.int32, (8, 3 * ROWS), 1)
+            group = jnp.zeros((8, 3 * ROWS), jnp.float32)
+            for at, term in enumerate(terms[start : start + 8]):
+                value = term[0] if side == 0 else 1.0
+                here = (row == at) & (column == term[1 + side])
+                group = jnp.where(here, value, group)
+            groups.append(group)
+        made.append(jnp.concatenate(groups, axis=0).astype(jnp.bfloat16))
+    return made
 
 
 def split_pieces(tile):
@@ -130,45 +137,64 @@
         recv_tile[j] = tile
 
 
-def src_prep_kernel(count, me, *refs):
-    packed = refs[:count]
-    mf, ms, md, nul, sf, ss, sd, em, lists = refs[count:]
-    list_at = SB * BS + me[0] * TILE + 8
+def src_prep_kernel(count, cut, me, *refs):
+    inputs = count + cut
+    sf, ss, sd, em, lists = refs[inputs:]
+    mats = selections(1)
+
+    def rows_of(d):
+        if d < count - cut:
+            return lambda start, size: refs[d][pl.ds(start, size), :]
+        first, second = refs[count - cut + 2 * (d - count + cut) :][:2]
+
+        def rows(start, size):
+            if isinstance(start, int) and start < FIRST:
+                return first[pl.ds(start, size), :]
+            return second[pl.ds(start - FIRST, size), :]
+
+        return rows
+
     for d in range(count):
-        ref = packed[d]
+        rows = rows_of(d)
         for k in range(SB):
-            em[d * SB + k] = ref[k * BS : (k + 1) * BS, :].astype(jnp.bfloat16)
-        tiles = [ref[SB * BS + k * TILE : SB * BS + k * TILE + 8, :] for k in range(SB)]
+            em[d * SB + k] = rows(k * BS, BS).astype(jnp.bfloat16)
+        tiles = [rows(SB * BS + k * TILE, 8) for k in range(SB)]
         q = split_pieces(jnp.concatenate(tiles, axis=1))
-        lists[d] = ref[pl.ds(pl.multiple_of(list_at, 8), 8), :].astype(jnp.int32)
-        for m, out in ((mf, sf), (ms, ss), (md, sd)):
-            values = dot(m[...], q).astype(jnp.bfloat16)
+        list_at = pl.multiple_of(SB * BS + me[0] * TILE + 8, 8)
+        lists[d] = rows(list_at, 8).astype(jnp.int32)
+        for m, out in zip(mats, (sf, ss, sd)):
+            values = dot(m, q).astype(jnp.bfloat16)
             for k in range(SB):
                 out[d * SB + k] = values[:, k * BS : (k + 1) * BS]
     null = count * SB
     em[null] = jnp.zeros((BS, BS), jnp.bfloat16)
     sf[null] = jnp.zeros((KF, BS), jnp.bfloat16)
     ss[null] = jnp.zeros((KS, BS), jnp.bfloat16)
-    sd[null] = nul[...]
-
-
-def sweep_kernel(count, blocks, added, distance, my_y, lists, tiles, mf, ms, md, sf, ss, sd, em, *refs):
-    if added:
+    first_row = lax.broadcasted_iota(jnp.int32, (KD, BS), 0) == 0
+    sd[null] = jnp.where(first_row, 1.0, 0.0).astype(jnp.bfloat16)
+
+
+def sweep_kernel(count, blocks, added, distance, my_y, lists, tiles, sf, ss, sd, em, *refs):
+    if added == 2:
+        before, passing, out, rf, rs, rd, ids, owner = refs
+    elif added:
         before, out, rf, rs, rd, ids, owner = refs
     else:
         out, rf, rs, rd, ids, owner = refs
     target = (my_y[0] + distance) & (NY - 1)
-    base = ((target & (NYL - 1)) * NYH + (target >> 1)) * NZ if added else 0
+    base = ((target & (NYL - 1)) * NYH + (target >> 1)) * NZ if blocks == NZ else 0
     null = count * SB
     slots = count * CAP // 2
 
+    mats = selections(0)
     for j in range(blocks):
         q = split_pieces(tiles[base + j])
-        for m, ref in ((mf, rf), (ms, rs), (md, rd)):
+        for m, ref in zip(mats, (rf, rs, rd)):
             ref[j] = lax.dot_general(
-                q, m[...], (((0,), (1,)), ((), ())), preferred_element_type=jnp.float32
+                q, m, (((0,), (1,)), ((), ())), preferred_element_type=jnp.float32
             ).astype(jnp.bfloat16)
-        out[j] = before[base + j] if added else jnp.zeros((BS, BS), jnp.float32)
+        start = before[base + j] if added else jnp.zeros((BS, BS), jnp.float32)
+        out[j] = start + passing[j - HALF] if added == 2 and j >= HALF else start
 
     def one_block(j, n):
         row = (((base + j) >> 4)) * CAP
@@ -186,9 +212,9 @@
         return n + n % 2
 
     n = lax.fori_loop(0, blocks, one_block, 0)
-    for t in range(2 * UNROLL):
+    for t in range(2 * TAIL):
         ids[n + t] = null
-    for t in range(UNROLL):
+    for t in range(TAIL):
         owner[n // 2 + t] = 0
 
     def front(u):
@@ -208,13 +234,20 @@
         j = owner[u]
         out[j] = out[j] + dot(values, jnp.concatenate([em[a], em[b]], axis=0))
 
-    def step(i, carry):
-        values = [front(i * UNROLL + r) for r in range(UNROLL)]
-        for r in range(UNROLL):
-            back(i * UNROLL + r, values[r])
-        return carry
-
-    lax.fori_loop(0, pl.cdiv(n // 2, UNROLL), step, 0)
+    def run(first_unit, width, steps):
+        def step(i, carry):
+            units = [first_unit + i * width + r for r in range(width)]
+            values = [front(u) for u in units]
+            for u, value in zip(units, values):
+                back(u, value)
+            return carry
+
+        lax.fori_loop(0, steps, step, 0)
+
+    units = n // 2
+    long = units // UNROLL
+    run(0, UNROLL, long)
+    run(long * UNROLL, TAIL, pl.cdiv(units - long * UNROLL, TAIL))
 
 
 VMEM_SPEC = pl.BlockSpec(memory_space=pltpu.VMEM)
@@ -227,11 +260,12 @@
     return jax.ShapeDtypeStruct(shape, BF16)
 
 
-def src_prep(me, packed, mats, nul):
-    count = len(packed)
+def src_prep(me, whole, parts=()):
+    packed = whole + [part for pair in parts for part in pair]
+    count = len(whole) + len(parts)
     rows = count * SB + 1
     return pl.pallas_call(
-        functools.partial(src_prep_kernel, count),
+        functools.partial(src_prep_kernel, count, len(parts)),
         out_shape=[
             bf16_shape(rows, KF, BS),
             bf16_shape(rows, KS, BS),
@@ -239,22 +273,21 @@
             bf16_shape(rows, BS, BS),
             jax.ShapeDtypeStruct((count, 8, BS), jnp.int32),
         ],
-        in_specs=[SMEM_SPEC] + [VMEM_SPEC] * (count + 4),
+        in_specs=[SMEM_SPEC] + [VMEM_SPEC] * len(packed),
         out_specs=[VMEM_SPEC] * 5,
         name="src_prep",
         compiler_params=PARAMS,
         cost_estimate=pl.CostEstimate(flops=10**6, bytes_accessed=10**6, transcendentals=0),
-    )(me, *packed, *mats, nul)
-
-
-def sweep(my_y, distance, tiles, mats, src, blocks, before=None):
+    )(me, *packed)
+
+
+def sweep(my_y, distance, tiles, src, blocks, *extra):
     *src, lists = src
     count = lists.shape[0]
-    extra = () if before is None else (before,)
     return pl.pallas_call(
-        functools.partial(sweep_kernel, count, blocks, before is not None, distance),
+        functools.partial(sweep_kernel, count, blocks, len(extra), distance),
         out_shape=jax.ShapeDtypeStruct((blocks, BS, BS), jnp.float32),
-        in_specs=[SMEM_SPEC] * 2 + [VMEM_SPEC] * (8 + len(extra)),
+        in_specs=[SMEM_SPEC] * 2 + [VMEM_SPEC] * (5 + len(extra)),
         out_specs=VMEM_SPEC,
         scratch_shapes=[
             pltpu.VMEM((blocks, BS, KF), BF16),
@@ -266,7 +299,7 @@
         name="sweep",
         compiler_params=PARAMS,
         cost_estimate=pl.CostEstimate(flops=10**6, bytes_accessed=10**6, transcendentals=0),
-    )(my_y, lists, tiles, *mats, *src, *extra)
+    )(my_y, lists, tiles, *src, *extra)
 
 
 def pack(*operands):
@@ -279,7 +312,7 @@
         in_specs=[VMEM_SPEC] * 9,
         out_specs=[VMEM_SPEC] * 2,
         name="pack",
-        compiler_params=PARAMS,
+        compiler_params=pltpu.CompilerParams(vmem_limit_bytes=60 << 20),
         cost_estimate=pl.CostEstimate(flops=10**6, bytes_accessed=10**6, transcendentals=0),
     )(*operands)
 
@@ -303,11 +336,6 @@
     visible_lists,
     visible_counts,
 ):
-    mats = selection_matrices()
-    recv_mats = [jnp.asarray(r, BF16) for r, _ in mats]
-    src_mats = [jnp.asarray(s, BF16) for _, s in mats]
-    nul = jnp.asarray(null_spread(), BF16)
-
     mine, recv_tile = pack(
         incident,
         src_pos,
@@ -328,26 +356,33 @@
 
     me = (lax.axis_index("x") * NC + lax.axis_index("c")).astype(jnp.int32).reshape(1)
     my_y = (lax.axis_index("yh") * NYL + lax.axis_index("yl")).astype(jnp.int32).reshape(1)
-    far = [along_x(mine, d) for d in (1, 3, 2)]
-    near = [mine, other_core(mine)]
+    left, right = along_x(mine, 1), along_x(mine, 3)
+    own = other_core(mine)
 
     tiles = lax.all_to_all(recv_tile, ("yl", "yh", "z"), 0, 0, tiled=True)
 
-    near = src_prep(me, near, src_mats, nul)
-    begun = sweep(my_y, 0, tiles, recv_mats, near, NJ)
-    far = lax.optimization_barrier((*far, tiles, near[0]))
-    far = list(far[:3])
-    far = far + [other_core(block) for block in far]
-    src = src_prep(me, far, src_mats, nul)
-
-    def chunk(distance):
-        return sweep(my_y, distance, tiles, recv_mats, src, NZ, begun)
+    near = src_prep(me, [mine, own])
+    left, right, tiles, first = lax.optimization_barrier((left, right, tiles, near[0]))
+    near = [first, *near[1:]]
+    far = [along_x(left[:FIRST], 1), along_x(right[FIRST:], 3)]
+    sides = [left, right, other_core(left), other_core(right)]
+
+    begun = sweep(my_y, 0, tiles, near, NJ)
+    *far, begun = lax.optimization_barrier((*far, begun))
+    src = src_prep(me, sides, [far, [other_core(part) for part in far]])
 
     def along_y(block, distance):
         return lax.ppermute(block, ("yl", "yh"), y_route(distance))
 
-    arrived = [along_y(chunk(d), d) for d in (2, 1, 3)]
-    total = chunk(0) + arrived[0] + arrived[1] + arrived[2]
+    def part(distance, *passing):
+        return sweep(my_y, distance, tiles, src, NZ, begun, *passing)
+
+    across = part(2)
+    by_left, by_right = along_y(across[:HALF], 1), along_y(across[HALF:], 3)
+    ahead = part(1)
+    ahead = along_y(jnp.concatenate([ahead[:HALF] + by_left, ahead[HALF:]], axis=0), 1)
+    behind = along_y(part(3, by_right), 3)
+    total = part(0) + ahead + behind
     pieces = lax.all_to_all(total, "z", 0, 0, tiled=True)
     return direct + jnp.sum(pieces, axis=0)
 

time: 124 us -> 109 us (0.88)
  blocking collectives: 28.8 us -> 19.3 us
  local copies, waits for them, and re-layouts: 14.9 us -> 5.75 us
  starting transfers between devices: 25.7 us -> 30.1 us
  Pallas kernels: 38.8 us -> 36.7 us
  waiting for transfers between devices: 13.4 us -> 15.2 us
    unnamed x52 -> x12, local copies, waits for them, and re-layouts: 14.9 us -> 4.25 us
    all_to_all x1, blocking collectives: 28.8 us -> 19.3 us  [shards(): pieces = lax.all_to_all(total, 'z', 0, 0, tiled=True)]
    pallas_call x7, Pallas kernels: 38.1 us -> 34.8 us  [the longest x5 32.7 us: sweep(): pl.pallas_call(functools.partial(sweep_kernel, count, blocks, len(extra),...]
    ppermute x3 -> x4, waiting for transfers between devices: 3.26 us -> 0.01 us  [along_x(): lax.ppermute(block, 'x', [(i, (i + distance) % NX) for i in range(NX)])]
    ppermute x3 -> x4, starting transfers between devices: 8.97 us -> 11 us  [along_y(): return lax.ppermute(block, ('yl', 'yh'), y_route(distance))]
    all_to_all x1, waiting for transfers between devices: 5.8 us -> 7.73 us  [shards(): tiles = lax.all_to_all(recv_tile, ('yl', 'yh', 'z'), 0, 0, tiled=True)]
    ppermute x3 -> x4, starting transfers between devices: 4.64 us -> 6.47 us  [along_x(): lax.ppermute(block, 'x', [(i, (i + distance) % NX) for i in range(NX)])]
    ppermute x4 -> x5, waiting for transfers between devices: 0.01 us -> 1.71 us  [other_core(): return lax.ppermute(block, 'c', [(0, 1), (1, 0)])]
  transfers between devices with their start and end apart: 11 -> 14, of which waited for: 4 -> 4; matrix products, arithmetic and copies ran while one was open for 0% -> 1% of each run, Pallas kernels for 24% -> 24%
where the time goes in v4:
time: 109 us; the launch traced here: 108 us
  Pallas kernels  36.7 us (34%)
  starting transfers between devices  30.1 us (28%)
  blocking collectives  19.3 us (18%)
  waiting for transfers between devices  15.2 us (14%)
  local copies, waits for them, and re-layouts  5.75 us (5%)
    pallas_call x5, Pallas kernels, sweep(): pl.pallas_call(functools.partial(sweep_kernel, count, blocks, len(extra),...  32.7 us
    all_to_all x1, blocking collectives, shards(): pieces = lax.all_to_all(total, 'z', 0, 0, tiled=True)  19.3 us
    all_to_all x1, starting transfers between devices, shards(): tiles = lax.all_to_all(recv_tile, ('yl', 'yh', 'z'), 0, 0, tiled=True)  11.5 us
    ppermute x4, starting transfers between devices, along_y(): return lax.ppermute(block, ('yl', 'yh'), y_route(distance))  11 us
    all_to_all x1, waiting for transfers between devices, shards(): tiles = lax.all_to_all(recv_tile, ('yl', 'yh', 'z'), 0, 0, tiled=True)  7.73 us
    ppermute x4, starting transfers between devices, along_x(): lax.ppermute(block, 'x', [(i, (i + distance) % NX) for i in range(NX)])  6.47 us
    ppermute x4, waiting for transfers between devices, along_y(): return lax.ppermute(block, ('yl', 'yh'), y_route(distance))  5.72 us
    unnamed x12, local copies, waits for them, and re-layouts  4.25 us
  transfers between devices with their start and end apart: 14, of which 4 were waited for; matrix products, arithmetic and copies ran while one was open for 1% of the time, Pallas kernels for 24%

profile of v4, /device:TPU:6, one launch (start us, length us, event | category | flops | bytes accessed | tf_op | source)
XLA Modules:
  0.0 108.1 jit_solution(2852158323957302121)
XLA Ops:
  0.0 2.0 %pack.1 = (f32[1152,128]{1,0:T(8,128)}, f32[32,8,128]{2,1,0:T(8,128)}) custom-call(bf16[1024,128]{1,0:T(8,128)(2,1)} %incident.1, f32[3,1024]{1,0:T(4,128)} %pos.1, f32[2,1024]{1,0:T(2,128)} %angles.1, f32[1,1024]{1,0:T(1,128)} %bitcast.10, f32[1,1024]{1,0:T(1,128)} %bitcast.11, s32[16,4,16]{2,1,0:T(4,128)} %bitcast.8, s32[16,16]{1,0:T(8,128)} %bitcast.9, ...), custom_call_target="tpu_custom_call" | custom-call | flops 1000000 | bytes 1000000 | tf_op jit(solution)/shard_map/pack/pallas_call | solution.py:306
  2.0 0.8 collective-permute-start.1
  2.8 2.4 %collective-permute-start = (f32[1152,128]{1,0:T(8,128)}, f32[1152,128]{1,0:T(8,128)S(1)}, u32[]{:S(2)}, u32[]{:S(2)}) collective-permute-start(f32[1152,128]{1,0:T(8,128)} %get-tuple-element.24.refs_0_), channel_id=1, source_target_pairs={{0,64},{64,128},{128,192},{192,0},{1,65},{65,129},{129,193},{193,1... | collective-permute-start | bytes 1769480 | tf_op jit(solution)/shard_map/ppermute | solution.py:352
  5.2 11.5 %all-to-all-start = ((f32[32,8,128]{2,1,0:T(8,128)}), f32[32,8,128]{2,1,0:T(8,128)S(1)}, u32[]{:S(2)}, u32[]{:S(2)}) async-start(f32[32,8,128]{2,1,0:T(8,128)} %get-tuple-element.25), calls=%async_computation | async-start | bytes 262144 | tf_op jit(solution)/shard_map/all_to_all | solution.py:362
  16.8 1.1 copy-done
  17.8 0.4 src_prep.2
  18.2 0.7 copy-done.1
  18.9 0.7 copy-done.3
  19.5 7.7 %all-to-all-done.tiles = f32[32,8,128]{2,1,0:T(8,128)S(1)} async-done(((f32[32,8,128]{2,1,0:T(8,128)}), f32[32,8,128]{2,1,0:T(8,128)S(1)}, u32[]{:S(2)}, u32[]{:S(2)}) %all-to-all-start) | async-done | bytes 131104 | tf_op jit(solution)/shard_map/all_to_all | solution.py:362
  27.3 0.7 slice.19
  28.0 0.7 slice.18
  28.7 3.2 %collective-permute-start.5 = (f32[512,128]{1,0:T(8,128)}, f32[512,128]{1,0:T(8,128)}, u32[]{:S(2)}, u32[]{:S(2)}) collective-permute-start(f32[512,128]{1,0:T(8,128)} %slice.18), channel_id=1, source_target_pairs={{0,64},{64,128},{128,192},{192,0},{1,65},{65,129},{129,193},{193,1... | collective-permute-start | bytes 786440 | tf_op jit(solution)/shard_map/ppermute | solution.py:352
  32.0 0.5 collective-permute-start.4
  32.5 0.9 copy-done.2
  33.4 0.9 copy-done.4
  34.3 7.3 %sweep.5.refs_0_ = f32[32,128,128]{2,1,0:T(8,128)S(1)} custom-call(s32[1]{0:T(128)} %bitcast.my_y, s32[2,8,128]{2,1,0:T(8,128)S(1)} %get-tuple-element.29.lists, f32[32,8,128]{2,1,0:T(8,128)S(1)} %all-to-all-done.tiles, bf16[17,32,128]{2,1,0:T(8,128)(2,1)S(1)} %get-tuple-element.31.sf, bf16[17,32,128]{2,1,0:T(8,128)(2,1)S(1)} %copy-done.4, ...), custom_call_target="tpu_custom_call" | custom-call | flops 1000000 | bytes 1000000 | tf_op jit(solution)/shard_map/sweep/pallas_call | solution.py:287
  41.7 0.3 collective-permute-start.8
  42.0 0.3 collective-permute-start.7
  42.3 1.7 %collective-permute-done.7.refs_6_ = f32[512,128]{1,0:T(8,128)S(1)} collective-permute-done((f32[512,128]{1,0:T(8,128)}, f32[512,128]{1,0:T(8,128)S(1)}, u32[]{:S(2)}, u32[]{:S(2)}) %collective-permute-start.7) | collective-permute-done | bytes 262176 | tf_op jit(solution)/shard_map/ppermute | solution.py:355
  44.0 1.7 %src_prep.3 = (bf16[49,32,128]{2,1,0:T(8,128)(2,1)S(1)}, bf16[49,32,128]{2,1,0:T(8,128)(2,1)S(1)}, bf16[49,48,128]{2,1,0:T(8,128)(2,1)S(1)}, bf16[49,128,128]{2,1,0:T(8,128)(2,1)S(1)}, s32[6,8,128]{2,1,0:T(8,128)S(1)}) custom-call(s32[1]{0:T(128)} %bitcast.1.me, f32[1152,128]{1,0:T(8,128)S(1)} %collective-permute-done.refs_0_, ...), custom_call_target="tpu_custom_call" | custom-call | flops 1000000 | bytes 1000000 | tf_op jit(solution)/shard_map/src_prep/pallas_call | solution.py:267
  45.6 6.7 %sweep.8 = f32[8,128,128]{2,1,0:T(8,128)S(1)} custom-call(s32[1]{0:T(128)} %bitcast.my_y, s32[6,8,128]{2,1,0:T(8,128)S(1)} %get-tuple-element.37.lists, f32[32,8,128]{2,1,0:T(8,128)S(1)} %all-to-all-done.tiles, bf16[49,32,128]{2,1,0:T(8,128)(2,1)S(1)} %get-tuple-element.38.sf, bf16[49,32,128]{2,1,0:T(8,128)(2,1)S(1)} %get-tuple-element.39.ss, ...), custom_call_target="tpu_custom_call" | custom-call | flops 1000000 | bytes 1000000 | tf_op jit(solution)/shard_map/sweep/pallas_call | solution.py:287
  52.4 4.9 %collective-permute-start.9 = (f32[4,128,128]{2,1,0:T(8,128)S(1)}, f32[4,128,128]{2,1,0:T(8,128)S(1)}, u32[]{:S(2)}, u32[]{:S(2)}) collective-permute-start(f32[4,128,128]{2,1,0:T(8,128)S(1)} %get-tuple-element.45), channel_id=1, source_target_pairs={{0,32},{32,8},{8,40},{40,0},{1,33},{33,9},{9,41},{41,1},{2,34},{34... | collective-permute-start | bytes 786440 | tf_op jit(solution)/shard_map/ppermute | solution.py:375
  57.2 1.2 %collective-permute-start.11 = (f32[4,128,128]{2,1,0:T(8,128)S(1)}, f32[4,128,128]{2,1,0:T(8,128)S(1)}, u32[]{:S(2)}, u32[]{:S(2)}) collective-permute-start(f32[4,128,128]{2,1,0:T(8,128)S(1)} %get-tuple-element.46), channel_id=1, source_target_pairs={{0,40},{32,0},{8,32},{40,8},{1,41},{33,1},{9,33},{41,9},{2,42},{34... | collective-permute-start | bytes 786440 | tf_op jit(solution)/shard_map/ppermute | solution.py:375
  58.5 6.5 %sweep.7 = f32[8,128,128]{2,1,0:T(8,128)S(1)} custom-call(s32[1]{0:T(128)} %bitcast.my_y, s32[6,8,128]{2,1,0:T(8,128)S(1)} %get-tuple-element.37.lists, f32[32,8,128]{2,1,0:T(8,128)S(1)} %all-to-all-done.tiles, bf16[49,32,128]{2,1,0:T(8,128)(2,1)S(1)} %get-tuple-element.38.sf, bf16[49,32,128]{2,1,0:T(8,128)(2,1)S(1)} %get-tuple-element.39.ss, ...), custom_call_target="tpu_custom_call" | custom-call | flops 1000000 | bytes 1000000 | tf_op jit(solution)/shard_map/sweep/pallas_call | solution.py:287
  64.9 0.3 collective-permute-done.9
  65.4 0.6 collective-permute-start.10
  66.0 6.5 %sweep.9 = f32[8,128,128]{2,1,0:T(8,128)S(1)} custom-call(s32[1]{0:T(128)} %bitcast.my_y, s32[6,8,128]{2,1,0:T(8,128)S(1)} %get-tuple-element.37.lists, f32[32,8,128]{2,1,0:T(8,128)S(1)} %all-to-all-done.tiles, bf16[49,32,128]{2,1,0:T(8,128)(2,1)S(1)} %get-tuple-element.38.sf, bf16[49,32,128]{2,1,0:T(8,128)(2,1)S(1)} %get-tuple-element.39.ss, ...), custom_call_target="tpu_custom_call" | custom-call | flops 1000000 | bytes 1000000 | tf_op jit(solution)/shard_map/sweep/pallas_call | solution.py:287
  72.4 4.3 %collective-permute-start.12 = (f32[8,128,128]{2,1,0:T(8,128)S(1)}, f32[8,128,128]{2,1,0:T(8,128)S(1)}, u32[]{:S(2)}, u32[]{:S(2)}) collective-permute-start(f32[8,128,128]{2,1,0:T(8,128)S(1)} %sweep.9), channel_id=1, source_target_pairs={{0,40},{32,0},{8,32},{40,8},{1,41},{33,1},{9,33},{41,9},{2,42},{34... | collective-permute-start | bytes 1572872 | tf_op jit(solution)/shard_map/ppermute | solution.py:375
  76.8 5.8 %sweep.6 = f32[8,128,128]{2,1,0:T(8,128)S(1)} custom-call(s32[1]{0:T(128)} %bitcast.my_y, s32[6,8,128]{2,1,0:T(8,128)S(1)} %get-tuple-element.37.lists, f32[32,8,128]{2,1,0:T(8,128)S(1)} %all-to-all-done.tiles, bf16[49,32,128]{2,1,0:T(8,128)(2,1)S(1)} %get-tuple-element.38.sf, bf16[49,32,128]{2,1,0:T(8,128)(2,1)S(1)} %get-tuple-element.39.ss, ...), custom_call_target="tpu_custom_call" | custom-call | flops 1000000 | bytes 1000000 | tf_op jit(solution)/shard_map/sweep/pallas_call | solution.py:287
  82.6 5.4 %collective-permute-done.12 = f32[8,128,128]{2,1,0:T(8,128)S(1)} collective-permute-done((f32[8,128,128]{2,1,0:T(8,128)S(1)}, f32[8,128,128]{2,1,0:T(8,128)S(1)}, u32[]{:S(2)}, u32[]{:S(2)}) %collective-permute-start.12) | collective-permute-done | bytes 524320 | tf_op jit(solution)/shard_map/ppermute | solution.py:375
  88.1 19.3 %all_to_all.10 = f32[8,128,128]{2,1,0:T(8,128)S(1)} all-to-all(f32[8,128,128]{2,1,0:T(8,128)S(1)} %add_add_fusion), channel_id=1, replica_groups=mesh['x'=4,'yl'=2,'c'=2,'yh'=2,'z'=8] {'z'}, dimensions={0} | all-to-all | bytes 1048576 | tf_op jit(solution)/shard_map/all_to_all | solution.py:386
  107.5 0.6 add.23
  (25 shorter events, 0.3 us)
Async XLA Ops:
  2.0 14.7 %collective-permute-start.2 = (f32[1152,128]{1,0:T(8,128)}, f32[1152,128]{1,0:T(8,128)S(1)}, u32[]{:S(2)}, u32[]{:S(2)}) collective-permute-start(f32[1152,128]{1,0:T(8,128)} %get-tuple-element.24.refs_0_), channel_id=1, source_target_pairs={{0,16},{16,0},{1,17},{17,1},{2,18},{18,2},{3,19},{19,3},{4,20},{20... | collective-permute-start | bytes 1769480 | tf_op jit(solution)/shard_map/ppermute | solution.py:355
  2.0 25.3 %collective-permute-start.1 = (f32[1152,128]{1,0:T(8,128)}, f32[1152,128]{1,0:T(8,128)S(1)}, u32[]{:S(2)}, u32[]{:S(2)}) collective-permute-start(f32[1152,128]{1,0:T(8,128)} %get-tuple-element.24.refs_0_), channel_id=1, source_target_pairs={{0,192},{64,0},{128,64},{192,128},{1,193},{65,1},{129,65},{193,129... | collective-permute-start | bytes 1769480 | tf_op jit(solution)/shard_map/ppermute | solution.py:352
  2.8 24.4 %collective-permute-start = (f32[1152,128]{1,0:T(8,128)}, f32[1152,128]{1,0:T(8,128)S(1)}, u32[]{:S(2)}, u32[]{:S(2)}) collective-permute-start(f32[1152,128]{1,0:T(8,128)} %get-tuple-element.24.refs_0_), channel_id=1, source_target_pairs={{0,64},{64,128},{128,192},{192,0},{1,65},{65,129},{129,193},{193,1... | collective-permute-start | bytes 1769480 | tf_op jit(solution)/shard_map/ppermute | solution.py:352
  5.2 22.0 %all-to-all-start = ((f32[32,8,128]{2,1,0:T(8,128)}), f32[32,8,128]{2,1,0:T(8,128)S(1)}, u32[]{:S(2)}, u32[]{:S(2)}) async-start(f32[32,8,128]{2,1,0:T(8,128)} %get-tuple-element.25), calls=%async_computation | async-start | bytes 262144 | tf_op jit(solution)/shard_map/all_to_all | solution.py:362
  16.7 1.1 copy-start
  18.2 0.7 copy-start.1
  18.9 0.7 copy-start.3
  28.0 13.7 %collective-permute-start.6 = (f32[640,128]{1,0:T(8,128)}, f32[640,128]{1,0:T(8,128)S(1)}, u32[]{:S(2)}, u32[]{:S(2)}) collective-permute-start(f32[640,128]{1,0:T(8,128)} %slice.19), channel_id=1, source_target_pairs={{0,192},{64,0},{128,64},{192,128},{1,193},{65,1},{129,65},{193,129... | collective-permute-start | bytes 983048 | tf_op jit(solution)/shard_map/ppermute | solution.py:352
  28.7 12.9 %collective-permute-start.5 = (f32[512,128]{1,0:T(8,128)}, f32[512,128]{1,0:T(8,128)}, u32[]{:S(2)}, u32[]{:S(2)}) collective-permute-start(f32[512,128]{1,0:T(8,128)} %slice.18), channel_id=1, source_target_pairs={{0,64},{64,128},{128,192},{192,0},{1,65},{65,129},{129,193},{193,1... | collective-permute-start | bytes 786440 | tf_op jit(solution)/shard_map/ppermute | solution.py:352
  32.0 10.3 %collective-permute-start.3 = (f32[1152,128]{1,0:T(8,128)S(1)}, f32[1152,128]{1,0:T(8,128)S(1)}, u32[]{:S(2)}, u32[]{:S(2)}) collective-permute-start(f32[1152,128]{1,0:T(8,128)S(1)} %collective-permute-done.refs_0_), channel_id=1, source_target_pairs={{0,16},{16,0},{1,17},{17,1},{2,18},{18,2},{3,19},{19,3},{4,20},{20... | collective-permute-start | bytes 1769480 | tf_op jit(solution)/shard_map/ppermute | solution.py:355
  32.0 10.3 %collective-permute-start.4 = (f32[1152,128]{1,0:T(8,128)S(1)}, f32[1152,128]{1,0:T(8,128)S(1)}, u32[]{:S(2)}, u32[]{:S(2)}) collective-permute-start(f32[1152,128]{1,0:T(8,128)S(1)} %collective-permute-done.1.refs_1_), channel_id=1, source_target_pairs={{0,16},{16,0},{1,17},{17,1},{2,18},{18,2},{3,19},{19,3},{4,20},{20... | collective-permute-start | bytes 1769480 | tf_op jit(solution)/shard_map/ppermute | solution.py:355
  32.5 0.9 copy-start.2
  33.4 0.9 copy-start.4
  41.7 2.3 %collective-permute-start.8 = (f32[640,128]{1,0:T(8,128)S(1)}, f32[640,128]{1,0:T(8,128)S(1)}, u32[]{:S(2)}, u32[]{:S(2)}) collective-permute-start(f32[640,128]{1,0:T(8,128)S(1)} %collective-permute-done.6.refs_5_), channel_id=1, source_target_pairs={{0,16},{16,0},{1,17},{17,1},{2,18},{18,2},{3,19},{19,3},{4,20},{20... | collective-permute-start | bytes 983048 | tf_op jit(solution)/shard_map/ppermute | solution.py:355
  42.0 2.0 %collective-permute-start.7 = (f32[512,128]{1,0:T(8,128)}, f32[512,128]{1,0:T(8,128)S(1)}, u32[]{:S(2)}, u32[]{:S(2)}) collective-permute-start(f32[512,128]{1,0:T(8,128)} %collective-permute-done.5.refs_4_), channel_id=1, source_target_pairs={{0,16},{16,0},{1,17},{17,1},{2,18},{18,2},{3,19},{19,3},{4,20},{20... | collective-permute-start | bytes 786440 | tf_op jit(solution)/shard_map/ppermute | solution.py:355
  52.4 12.9 %collective-permute-start.9 = (f32[4,128,128]{2,1,0:T(8,128)S(1)}, f32[4,128,128]{2,1,0:T(8,128)S(1)}, u32[]{:S(2)}, u32[]{:S(2)}) collective-permute-start(f32[4,128,128]{2,1,0:T(8,128)S(1)} %get-tuple-element.45), channel_id=1, source_target_pairs={{0,32},{32,8},{8,40},{40,0},{1,33},{33,9},{9,41},{41,1},{2,34},{34... | collective-permute-start | bytes 786440 | tf_op jit(solution)/shard_map/ppermute | solution.py:375
  57.2 8.7 %collective-permute-start.11 = (f32[4,128,128]{2,1,0:T(8,128)S(1)}, f32[4,128,128]{2,1,0:T(8,128)S(1)}, u32[]{:S(2)}, u32[]{:S(2)}) collective-permute-start(f32[4,128,128]{2,1,0:T(8,128)S(1)} %get-tuple-element.46), channel_id=1, source_target_pairs={{0,40},{32,0},{8,32},{40,8},{1,41},{33,1},{9,33},{41,9},{2,42},{34... | collective-permute-start | bytes 786440 | tf_op jit(solution)/shard_map/ppermute | solution.py:375
  65.4 17.2 %collective-permute-start.10 = (f32[8,128,128]{2,1,0:T(8,128)S(1)}, f32[8,128,128]{2,1,0:T(8,128)S(1)}, u32[]{:S(2)}, u32[]{:S(2)}) collective-permute-start(f32[8,128,128]{2,1,0:T(8,128)S(1)} %pad_maximum_fusion), channel_id=1, source_target_pairs={{0,32},{32,8},{8,40},{40,0},{1,33},{33,9},{9,41},{41,1},{2,34},{34... | collective-permute-start | bytes 1572872 | tf_op jit(solution)/shard_map/ppermute | solution.py:375
  72.4 15.5 %collective-permute-start.12 = (f32[8,128,128]{2,1,0:T(8,128)S(1)}, f32[8,128,128]{2,1,0:T(8,128)S(1)}, u32[]{:S(2)}, u32[]{:S(2)}) collective-permute-start(f32[8,128,128]{2,1,0:T(8,128)S(1)} %sweep.9), channel_id=1, source_target_pairs={{0,40},{32,0},{8,32},{40,8},{1,41},{33,1},{9,33},{41,9},{2,42},{34... | collective-permute-start | bytes 1572872 | tf_op jit(solution)/shard_map/ppermute | solution.py:375
  82.6 24.9 %copy-start.5 = (f32[128,128]{1,0:T(8,128)S(1)}, f32[128,128]{1,0:T(8,128)}, u32[]{:S(2)}) copy-start(f32[128,128]{1,0:T(8,128)} %param.17) | copy-start | bytes 196612

commit v5 on v4

--- a/solution.py
+++ b/solution.py
@@ -22,7 +22,7 @@
 ROWS, DOT, SQA, SQB, ONE = 16, 8, 9, 10, 11
 KF, KS, KD = 32, 32, 48
 VMEM_LIMIT = 16 << 20
-UNROLL, TAIL = 16, 4
+UNROLL, TAIL = 16, 8
 HALF = NZ // 2
 FIRST = 4 * BS
 
@@ -111,10 +111,11 @@
 
 
 def pack_kernel(
-    incident, pos, angles, area, keep, lists, counts, recv_pos, recv_angles, packed, recv_tile
+    incident, pos, angles, area, keep, lists, counts, recv_pos, recv_angles, first, second, recv_tile
 ):
-    packed[: SB * BS, :] = incident[...].astype(jnp.float32)
-    packed[SB * BS :, :] = jnp.zeros((SB * TILE, BS), jnp.float32)
+    first[...] = incident[:FIRST, :].astype(jnp.float32)
+    second[: SB * BS - FIRST, :] = incident[FIRST:, :].astype(jnp.float32)
+    second[SB * BS - FIRST :, :] = jnp.zeros((SB * TILE, BS), jnp.float32)
     scale = keep[...] * area[...] * (1.0 / np.pi)
     rows = [pos[a : a + 1, :] - CENTRE for a in range(3)]
     rows += [component * scale for component in direction(angles[...])]
@@ -122,13 +123,13 @@
     tile = jnp.concatenate(rows, axis=0)
     slot = lax.broadcasted_iota(jnp.int32, (CAP, NYH * NZ), 0)
     for k in range(SB):
-        at = SB * BS + k * TILE
-        packed[at : at + 8, :] = tile[:, k * BS : (k + 1) * BS]
+        at = SB * BS - FIRST + k * TILE
+        second[at : at + 8, :] = tile[:, k * BS : (k + 1) * BS]
         for yl in range(NYL):
             slab = ((k // NC) * NYL + yl) * NC + k % NC
             live = slot < counts[slab : slab + 1, :]
             marked = jnp.where(live, lists[slab], -1).astype(jnp.float32)
-            packed[at + 8 + yl * CAP : at + 8 + (yl + 1) * CAP, : NYH * NZ] = marked
+            second[at + 8 + yl * CAP : at + 8 + (yl + 1) * CAP, : NYH * NZ] = marked
     rows = [recv_pos[a : a + 1, :] - CENTRE for a in range(3)]
     rows += direction(recv_angles[...])
     rows += [jnp.zeros((2, BS), jnp.float32)]
@@ -137,31 +138,18 @@
         recv_tile[j] = tile
 
 
-def src_prep_kernel(count, cut, me, *refs):
-    inputs = count + cut
-    sf, ss, sd, em, lists = refs[inputs:]
+def prepare(me, parts, sf, ss, sd, em, lists):
     mats = selections(1)
-
-    def rows_of(d):
-        if d < count - cut:
-            return lambda start, size: refs[d][pl.ds(start, size), :]
-        first, second = refs[count - cut + 2 * (d - count + cut) :][:2]
-
-        def rows(start, size):
-            if isinstance(start, int) and start < FIRST:
-                return first[pl.ds(start, size), :]
-            return second[pl.ds(start - FIRST, size), :]
-
-        return rows
-
-    for d in range(count):
-        rows = rows_of(d)
+    count = len(parts)
+    for d, (first, second) in enumerate(parts):
         for k in range(SB):
-            em[d * SB + k] = rows(k * BS, BS).astype(jnp.bfloat16)
-        tiles = [rows(SB * BS + k * TILE, 8) for k in range(SB)]
+            ref, start = (first, k * BS) if k * BS < FIRST else (second, k * BS - FIRST)
+            em[d * SB + k] = ref[start : start + BS, :].astype(jnp.bfloat16)
+        at = SB * BS - FIRST
+        tiles = [second[at + k * TILE : at + k * TILE + 8, :] for k in range(SB)]
         q = split_pieces(jnp.concatenate(tiles, axis=1))
-        list_at = pl.multiple_of(SB * BS + me[0] * TILE + 8, 8)
-        lists[d] = rows(list_at, 8).astype(jnp.int32)
+        list_at = pl.multiple_of(at + me[0] * TILE + 8, 8)
+        lists[d] = second[pl.ds(list_at, 8), :].astype(jnp.int32)
         for m, out in zip(mats, (sf, ss, sd)):
             values = dot(m, q).astype(jnp.bfloat16)
             for k in range(SB):
@@ -174,31 +162,41 @@
     sd[null] = jnp.where(first_row, 1.0, 0.0).astype(jnp.bfloat16)
 
 
-def sweep_kernel(count, blocks, added, distance, my_y, lists, tiles, sf, ss, sd, em, *refs):
-    if added == 2:
-        before, passing, out, rf, rs, rd, ids, owner = refs
-    elif added:
-        before, out, rf, rs, rd, ids, owner = refs
-    else:
-        out, rf, rs, rd, ids, owner = refs
-    target = (my_y[0] + distance) & (NY - 1)
-    base = ((target & (NYL - 1)) * NYH + (target >> 1)) * NZ if blocks == NZ else 0
-    null = count * SB
-    slots = count * CAP // 2
-
+def src_prep_kernel(count, me, *refs):
+    prepare(me, list(zip(refs[: 2 * count : 2], refs[1 : 2 * count : 2])), *refs[2 * count :])
+
+
+def recv_prep_kernel(tiles, rf, rs, rd):
     mats = selections(0)
-    for j in range(blocks):
-        q = split_pieces(tiles[base + j])
+    for j in range(NJ):
+        q = split_pieces(tiles[j])
         for m, ref in zip(mats, (rf, rs, rd)):
             ref[j] = lax.dot_general(
                 q, m, (((0,), (1,)), ((), ())), preferred_element_type=jnp.float32
             ).astype(jnp.bfloat16)
-        start = before[base + j] if added else jnp.zeros((BS, BS), jnp.float32)
-        out[j] = start + passing[j - HALF] if added == 2 and j >= HALF else start
+
+
+def sweep_kernel(count, blocks, added, distance, my_y, lists, rf, rs, rd, sf, ss, sd, em, *refs):
+    *before, out, ids, owner = refs
+    null = sf.shape[0] - 1
+    slots = count * CAP // 2
+
+    def block_of(j):
+        target = (my_y[0] + distance + (j >> 3)) & (NY - 1)
+        return ((target & (NYL - 1)) * NYH + (target >> 1)) * NZ + (j & (NZ - 1))
+
+    for j in range(blocks):
+        start = jnp.zeros((BS, BS), jnp.float32)
+        if added:
+            start = before[0][(distance - 1) * NZ + j]
+        if added == 2 and j >= HALF:
+            start = start + before[1][j - HALF]
+        out[j] = start
 
     def one_block(j, n):
-        row = (((base + j) >> 4)) * CAP
-        lane = (base + j) & (NYH * NZ - 1)
+        block = block_of(j)
+        row = (block >> 4) * CAP
+        lane = block & (NYH * NZ - 1)
         for t in range(slots):
             owner[n // 2 + t] = j
         for d in range(count):
@@ -219,7 +217,7 @@
 
     def front(u):
         a, b = ids[2 * u], ids[2 * u + 1]
-        j = owner[u]
+        j = block_of(owner[u])
 
         def pair(ref):
             return jnp.concatenate([ref[a], ref[b]], axis=1)
@@ -260,12 +258,11 @@
     return jax.ShapeDtypeStruct(shape, BF16)
 
 
-def src_prep(me, whole, parts=()):
-    packed = whole + [part for pair in parts for part in pair]
-    count = len(whole) + len(parts)
+def src_prep(me, parts):
+    count = len(parts)
     rows = count * SB + 1
     return pl.pallas_call(
-        functools.partial(src_prep_kernel, count, len(parts)),
+        functools.partial(src_prep_kernel, count),
         out_shape=[
             bf16_shape(rows, KF, BS),
             bf16_shape(rows, KS, BS),
@@ -273,44 +270,53 @@
             bf16_shape(rows, BS, BS),
             jax.ShapeDtypeStruct((count, 8, BS), jnp.int32),
         ],
-        in_specs=[SMEM_SPEC] + [VMEM_SPEC] * len(packed),
+        in_specs=[SMEM_SPEC] + [VMEM_SPEC] * (2 * count),
         out_specs=[VMEM_SPEC] * 5,
         name="src_prep",
         compiler_params=PARAMS,
         cost_estimate=pl.CostEstimate(flops=10**6, bytes_accessed=10**6, transcendentals=0),
-    )(me, *packed)
-
-
-def sweep(my_y, distance, tiles, src, blocks, *extra):
+    )(me, *[part for pair in parts for part in pair])
+
+
+def recv_prep(tiles):
+    return pl.pallas_call(
+        recv_prep_kernel,
+        out_shape=[bf16_shape(NJ, BS, KF), bf16_shape(NJ, BS, KS), bf16_shape(NJ, BS, KD)],
+        in_specs=[VMEM_SPEC],
+        out_specs=[VMEM_SPEC] * 3,
+        name="recv_prep",
+        compiler_params=PARAMS,
+        cost_estimate=pl.CostEstimate(flops=10**6, bytes_accessed=10**6, transcendentals=0),
+    )(tiles)
+
+
+def sweep(my_y, distance, recv, src, count, blocks, *before):
     *src, lists = src
-    count = lists.shape[0]
     return pl.pallas_call(
-        functools.partial(sweep_kernel, count, blocks, len(extra), distance),
+        functools.partial(sweep_kernel, count, blocks, len(before), distance),
         out_shape=jax.ShapeDtypeStruct((blocks, BS, BS), jnp.float32),
-        in_specs=[SMEM_SPEC] * 2 + [VMEM_SPEC] * (5 + len(extra)),
+        in_specs=[SMEM_SPEC] * 2 + [VMEM_SPEC] * (7 + len(before)),
         out_specs=VMEM_SPEC,
         scratch_shapes=[
-            pltpu.VMEM((blocks, BS, KF), BF16),
-            pltpu.VMEM((blocks, BS, KS), BF16),
-            pltpu.VMEM((blocks, BS, KD), BF16),
             pltpu.SMEM((blocks * count * CAP + 4 * UNROLL,), jnp.int32),
             pltpu.SMEM((blocks * count * CAP // 2 + count * CAP + 2 * UNROLL,), jnp.int32),
         ],
         name="sweep",
         compiler_params=PARAMS,
         cost_estimate=pl.CostEstimate(flops=10**6, bytes_accessed=10**6, transcendentals=0),
-    )(my_y, lists, tiles, *src, *extra)
+    )(my_y, lists, *recv, *src, *before)
 
 
 def pack(*operands):
     return pl.pallas_call(
         pack_kernel,
         out_shape=[
-            jax.ShapeDtypeStruct((SB * (BS + TILE), BS), jnp.float32),
+            jax.ShapeDtypeStruct((FIRST, BS), jnp.float32),
+            jax.ShapeDtypeStruct((SB * (BS + TILE) - FIRST, BS), jnp.float32),
             jax.ShapeDtypeStruct((NJ, 8, BS), jnp.float32),
         ],
         in_specs=[VMEM_SPEC] * 9,
-        out_specs=[VMEM_SPEC] * 2,
+        out_specs=[VMEM_SPEC] * 3,
         name="pack",
         compiler_params=pltpu.CompilerParams(vmem_limit_bytes=60 << 20),
         cost_estimate=pl.CostEstimate(flops=10**6, bytes_accessed=10**6, transcendentals=0),
@@ -336,7 +342,7 @@
     visible_lists,
     visible_counts,
 ):
-    mine, recv_tile = pack(
+    *mine, recv_tile = pack(
         incident,
         src_pos,
         src_angles,
@@ -356,33 +362,36 @@
 
     me = (lax.axis_index("x") * NC + lax.axis_index("c")).astype(jnp.int32).reshape(1)
     my_y = (lax.axis_index("yh") * NYL + lax.axis_index("yl")).astype(jnp.int32).reshape(1)
-    left, right = along_x(mine, 1), along_x(mine, 3)
-    own = other_core(mine)
+    left = [along_x(mine[0], 1), None]
+    right = [None, along_x(mine[1], 3)]
+    left[1], right[0] = along_x(mine[1], 1), along_x(mine[0], 3)
+    own = [other_core(part) for part in mine]
 
     tiles = lax.all_to_all(recv_tile, ("yl", "yh", "z"), 0, 0, tiled=True)
 
-    near = src_prep(me, [mine, own])
-    left, right, tiles, first = lax.optimization_barrier((left, right, tiles, near[0]))
-    near = [first, *near[1:]]
-    far = [along_x(left[:FIRST], 1), along_x(right[FIRST:], 3)]
-    sides = [left, right, other_core(left), other_core(right)]
-
-    begun = sweep(my_y, 0, tiles, near, NJ)
+    *left, right[0], right[1], own[0], own[1], tiles = lax.optimization_barrier(
+        (*left, *right, *own, tiles)
+    )
+    far = [along_x(left[0], 1), along_x(right[1], 3)]
+    sides = [left, right] + [[other_core(part) for part in pair] for pair in (left, right)]
+
+    recv = recv_prep(tiles)
+    begun = sweep(my_y, 1, recv, src_prep(me, [mine, own]), 2, 3 * NZ)
     *far, begun = lax.optimization_barrier((*far, begun))
-    src = src_prep(me, sides, [far, [other_core(part) for part in far]])
+    src = src_prep(me, sides + [far, [other_core(part) for part in far]] + [mine, own])
 
     def along_y(block, distance):
         return lax.ppermute(block, ("yl", "yh"), y_route(distance))
 
     def part(distance, *passing):
-        return sweep(my_y, distance, tiles, src, NZ, begun, *passing)
+        return sweep(my_y, distance, recv, src, GROUP - 2, NZ, begun, *passing)
 
     across = part(2)
     by_left, by_right = along_y(across[:HALF], 1), along_y(across[HALF:], 3)
     ahead = part(1)
     ahead = along_y(jnp.concatenate([ahead[:HALF] + by_left, ahead[HALF:]], axis=0), 1)
     behind = along_y(part(3, by_right), 3)
-    total = part(0) + ahead + behind
+    total = sweep(my_y, 0, recv, src, GROUP, NZ) + ahead + behind
     pieces = lax.all_to_all(total, "z", 0, 0, tiled=True)
     return direct + jnp.sum(pieces, axis=0)
 

time: 109 us -> 108 us (level)
  blocking collectives: 19.3 us -> 42 us
  starting transfers between devices: 30.1 us -> 17.9 us
  waiting for transfers between devices: 15.2 us -> 4.18 us
  Pallas kernels: 36.7 us -> 40.6 us
  local copies, waits for them, and re-layouts: 5.75 us -> 1.96 us
    all_to_all x0 -> x1, blocking collectives: none -> 22 us  [shards(): tiles = lax.all_to_all(recv_tile, ('yl', 'yh', 'z'), 0, 0, tiled=True)]
    all_to_all x1 -> x0, starting transfers between devices: 11.5 us -> none  [shards(): tiles = lax.all_to_all(recv_tile, ('yl', 'yh', 'z'), 0, 0, tiled=True)]
    all_to_all x1 -> x0, waiting for transfers between devices: 7.73 us -> none  [shards(): tiles = lax.all_to_all(recv_tile, ('yl', 'yh', 'z'), 0, 0, tiled=True)]
    ppermute x4, starting transfers between devices: 11 us -> 5.97 us  [along_y(): return lax.ppermute(block, ('yl', 'yh'), y_route(distance))]
    pallas_call x8 -> x9, Pallas kernels: 36.7 us -> 40.6 us  [the longest x5 36.3 us: sweep(): pl.pallas_call(functools.partial(sweep_kernel, count, blocks, len(before)...]
    ppermute x4 -> x6, starting transfers between devices: 6.47 us -> 9.78 us  [along_x(): lax.ppermute(block, 'x', [(i, (i + distance) % NX) for i in range(NX)])]
    ppermute x4, waiting for transfers between devices: 5.72 us -> 2.66 us  [along_y(): return lax.ppermute(block, ('yl', 'yh'), y_route(distance))]
    unnamed x12 -> x6, local copies, waits for them, and re-layouts: 4.25 us -> 1.92 us
  transfers between devices with their start and end apart: 14 -> 18, of which waited for: 4 -> 3; matrix products, arithmetic and copies ran while one was open for 1% -> 0% of each run, Pallas kernels for 24% -> 29%
where the time goes in v5:
time: 108 us
  blocking collectives  42 us (39%)
  Pallas kernels  40.6 us (38%)
  starting transfers between devices  17.9 us (17%)
  waiting for transfers between devices  4.18 us (4%)
  local copies, waits for them, and re-layouts  1.96 us (2%)
    pallas_call x5, Pallas kernels, sweep(): pl.pallas_call(functools.partial(sweep_kernel, count, blocks, len(before)...  36.3 us
    all_to_all x1, blocking collectives, shards(): tiles = lax.all_to_all(recv_tile, ('yl', 'yh', 'z'), 0, 0, tiled=True)  22 us
    all_to_all x1, blocking collectives, shards(): pieces = lax.all_to_all(total, 'z', 0, 0, tiled=True)  20.1 us
    ppermute x6, starting transfers between devices, along_x(): lax.ppermute(block, 'x', [(i, (i + distance) % NX) for i in range(NX)])  9.78 us
    ppermute x4, starting transfers between devices, along_y(): return lax.ppermute(block, ('yl', 'yh'), y_route(distance))  5.97 us
    ppermute x4, waiting for transfers between devices, along_y(): return lax.ppermute(block, ('yl', 'yh'), y_route(distance))  2.66 us
  transfers between devices with their start and end apart: 18, of which 3 were waited for; matrix products, arithmetic and copies ran while one was open for 0% of the time, Pallas kernels for 29%

profile of v5, /device:TPU:6, one launch (start us, length us, event | category | flops | bytes accessed | tf_op | source)
XLA Modules:
  0.0 107.7 jit_solution(1986370221034917443)
XLA Ops:
  0.0 2.0 %pack.1 = (f32[512,128]{1,0:T(8,128)}, f32[640,128]{1,0:T(8,128)}, f32[32,8,128]{2,1,0:T(8,128)}) custom-call(bf16[1024,128]{1,0:T(8,128)(2,1)} %incident.1, f32[3,1024]{1,0:T(4,128)} %pos.1, f32[2,1024]{1,0:T(2,128)} %angles.1, f32[1,1024]{1,0:T(1,128)} %bitcast.10, f32[1,1024]{1,0:T(1,128)} %bitcast.11, s32[16,4,16]{2,1,0:T(4,128)} %bitcast.8, ...), custom_call_target="tpu_custom_call" | custom-call | flops 1000000 | bytes 1000000 | tf_op jit(solution)/shard_map/pack/pallas_call | solution.py:311
  2.0 0.5 collective-permute-start.5
  2.5 0.8 collective-permute-start.3
  3.3 2.4 %collective-permute-start.1 = (f32[640,128]{1,0:T(8,128)}, f32[640,128]{1,0:T(8,128)S(1)}, u32[]{:S(2)}, u32[]{:S(2)}) collective-permute-start(f32[640,128]{1,0:T(8,128)} %get-tuple-element.32.refs_1_.refs_13_), channel_id=1, source_target_pairs={{0,64},{64,128},{128,192},{192,0},{1,65},{65,129},{129,193},{193,1... | collective-permute-start | bytes 983048 | tf_op jit(solution)/shard_map/ppermute | solution.py:358
  5.7 3.2 %collective-permute-start = (f32[512,128]{1,0:T(8,128)}, f32[512,128]{1,0:T(8,128)S(1)}, u32[]{:S(2)}, u32[]{:S(2)}) collective-permute-start(f32[512,128]{1,0:T(8,128)} %get-tuple-element.31.refs_0_.refs_12_), channel_id=1, source_target_pairs={{0,64},{64,128},{128,192},{192,0},{1,65},{65,129},{129,193},{193,1... | collective-permute-start | bytes 786440 | tf_op jit(solution)/shard_map/ppermute | solution.py:358
  9.0 22.0 %all_to_all.10.tiles = f32[32,8,128]{2,1,0:T(8,128)S(1)} all-to-all(f32[32,8,128]{2,1,0:T(8,128)} %get-tuple-element.33), channel_id=1, replica_groups=mesh['x'=4,'yl'=2,'c'=2,'yh'=2,'z'=8] {'yl','yh','z'}, dimensions={0} | all-to-all | bytes 262144 | tf_op jit(solution)/shard_map/all_to_all | solution.py:370
  31.0 0.1 collective-permute-start.11
  31.1 3.2 %collective-permute-start.10 = (f32[512,128]{1,0:T(8,128)S(1)}, f32[512,128]{1,0:T(8,128)S(1)}, u32[]{:S(2)}, u32[]{:S(2)}) collective-permute-start(f32[512,128]{1,0:T(8,128)S(1)} %collective-permute-done.refs_0_), channel_id=1, source_target_pairs={{0,64},{64,128},{128,192},{192,0},{1,65},{65,129},{129,193},{193,1... | collective-permute-start | bytes 786440 | tf_op jit(solution)/shard_map/ppermute | solution.py:358
  34.3 0.5 collective-permute-start.9
  34.8 1.1 recv_prep.1
  35.9 1.0 copy-done
  36.9 0.9 copy-done.1
  37.8 0.4 src_prep.2
  38.2 7.0 %sweep.5.refs_0_ = f32[24,128,128]{2,1,0:T(8,128)S(1)} custom-call(s32[1]{0:T(128)} %bitcast.my_y, s32[2,8,128]{2,1,0:T(8,128)S(1)} %get-tuple-element.40.lists, bf16[32,128,32]{2,1,0:T(8,128)(2,1)S(1)} %get-tuple-element.42.rf, bf16[32,128,32]{2,1,0:T(8,128)(2,1)S(1)} %get-tuple-element.43.rs, bf16[32,128,48]{2,1,0:T(8,128)(2,1)S(1)} %get-tuple-element.44.rd, ...), custom_call_target="tpu_custom_call" | custom-call | flops 1000000 | bytes 1000000 | tf_op jit(solution)/shard_map/sweep/pallas_call | solution.py:295
  45.2 0.6 collective-permute-start.13
  45.8 0.3 collective-permute-start.6
  46.1 0.2 collective-permute-start.12
  46.3 1.1 %collective-permute-done.6.refs_4_ = f32[512,128]{1,0:T(8,128)S(1)} collective-permute-done((f32[512,128]{1,0:T(8,128)S(1)}, f32[512,128]{1,0:T(8,128)S(1)}, u32[]{:S(2)}, u32[]{:S(2)}) %collective-permute-start.6) | collective-permute-done | bytes 262176 | tf_op jit(solution)/shard_map/ppermute | solution.py:361
  47.4 0.4 collective-permute-done.12.refs_10_
  47.8 0.8 src_prep.3
  48.6 7.0 %sweep.8 = f32[8,128,128]{2,1,0:T(8,128)S(1)} custom-call(s32[1]{0:T(128)} %bitcast.my_y, s32[8,8,128]{2,1,0:T(8,128)S(1)} %get-tuple-element.51.lists, bf16[32,128,32]{2,1,0:T(8,128)(2,1)S(1)} %get-tuple-element.42.rf, bf16[32,128,32]{2,1,0:T(8,128)(2,1)S(1)} %get-tuple-element.43.rs, bf16[32,128,48]{2,1,0:T(8,128)(2,1)S(1)} %get-tuple-element.44.rd, ...), custom_call_target="tpu_custom_call" | custom-call | flops 1000000 | bytes 1000000 | tf_op jit(solution)/shard_map/sweep/pallas_call | solution.py:295
  55.7 0.1 collective-permute-start.14
  55.8 3.2 %collective-permute-start.16 = (f32[4,128,128]{2,1,0:T(8,128)S(1)}, f32[4,128,128]{2,1,0:T(8,128)S(1)}, u32[]{:S(2)}, u32[]{:S(2)}) collective-permute-start(f32[4,128,128]{2,1,0:T(8,128)S(1)} %get-tuple-element.60), channel_id=1, source_target_pairs={{0,40},{32,0},{8,32},{40,8},{1,41},{33,1},{9,33},{41,9},{2,42},{34... | collective-permute-start | bytes 786440 | tf_op jit(solution)/shard_map/ppermute | solution.py:384
  59.0 7.6 %sweep.7 = f32[8,128,128]{2,1,0:T(8,128)S(1)} custom-call(s32[1]{0:T(128)} %bitcast.my_y, s32[8,8,128]{2,1,0:T(8,128)S(1)} %get-tuple-element.51.lists, bf16[32,128,32]{2,1,0:T(8,128)(2,1)S(1)} %get-tuple-element.42.rf, bf16[32,128,32]{2,1,0:T(8,128)(2,1)S(1)} %get-tuple-element.43.rs, bf16[32,128,48]{2,1,0:T(8,128)(2,1)S(1)} %get-tuple-element.44.rd, ...), custom_call_target="tpu_custom_call" | custom-call | flops 1000000 | bytes 1000000 | tf_op jit(solution)/shard_map/sweep/pallas_call | solution.py:295
  66.7 0.1 collective-permute-start.15
  66.8 7.0 %sweep.9 = f32[8,128,128]{2,1,0:T(8,128)S(1)} custom-call(s32[1]{0:T(128)} %bitcast.my_y, s32[8,8,128]{2,1,0:T(8,128)S(1)} %get-tuple-element.51.lists, bf16[32,128,32]{2,1,0:T(8,128)(2,1)S(1)} %get-tuple-element.42.rf, bf16[32,128,32]{2,1,0:T(8,128)(2,1)S(1)} %get-tuple-element.43.rs, bf16[32,128,48]{2,1,0:T(8,128)(2,1)S(1)} %get-tuple-element.44.rd, ...), custom_call_target="tpu_custom_call" | custom-call | flops 1000000 | bytes 1000000 | tf_op jit(solution)/shard_map/sweep/pallas_call | solution.py:295
  73.8 2.6 %collective-permute-start.17 = (f32[8,128,128]{2,1,0:T(8,128)S(1)}, f32[8,128,128]{2,1,0:T(8,128)S(1)}, u32[]{:S(2)}, u32[]{:S(2)}) collective-permute-start(f32[8,128,128]{2,1,0:T(8,128)S(1)} %sweep.9), channel_id=1, source_target_pairs={{0,40},{32,0},{8,32},{40,8},{1,41},{33,1},{9,33},{41,9},{2,42},{34... | collective-permute-start | bytes 1572872 | tf_op jit(solution)/shard_map/ppermute | solution.py:384
  76.4 7.7 %sweep.6 = f32[8,128,128]{2,1,0:T(8,128)S(1)} custom-call(s32[1]{0:T(128)} %bitcast.my_y, s32[8,8,128]{2,1,0:T(8,128)S(1)} %get-tuple-element.51.lists, bf16[32,128,32]{2,1,0:T(8,128)(2,1)S(1)} %get-tuple-element.42.rf, bf16[32,128,32]{2,1,0:T(8,128)(2,1)S(1)} %get-tuple-element.43.rs, bf16[32,128,48]{2,1,0:T(8,128)(2,1)S(1)} %get-tuple-element.44.rd, ...), custom_call_target="tpu_custom_call" | custom-call | flops 1000000 | bytes 1000000 | tf_op jit(solution)/shard_map/sweep/pallas_call | solution.py:295
  84.2 2.7 %collective-permute-done.17 = f32[8,128,128]{2,1,0:T(8,128)S(1)} collective-permute-done((f32[8,128,128]{2,1,0:T(8,128)S(1)}, f32[8,128,128]{2,1,0:T(8,128)S(1)}, u32[]{:S(2)}, u32[]{:S(2)}) %collective-permute-start.17) | collective-permute-done | bytes 524320 | tf_op jit(solution)/shard_map/ppermute | solution.py:384
  86.8 0.1 add_add_fusion
  86.9 20.1 %all_to_all.11 = f32[8,128,128]{2,1,0:T(8,128)S(1)} all-to-all(f32[8,128,128]{2,1,0:T(8,128)S(1)} %add_add_fusion), channel_id=1, replica_groups=mesh['x'=4,'yl'=2,'c'=2,'yh'=2,'z'=8] {'z'}, dimensions={0} | all-to-all | bytes 1048576 | tf_op jit(solution)/shard_map/all_to_all | solution.py:395
  107.1 0.6 add.23
  (27 shorter events, 0.2 us)
Async XLA Ops:
  2.0 3.8 %collective-permute-start.4 = (f32[512,128]{1,0:T(8,128)}, f32[512,128]{1,0:T(8,128)S(1)}, u32[]{:S(2)}, u32[]{:S(2)}) collective-permute-start(f32[512,128]{1,0:T(8,128)} %get-tuple-element.31.refs_0_.refs_12_), channel_id=1, source_target_pairs={{0,16},{16,0},{1,17},{17,1},{2,18},{18,2},{3,19},{19,3},{4,20},{20... | collective-permute-start | bytes 786440 | tf_op jit(solution)/shard_map/ppermute | solution.py:361
  2.0 29.0 %collective-permute-start.5 = (f32[640,128]{1,0:T(8,128)}, f32[640,128]{1,0:T(8,128)S(1)}, u32[]{:S(2)}, u32[]{:S(2)}) collective-permute-start(f32[640,128]{1,0:T(8,128)} %get-tuple-element.32.refs_1_.refs_13_), channel_id=1, source_target_pairs={{0,16},{16,0},{1,17},{17,1},{2,18},{18,2},{3,19},{19,3},{4,20},{20... | collective-permute-start | bytes 983048 | tf_op jit(solution)/shard_map/ppermute | solution.py:361
  2.5 28.5 %collective-permute-start.3 = (f32[640,128]{1,0:T(8,128)}, f32[640,128]{1,0:T(8,128)S(1)}, u32[]{:S(2)}, u32[]{:S(2)}) collective-permute-start(f32[640,128]{1,0:T(8,128)} %get-tuple-element.32.refs_1_.refs_13_), channel_id=1, source_target_pairs={{0,192},{64,0},{128,64},{192,128},{1,193},{65,1},{129,65},{193,129... | collective-permute-start | bytes 983048 | tf_op jit(solution)/shard_map/ppermute | solution.py:358
  3.3 27.6 %collective-permute-start.1 = (f32[640,128]{1,0:T(8,128)}, f32[640,128]{1,0:T(8,128)S(1)}, u32[]{:S(2)}, u32[]{:S(2)}) collective-permute-start(f32[640,128]{1,0:T(8,128)} %get-tuple-element.32.refs_1_.refs_13_), channel_id=1, source_target_pairs={{0,64},{64,128},{128,192},{192,0},{1,65},{65,129},{129,193},{193,1... | collective-permute-start | bytes 983048 | tf_op jit(solution)/shard_map/ppermute | solution.py:358
  5.7 25.2 %collective-permute-start.2 = (f32[512,128]{1,0:T(8,128)}, f32[512,128]{1,0:T(8,128)S(1)}, u32[]{:S(2)}, u32[]{:S(2)}) collective-permute-start(f32[512,128]{1,0:T(8,128)} %get-tuple-element.31.refs_0_.refs_12_), channel_id=1, source_target_pairs={{0,192},{64,0},{128,64},{192,128},{1,193},{65,1},{129,65},{193,129... | collective-permute-start | bytes 786440 | tf_op jit(solution)/shard_map/ppermute | solution.py:358
  5.7 25.2 %collective-permute-start = (f32[512,128]{1,0:T(8,128)}, f32[512,128]{1,0:T(8,128)S(1)}, u32[]{:S(2)}, u32[]{:S(2)}) collective-permute-start(f32[512,128]{1,0:T(8,128)} %get-tuple-element.31.refs_0_.refs_12_), channel_id=1, source_target_pairs={{0,64},{64,128},{128,192},{192,0},{1,65},{65,129},{129,193},{193,1... | collective-permute-start | bytes 786440 | tf_op jit(solution)/shard_map/ppermute | solution.py:358
  31.0 14.2 %collective-permute-start.11 = (f32[640,128]{1,0:T(8,128)S(1)}, f32[640,128]{1,0:T(8,128)S(1)}, u32[]{:S(2)}, u32[]{:S(2)}) collective-permute-start(f32[640,128]{1,0:T(8,128)S(1)} %collective-permute-done.3.refs_3_), channel_id=1, source_target_pairs={{0,192},{64,0},{128,64},{192,128},{1,193},{65,1},{129,65},{193,129... | collective-permute-start | bytes 983048 | tf_op jit(solution)/shard_map/ppermute | solution.py:358
  31.1 14.1 %collective-permute-start.10 = (f32[512,128]{1,0:T(8,128)S(1)}, f32[512,128]{1,0:T(8,128)S(1)}, u32[]{:S(2)}, u32[]{:S(2)}) collective-permute-start(f32[512,128]{1,0:T(8,128)S(1)} %collective-permute-done.refs_0_), channel_id=1, source_target_pairs={{0,64},{64,128},{128,192},{192,0},{1,65},{65,129},{129,193},{193,1... | collective-permute-start | bytes 786440 | tf_op jit(solution)/shard_map/ppermute | solution.py:358
  34.3 11.8 %collective-permute-start.8 = (f32[512,128]{1,0:T(8,128)S(1)}, f32[512,128]{1,0:T(8,128)S(1)}, u32[]{:S(2)}, u32[]{:S(2)}) collective-permute-start(f32[512,128]{1,0:T(8,128)S(1)} %collective-permute-done.2.refs_2_), channel_id=1, source_target_pairs={{0,16},{16,0},{1,17},{17,1},{2,18},{18,2},{3,19},{19,3},{4,20},{20... | collective-permute-start | bytes 786440 | tf_op jit(solution)/shard_map/ppermute | solution.py:361
  34.3 13.1 %collective-permute-start.9 = (f32[640,128]{1,0:T(8,128)S(1)}, f32[640,128]{1,0:T(8,128)S(1)}, u32[]{:S(2)}, u32[]{:S(2)}) collective-permute-start(f32[640,128]{1,0:T(8,128)S(1)} %collective-permute-done.3.refs_3_), channel_id=1, source_target_pairs={{0,16},{16,0},{1,17},{17,1},{2,18},{18,2},{3,19},{19,3},{4,20},{20... | collective-permute-start | bytes 983048 | tf_op jit(solution)/shard_map/ppermute | solution.py:361
  34.8 12.6 %collective-permute-start.7 = (f32[640,128]{1,0:T(8,128)S(1)}, f32[640,128]{1,0:T(8,128)S(1)}, u32[]{:S(2)}, u32[]{:S(2)}) collective-permute-start(f32[640,128]{1,0:T(8,128)S(1)} %collective-permute-done.1.refs_1_), channel_id=1, source_target_pairs={{0,16},{16,0},{1,17},{17,1},{2,18},{18,2},{3,19},{19,3},{4,20},{20... | collective-permute-start | bytes 983048 | tf_op jit(solution)/shard_map/ppermute | solution.py:361
  35.9 1.0 copy-start
  36.9 0.9 copy-start.1
  45.2 2.6 %collective-permute-start.13 = (f32[640,128]{1,0:T(8,128)S(1)}, f32[640,128]{1,0:T(8,128)S(1)}, u32[]{:S(2)}, u32[]{:S(2)}) collective-permute-start(f32[640,128]{1,0:T(8,128)S(1)} %collective-permute-done.11.refs_9_), channel_id=1, source_target_pairs={{0,16},{16,0},{1,17},{17,1},{2,18},{18,2},{3,19},{19,3},{4,20},{20... | collective-permute-start | bytes 983048 | tf_op jit(solution)/shard_map/ppermute | solution.py:361
  45.8 1.6 %collective-permute-start.6 = (f32[512,128]{1,0:T(8,128)S(1)}, f32[512,128]{1,0:T(8,128)S(1)}, u32[]{:S(2)}, u32[]{:S(2)}) collective-permute-start(f32[512,128]{1,0:T(8,128)S(1)} %collective-permute-done.refs_0_), channel_id=1, source_target_pairs={{0,16},{16,0},{1,17},{17,1},{2,18},{18,2},{3,19},{19,3},{4,20},{20... | collective-permute-start | bytes 786440 | tf_op jit(solution)/shard_map/ppermute | solution.py:361
  46.1 1.7 %collective-permute-start.12 = (f32[512,128]{1,0:T(8,128)S(1)}, f32[512,128]{1,0:T(8,128)S(1)}, u32[]{:S(2)}, u32[]{:S(2)}) collective-permute-start(f32[512,128]{1,0:T(8,128)S(1)} %collective-permute-done.10.refs_8_), channel_id=1, source_target_pairs={{0,16},{16,0},{1,17},{17,1},{2,18},{18,2},{3,19},{19,3},{4,20},{20... | collective-permute-start | bytes 786440 | tf_op jit(solution)/shard_map/ppermute | solution.py:361
  55.7 10.9 %collective-permute-start.14 = (f32[4,128,128]{2,1,0:T(8,128)S(1)}, f32[4,128,128]{2,1,0:T(8,128)S(1)}, u32[]{:S(2)}, u32[]{:S(2)}) collective-permute-start(f32[4,128,128]{2,1,0:T(8,128)S(1)} %get-tuple-element.59), channel_id=1, source_target_pairs={{0,32},{32,8},{8,40},{40,0},{1,33},{33,9},{9,41},{41,1},{2,34},{34... | collective-permute-start | bytes 786440 | tf_op jit(solution)/shard_map/ppermute | solution.py:384
  55.8 11.0 %collective-permute-start.16 = (f32[4,128,128]{2,1,0:T(8,128)S(1)}, f32[4,128,128]{2,1,0:T(8,128)S(1)}, u32[]{:S(2)}, u32[]{:S(2)}) collective-permute-start(f32[4,128,128]{2,1,0:T(8,128)S(1)} %get-tuple-element.60), channel_id=1, source_target_pairs={{0,40},{32,0},{8,32},{40,8},{1,41},{33,1},{9,33},{41,9},{2,42},{34... | collective-permute-start | bytes 786440 | tf_op jit(solution)/shard_map/ppermute | solution.py:384
  66.7 17.5 %collective-permute-start.15 = (f32[8,128,128]{2,1,0:T(8,128)S(1)}, f32[8,128,128]{2,1,0:T(8,128)S(1)}, u32[]{:S(2)}, u32[]{:S(2)}) collective-permute-start(f32[8,128,128]{2,1,0:T(8,128)S(1)} %pad_maximum_fusion), channel_id=1, source_target_pairs={{0,32},{32,8},{8,40},{40,0},{1,33},{33,9},{9,41},{41,1},{2,34},{34... | collective-permute-start | bytes 1572872 | tf_op jit(solution)/shard_map/ppermute | solution.py:384
  73.8 13.0 %collective-permute-start.17 = (f32[8,128,128]{2,1,0:T(8,128)S(1)}, f32[8,128,128]{2,1,0:T(8,128)S(1)}, u32[]{:S(2)}, u32[]{:S(2)}) collective-permute-start(f32[8,128,128]{2,1,0:T(8,128)S(1)} %sweep.9), channel_id=1, source_target_pairs={{0,40},{32,0},{8,32},{40,8},{1,41},{33,1},{9,33},{41,9},{2,42},{34... | collective-permute-start | bytes 1572872 | tf_op jit(solution)/shard_map/ppermute | solution.py:384
  84.2 22.9 %copy-start.2 = (f32[128,128]{1,0:T(8,128)S(1)}, f32[128,128]{1,0:T(8,128)}, u32[]{:S(2)}) copy-start(f32[128,128]{1,0:T(8,128)} %param.17) | copy-start | bytes 196612

commit v6 on v5

--- a/solution.py
+++ b/solution.py
@@ -23,8 +23,7 @@
 KF, KS, KD = 32, 32, 48
 VMEM_LIMIT = 16 << 20
 UNROLL, TAIL = 16, 8
-HALF = NZ // 2
-FIRST = 4 * BS
+FLUX = SB * BS
 
 
 def contraction_terms():
@@ -111,11 +110,10 @@
 
 
 def pack_kernel(
-    incident, pos, angles, area, keep, lists, counts, recv_pos, recv_angles, first, second, recv_tile
+    incident, pos, angles, area, keep, lists, counts, recv_pos, recv_angles, packed, recv_tile
 ):
-    first[...] = incident[:FIRST, :].astype(jnp.float32)
-    second[: SB * BS - FIRST, :] = incident[FIRST:, :].astype(jnp.float32)
-    second[SB * BS - FIRST :, :] = jnp.zeros((SB * TILE, BS), jnp.float32)
+    packed[:FLUX, :] = incident[...].astype(jnp.float32)
+    packed[FLUX:, :] = jnp.zeros((SB * TILE, BS), jnp.float32)
     scale = keep[...] * area[...] * (1.0 / np.pi)
     rows = [pos[a : a + 1, :] - CENTRE for a in range(3)]
     rows += [component * scale for component in direction(angles[...])]
@@ -123,13 +121,13 @@
     tile = jnp.concatenate(rows, axis=0)
     slot = lax.broadcasted_iota(jnp.int32, (CAP, NYH * NZ), 0)
     for k in range(SB):
-        at = SB * BS - FIRST + k * TILE
-        second[at : at + 8, :] = tile[:, k * BS : (k + 1) * BS]
+        at = FLUX + k * TILE
+        packed[at : at + 8, :] = tile[:, k * BS : (k + 1) * BS]
         for yl in range(NYL):
             slab = ((k // NC) * NYL + yl) * NC + k % NC
             live = slot < counts[slab : slab + 1, :]
             marked = jnp.where(live, lists[slab], -1).astype(jnp.float32)
-            second[at + 8 + yl * CAP : at + 8 + (yl + 1) * CAP, : NYH * NZ] = marked
+            packed[at + 8 + yl * CAP : at + 8 + (yl + 1) * CAP, : NYH * NZ] = marked
     rows = [recv_pos[a : a + 1, :] - CENTRE for a in range(3)]
     rows += direction(recv_angles[...])
     rows += [jnp.zeros((2, BS), jnp.float32)]
@@ -138,18 +136,17 @@
         recv_tile[j] = tile
 
 
-def prepare(me, parts, sf, ss, sd, em, lists):
+def src_prep_kernel(count, me, *refs):
+    packed = refs[:count]
+    sf, ss, sd, em, lists = refs[count:]
     mats = selections(1)
-    count = len(parts)
-    for d, (first, second) in enumerate(parts):
+    for d, ref in enumerate(packed):
         for k in range(SB):
-            ref, start = (first, k * BS) if k * BS < FIRST else (second, k * BS - FIRST)
-            em[d * SB + k] = ref[start : start + BS, :].astype(jnp.bfloat16)
-        at = SB * BS - FIRST
-        tiles = [second[at + k * TILE : at + k * TILE + 8, :] for k in range(SB)]
+            em[d * SB + k] = ref[k * BS : (k + 1) * BS, :].astype(jnp.bfloat16)
+        tiles = [ref[FLUX + k * TILE : FLUX + k * TILE + 8, :] for k in range(SB)]
         q = split_pieces(jnp.concatenate(tiles, axis=1))
-        list_at = pl.multiple_of(at + me[0] * TILE + 8, 8)
-        lists[d] = second[pl.ds(list_at, 8), :].astype(jnp.int32)
+        list_at = pl.multiple_of(FLUX + me[0] * TILE + 8, 8)
+        lists[d] = ref[pl.ds(list_at, 8), :].astype(jnp.int32)
         for m, out in zip(mats, (sf, ss, sd)):
             values = dot(m, q).astype(jnp.bfloat16)
             for k in range(SB):
@@ -162,10 +159,6 @@
     sd[null] = jnp.where(first_row, 1.0, 0.0).astype(jnp.bfloat16)
 
 
-def src_prep_kernel(count, me, *refs):
-    prepare(me, list(zip(refs[: 2 * count : 2], refs[1 : 2 * count : 2])), *refs[2 * count :])
-
-
 def recv_prep_kernel(tiles, rf, rs, rd):
     mats = selections(0)
     for j in range(NJ):
@@ -176,21 +169,24 @@
             ).astype(jnp.bfloat16)
 
 
-def sweep_kernel(count, blocks, added, distance, my_y, lists, rf, rs, rd, sf, ss, sd, em, *refs):
-    *before, out, ids, owner = refs
+def sweep_kernel(count, distances, added, sizes, my_y, lists, rf, rs, rd, sf, ss, sd, em, *refs):
+    before, outs = refs[:added], refs[added:-3]
+    out, ids, owner = refs[-3:]
+    blocks = len(distances) * NZ
     null = sf.shape[0] - 1
     slots = count * CAP // 2
 
     def block_of(j):
-        target = (my_y[0] + distance + (j >> 3)) & (NY - 1)
+        ahead = distances[0]
+        for at in range(1, len(distances)):
+            ahead = jnp.where(j >= at * NZ, distances[at], ahead)
+        target = (my_y[0] + ahead) & (NY - 1)
         return ((target & (NYL - 1)) * NYH + (target >> 1)) * NZ + (j & (NZ - 1))
 
     for j in range(blocks):
         start = jnp.zeros((BS, BS), jnp.float32)
         if added:
-            start = before[0][(distance - 1) * NZ + j]
-        if added == 2 and j >= HALF:
-            start = start + before[1][j - HALF]
+            start = before[0][(distances[j // NZ] - 1) * NZ + j % NZ]
         out[j] = start
 
     def one_block(j, n):
@@ -246,6 +242,10 @@
     long = units // UNROLL
     run(0, UNROLL, long)
     run(long * UNROLL, TAIL, pl.cdiv(units - long * UNROLL, TAIL))
+    at = 0
+    for ref, size in zip(outs, sizes):
+        ref[...] = out[at : at + size]
+        at += size
 
 
 VMEM_SPEC = pl.BlockSpec(memory_space=pltpu.VMEM)
@@ -258,8 +258,8 @@
     return jax.ShapeDtypeStruct(shape, BF16)
 
 
-def src_prep(me, parts):
-    count = len(parts)
+def src_prep(me, packed):
+    count = len(packed)
     rows = count * SB + 1
     return pl.pallas_call(
         functools.partial(src_prep_kernel, count),
@@ -270,12 +270,12 @@
             bf16_shape(rows, BS, BS),
             jax.ShapeDtypeStruct((count, 8, BS), jnp.int32),
         ],
-        in_specs=[SMEM_SPEC] + [VMEM_SPEC] * (2 * count),
+        in_specs=[SMEM_SPEC] + [VMEM_SPEC] * count,
         out_specs=[VMEM_SPEC] * 5,
         name="src_prep",
         compiler_params=PARAMS,
         cost_estimate=pl.CostEstimate(flops=10**6, bytes_accessed=10**6, transcendentals=0),
-    )(me, *[part for pair in parts for part in pair])
+    )(me, *packed)
 
 
 def recv_prep(tiles):
@@ -290,14 +290,17 @@
     )(tiles)
 
 
-def sweep(my_y, distance, recv, src, count, blocks, *before):
+def sweep(my_y, distances, recv, src, count, *before, sizes=None):
     *src, lists = src
+    blocks = len(distances) * NZ
+    sizes = sizes or (blocks,)
     return pl.pallas_call(
-        functools.partial(sweep_kernel, count, blocks, len(before), distance),
-        out_shape=jax.ShapeDtypeStruct((blocks, BS, BS), jnp.float32),
+        functools.partial(sweep_kernel, count, distances, len(before), sizes),
+        out_shape=[jax.ShapeDtypeStruct((size, BS, BS), jnp.float32) for size in sizes],
         in_specs=[SMEM_SPEC] * 2 + [VMEM_SPEC] * (7 + len(before)),
-        out_specs=VMEM_SPEC,
+        out_specs=[VMEM_SPEC] * len(sizes),
         scratch_shapes=[
+            pltpu.VMEM((blocks, BS, BS), jnp.float32),
             pltpu.SMEM((blocks * count * CAP + 4 * UNROLL,), jnp.int32),
             pltpu.SMEM((blocks * count * CAP // 2 + count * CAP + 2 * UNROLL,), jnp.int32),
         ],
@@ -311,12 +314,11 @@
     return pl.pallas_call(
         pack_kernel,
         out_shape=[
-            jax.ShapeDtypeStruct((FIRST, BS), jnp.float32),
-            jax.ShapeDtypeStruct((SB * (BS + TILE) - FIRST, BS), jnp.float32),
+            jax.ShapeDtypeStruct((FLUX + SB * TILE, BS), jnp.float32),
             jax.ShapeDtypeStruct((NJ, 8, BS), jnp.float32),
         ],
         in_specs=[VMEM_SPEC] * 9,
-        out_specs=[VMEM_SPEC] * 3,
+        out_specs=[VMEM_SPEC] * 2,
         name="pack",
         compiler_params=pltpu.CompilerParams(vmem_limit_bytes=60 << 20),
         cost_estimate=pl.CostEstimate(flops=10**6, bytes_accessed=10**6, transcendentals=0),
@@ -342,7 +344,7 @@
     visible_lists,
     visible_counts,
 ):
-    *mine, recv_tile = pack(
+    mine, recv_tile = pack(
         incident,
         src_pos,
         src_angles,
@@ -362,36 +364,28 @@
 
     me = (lax.axis_index("x") * NC + lax.axis_index("c")).astype(jnp.int32).reshape(1)
     my_y = (lax.axis_index("yh") * NYL + lax.axis_index("yl")).astype(jnp.int32).reshape(1)
-    left = [along_x(mine[0], 1), None]
-    right = [None, along_x(mine[1], 3)]
-    left[1], right[0] = along_x(mine[1], 1), along_x(mine[0], 3)
-    own = [other_core(part) for part in mine]
+    far = [along_x(mine, distance) for distance in (1, 3, 2)]
+    own = other_core(mine)
 
     tiles = lax.all_to_all(recv_tile, ("yl", "yh", "z"), 0, 0, tiled=True)
 
-    *left, right[0], right[1], own[0], own[1], tiles = lax.optimization_barrier(
-        (*left, *right, *own, tiles)
-    )
-    far = [along_x(left[0], 1), along_x(right[1], 3)]
-    sides = [left, right] + [[other_core(part) for part in pair] for pair in (left, right)]
-
+    own, tiles = lax.optimization_barrier((own, tiles))
     recv = recv_prep(tiles)
-    begun = sweep(my_y, 1, recv, src_prep(me, [mine, own]), 2, 3 * NZ)
+    (begun,) = sweep(my_y, (1, 2, 3), recv, src_prep(me, [mine, own]), 2)
     *far, begun = lax.optimization_barrier((*far, begun))
-    src = src_prep(me, sides + [far, [other_core(part) for part in far]] + [mine, own])
+    src = src_prep(me, far + [other_core(block) for block in far] + [mine, own])
 
     def along_y(block, distance):
         return lax.ppermute(block, ("yl", "yh"), y_route(distance))
 
-    def part(distance, *passing):
-        return sweep(my_y, distance, recv, src, GROUP - 2, NZ, begun, *passing)
-
-    across = part(2)
-    by_left, by_right = along_y(across[:HALF], 1), along_y(across[HALF:], 3)
-    ahead = part(1)
-    ahead = along_y(jnp.concatenate([ahead[:HALF] + by_left, ahead[HALF:]], axis=0), 1)
-    behind = along_y(part(3, by_right), 3)
-    total = sweep(my_y, 0, recv, src, GROUP, NZ) + ahead + behind
+    half = NZ // 2
+    parts = sweep(my_y, (2,), recv, src, GROUP - 2, begun, sizes=(half, half))
+    by_left, by_right = along_y(parts[0], 1), along_y(parts[1], 3)
+    ahead, behind = sweep(my_y, (1, 3), recv, src, GROUP - 2, begun, sizes=(NZ, NZ))
+    ahead = along_y(ahead.at[:half].add(by_left), 1)
+    behind = along_y(behind.at[half:].add(by_right), 3)
+    (total,) = sweep(my_y, (0,), recv, src, GROUP)
+    total = total + ahead + behind
     pieces = lax.all_to_all(total, "z", 0, 0, tiled=True)
     return direct + jnp.sum(pieces, axis=0)
 

time: 108 us -> 104 us (0.963)
  blocking collectives: 42 us -> 24.5 us
  waiting for transfers between devices: 4.18 us -> 18.8 us
  Pallas kernels: 40.6 us -> 34.6 us
  starting transfers between devices: 17.9 us -> 23.8 us
    all_to_all x1 -> x0, blocking collectives: 22 us -> none  [shards(): tiles = lax.all_to_all(recv_tile, ('yl', 'yh', 'z'), 0, 0, tiled=True)]
    all_to_all x0 -> x1, starting transfers between devices: none -> 11.5 us  [shards(): tiles = lax.all_to_all(recv_tile, ('yl', 'yh', 'z'), 0, 0, tiled=True)]
    all_to_all x0 -> x1, waiting for transfers between devices: none -> 10.5 us  [shards(): tiles = lax.all_to_all(recv_tile, ('yl', 'yh', 'z'), 0, 0, tiled=True)]
    pallas_call x6 -> x5, Pallas kernels: 38.3 us -> 32.3 us  [the longest x4 30.3 us: sweep(): pl.pallas_call(functools.partial(sweep_kernel, count, distances, len(befo...]
    ppermute x6 -> x3, starting transfers between devices: 9.78 us -> 4.64 us  [along_x(): lax.ppermute(block, 'x', [(i, (i + distance) % NX) for i in range(NX)])]
    all_to_all x1, blocking collectives: 20.1 us -> 24.5 us  [shards(): pieces = lax.all_to_all(total, 'z', 0, 0, tiled=True)]
    ppermute x4, waiting for transfers between devices: 2.66 us -> 5.2 us  [along_y(): return lax.ppermute(block, ('yl', 'yh'), y_route(distance))]
    ppermute x8 -> x4, waiting for transfers between devices: 1.5 us -> 3.08 us  [other_core(): return lax.ppermute(block, 'c', [(0, 1), (1, 0)])]
  transfers between devices with their start and end apart: 18 -> 12, of which waited for: 3 -> 6; matrix products, arithmetic and copies ran while one was open for 0% -> 0% of each run, Pallas kernels for 29% -> 25%
where the time goes in v6:
time: 104 us
  Pallas kernels  34.6 us (33%)
  blocking collectives  24.5 us (24%)
  starting transfers between devices  23.8 us (23%)
  waiting for transfers between devices  18.8 us (18%)
  local copies, waits for them, and re-layouts  1.06 us (1%)
    pallas_call x4, Pallas kernels, sweep(): pl.pallas_call(functools.partial(sweep_kernel, count, distances, len(befo...  30.3 us
    all_to_all x1, blocking collectives, shards(): pieces = lax.all_to_all(total, 'z', 0, 0, tiled=True)  24.5 us
    all_to_all x1, starting transfers between devices, shards(): tiles = lax.all_to_all(recv_tile, ('yl', 'yh', 'z'), 0, 0, tiled=True)  11.5 us
    all_to_all x1, waiting for transfers between devices, shards(): tiles = lax.all_to_all(recv_tile, ('yl', 'yh', 'z'), 0, 0, tiled=True)  10.5 us
    ppermute x4, starting transfers between devices, along_y(): return lax.ppermute(block, ('yl', 'yh'), y_route(distance))  6.97 us
    ppermute x4, waiting for transfers between devices, along_y(): return lax.ppermute(block, ('yl', 'yh'), y_route(distance))  5.2 us
    ppermute x3, starting transfers between devices, along_x(): lax.ppermute(block, 'x', [(i, (i + distance) % NX) for i in range(NX)])  4.64 us
    ppermute x4, waiting for transfers between devices, other_core(): return lax.ppermute(block, 'c', [(0, 1), (1, 0)])  3.08 us
  transfers between devices with their start and end apart: 12, of which 6 were waited for; matrix products, arithmetic and copies ran while one was open for 0% of the time, Pallas kernels for 25%

profile of v6, /device:TPU:6, one launch (start us, length us, event | category | flops | bytes accessed | tf_op | source)
XLA Modules:
  0.0 103.7 jit_solution(5034499841045223108)
XLA Ops:
  0.0 2.0 %pack.1 = (f32[1152,128]{1,0:T(8,128)}, f32[32,8,128]{2,1,0:T(8,128)}) custom-call(bf16[1024,128]{1,0:T(8,128)(2,1)} %incident.1, f32[3,1024]{1,0:T(4,128)} %pos.1, f32[2,1024]{1,0:T(2,128)} %angles.1, f32[1,1024]{1,0:T(1,128)} %bitcast.10, f32[1,1024]{1,0:T(1,128)} %bitcast.11, s32[16,4,16]{2,1,0:T(4,128)} %bitcast.8, s32[16,16]{1,0:T(8,128)} %bitcast.9, ...), custom_call_target="tpu_custom_call" | custom-call | flops 1000000 | bytes 1000000 | tf_op jit(solution)/shard_map/pack/pallas_call | solution.py:314
  2.0 1.4 %collective-permute-start.2 = (f32[1152,128]{1,0:T(8,128)}, f32[1152,128]{1,0:T(8,128)S(1)}, u32[]{:S(2)}, u32[]{:S(2)}) collective-permute-start(f32[1152,128]{1,0:T(8,128)} %get-tuple-element.54.refs_0_.refs_6_), channel_id=1, source_target_pairs={{0,128},{64,192},{128,0},{192,64},{1,129},{65,193},{129,1},{193,65... | collective-permute-start | bytes 1769480 | tf_op jit(solution)/shard_map/ppermute | solution.py:360
  3.4 1.7 %collective-permute-start.1 = (f32[1152,128]{1,0:T(8,128)}, f32[1152,128]{1,0:T(8,128)S(1)}, u32[]{:S(2)}, u32[]{:S(2)}) collective-permute-start(f32[1152,128]{1,0:T(8,128)} %get-tuple-element.54.refs_0_.refs_6_), channel_id=1, source_target_pairs={{0,192},{64,0},{128,64},{192,128},{1,193},{65,1},{129,65},{193,129... | collective-permute-start | bytes 1769480 | tf_op jit(solution)/shard_map/ppermute | solution.py:360
  5.1 1.6 %collective-permute-start = (f32[1152,128]{1,0:T(8,128)}, f32[1152,128]{1,0:T(8,128)S(1)}, u32[]{:S(2)}, u32[]{:S(2)}) collective-permute-start(f32[1152,128]{1,0:T(8,128)} %get-tuple-element.54.refs_0_.refs_6_), channel_id=1, source_target_pairs={{0,64},{64,128},{128,192},{192,0},{1,65},{65,129},{129,193},{193,1... | collective-permute-start | bytes 1769480 | tf_op jit(solution)/shard_map/ppermute | solution.py:360
  6.6 11.5 %all-to-all-start = ((f32[32,8,128]{2,1,0:T(8,128)}), f32[32,8,128]{2,1,0:T(8,128)S(1)}, u32[]{:S(2)}, u32[]{:S(2)}) async-start(f32[32,8,128]{2,1,0:T(8,128)} %get-tuple-element.55), calls=%async_computation | async-start | bytes 262144 | tf_op jit(solution)/shard_map/all_to_all | solution.py:370
  18.1 10.5 %all-to-all-done.tiles = f32[32,8,128]{2,1,0:T(8,128)S(1)} async-done(((f32[32,8,128]{2,1,0:T(8,128)}), f32[32,8,128]{2,1,0:T(8,128)S(1)}, u32[]{:S(2)}, u32[]{:S(2)}) %all-to-all-start) | async-done | bytes 131104 | tf_op jit(solution)/shard_map/all_to_all | solution.py:370
  28.6 1.1 %recv_prep.1 = (bf16[32,128,32]{2,1,0:T(8,128)(2,1)S(1)}, bf16[32,128,32]{2,1,0:T(8,128)(2,1)S(1)}, bf16[32,128,48]{2,1,0:T(8,128)(2,1)S(1)}) custom-call(f32[32,8,128]{2,1,0:T(8,128)S(1)} %all-to-all-done.tiles), custom_call_target="tpu_custom_call" | custom-call | flops 1000000 | bytes 1000000 | tf_op jit(solution)/shard_map/recv_prep/pallas_call | solution.py:282
  29.7 1.1 %copy-done = f32[1152,128]{1,0:T(8,128)S(1)} copy-done((f32[1152,128]{1,0:T(8,128)S(1)}, f32[1152,128]{1,0:T(8,128)}, u32[]{:S(2)}) %copy-start) | copy-done | bytes 589848
  30.8 0.4 src_prep.2
  31.1 6.4 %sweep.4.refs_0_ = f32[24,128,128]{2,1,0:T(8,128)S(1)} custom-call(s32[1]{0:T(128)} %bitcast.my_y, s32[2,8,128]{2,1,0:T(8,128)S(1)} %get-tuple-element.57.lists, bf16[32,128,32]{2,1,0:T(8,128)(2,1)S(1)} %get-tuple-element.59.rf, bf16[32,128,32]{2,1,0:T(8,128)(2,1)S(1)} %get-tuple-element.60.rs, bf16[32,128,48]{2,1,0:T(8,128)(2,1)S(1)} %get-tuple-element.61.rd, ...), custom_call_target="tpu_custom_call" | custom-call | flops 1000000 | bytes 1000000 | tf_op jit(solution)/shard_map/sweep/pallas_call | solution.py:297
  37.6 0.1 collective-permute-start.4
  37.7 0.5 collective-permute-start.5
  38.2 0.1 collective-permute-start.6
  38.3 1.4 %collective-permute-done.4.refs_3_ = f32[1152,128]{1,0:T(8,128)S(1)} collective-permute-done((f32[1152,128]{1,0:T(8,128)S(1)}, f32[1152,128]{1,0:T(8,128)S(1)}, u32[]{:S(2)}, u32[]{:S(2)}) %collective-permute-start.4) | collective-permute-done | bytes 589856 | tf_op jit(solution)/shard_map/ppermute | solution.py:363
  39.7 0.8 collective-permute-done.5.refs_4_
  40.5 0.8 collective-permute-done.6.refs_5_
  41.4 0.8 src_prep.3
  42.2 5.8 %sweep.7 = (f32[4,128,128]{2,1,0:T(8,128)S(1)}, f32[4,128,128]{2,1,0:T(8,128)S(1)}) custom-call(s32[1]{0:T(128)} %bitcast.my_y, s32[8,8,128]{2,1,0:T(8,128)S(1)} %get-tuple-element.69.lists, bf16[32,128,32]{2,1,0:T(8,128)(2,1)S(1)} %get-tuple-element.59.rf, bf16[32,128,32]{2,1,0:T(8,128)(2,1)S(1)} %get-tuple-element.60.rs, ...), custom_call_target="tpu_custom_call" | custom-call | flops 1000000 | bytes 1000000 | tf_op jit(solution)/shard_map/sweep/pallas_call | solution.py:297
  48.0 1.8 %collective-permute-start.9 = (f32[4,128,128]{2,1,0:T(8,128)S(1)}, f32[4,128,128]{2,1,0:T(8,128)S(1)}, u32[]{:S(2)}, u32[]{:S(2)}) collective-permute-start(f32[4,128,128]{2,1,0:T(8,128)S(1)} %get-tuple-element.78), channel_id=1, source_target_pairs={{0,40},{32,0},{8,32},{40,8},{1,41},{33,1},{9,33},{41,9},{2,42},{34... | collective-permute-start | bytes 786440 | tf_op jit(solution)/shard_map/ppermute | solution.py:379
  49.8 0.5 collective-permute-start.7
  50.3 10.4 %sweep.6 = (f32[8,128,128]{2,1,0:T(8,128)S(1)}, f32[8,128,128]{2,1,0:T(8,128)S(1)}) custom-call(s32[1]{0:T(128)} %bitcast.my_y, s32[8,8,128]{2,1,0:T(8,128)S(1)} %get-tuple-element.69.lists, bf16[32,128,32]{2,1,0:T(8,128)(2,1)S(1)} %get-tuple-element.59.rf, bf16[32,128,32]{2,1,0:T(8,128)(2,1)S(1)} %get-tuple-element.60.rs, ...), custom_call_target="tpu_custom_call" | custom-call | flops 1000000 | bytes 1000000 | tf_op jit(solution)/shard_map/sweep/pallas_call | solution.py:297
  60.7 0.1 add_dynamic-update-slice_fusion
  60.8 4.6 %collective-permute-start.10 = (f32[8,128,128]{2,1,0:T(8,128)S(1)}, f32[8,128,128]{2,1,0:T(8,128)S(1)}, u32[]{:S(2)}, u32[]{:S(2)}) collective-permute-start(f32[8,128,128]{2,1,0:T(8,128)S(1)} %add_dynamic-update-slice_fusion), channel_id=1, source_target_pairs={{0,40},{32,0},{8,32},{40,8},{1,41},{33,1},{9,33},{41,9},{2,42},{34... | collective-permute-start | bytes 1572872 | tf_op jit(solution)/shard_map/ppermute | solution.py:379
  65.3 0.1 add_dynamic-update-slice_fusion.1
  65.4 0.1 collective-permute-start.8
  65.5 7.8 %sweep.5 = f32[8,128,128]{2,1,0:T(8,128)S(1)} custom-call(s32[1]{0:T(128)} %bitcast.my_y, s32[8,8,128]{2,1,0:T(8,128)S(1)} %get-tuple-element.69.lists, bf16[32,128,32]{2,1,0:T(8,128)(2,1)S(1)} %get-tuple-element.59.rf, bf16[32,128,32]{2,1,0:T(8,128)(2,1)S(1)} %get-tuple-element.60.rs, bf16[32,128,48]{2,1,0:T(8,128)(2,1)S(1)} %get-tuple-element.61.rd, ...), custom_call_target="tpu_custom_call" | custom-call | flops 1000000 | bytes 1000000 | tf_op jit(solution)/shard_map/sweep/pallas_call | solution.py:297
  73.3 0.0 copy-start.1
  73.3 2.1 %collective-permute-done.10 = f32[8,128,128]{2,1,0:T(8,128)S(1)} collective-permute-done((f32[8,128,128]{2,1,0:T(8,128)S(1)}, f32[8,128,128]{2,1,0:T(8,128)S(1)}, u32[]{:S(2)}, u32[]{:S(2)}) %collective-permute-start.10) | collective-permute-done | bytes 524320 | tf_op jit(solution)/shard_map/ppermute | solution.py:379
  75.4 3.1 %collective-permute-done.8 = f32[8,128,128]{2,1,0:T(8,128)S(1)} collective-permute-done((f32[8,128,128]{2,1,0:T(8,128)S(1)}, f32[8,128,128]{2,1,0:T(8,128)S(1)}, u32[]{:S(2)}, u32[]{:S(2)}) %collective-permute-start.8) | collective-permute-done | bytes 524320 | tf_op jit(solution)/shard_map/ppermute | solution.py:379
  78.5 0.1 add_add_fusion
  78.5 24.5 %all_to_all.10 = f32[8,128,128]{2,1,0:T(8,128)S(1)} all-to-all(f32[8,128,128]{2,1,0:T(8,128)S(1)} %add_add_fusion), channel_id=1, replica_groups=mesh['x'=4,'yl'=2,'c'=2,'yh'=2,'z'=8] {'z'}, dimensions={0} | all-to-all | bytes 1048576 | tf_op jit(solution)/shard_map/all_to_all | solution.py:389
  103.1 0.6 add.35
  (10 shorter events, 0.1 us)
Async XLA Ops:
  2.0 26.6 %collective-permute-start.3 = (f32[1152,128]{1,0:T(8,128)}, f32[1152,128]{1,0:T(8,128)S(1)}, u32[]{:S(2)}, u32[]{:S(2)}) collective-permute-start(f32[1152,128]{1,0:T(8,128)} %get-tuple-element.54.refs_0_.refs_6_), channel_id=1, source_target_pairs={{0,16},{16,0},{1,17},{17,1},{2,18},{18,2},{3,19},{19,3},{4,20},{20... | collective-permute-start | bytes 1769480 | tf_op jit(solution)/shard_map/ppermute | solution.py:363
  2.0 35.6 %collective-permute-start.2 = (f32[1152,128]{1,0:T(8,128)}, f32[1152,128]{1,0:T(8,128)S(1)}, u32[]{:S(2)}, u32[]{:S(2)}) collective-permute-start(f32[1152,128]{1,0:T(8,128)} %get-tuple-element.54.refs_0_.refs_6_), channel_id=1, source_target_pairs={{0,128},{64,192},{128,0},{192,64},{1,129},{65,193},{129,1},{193,65... | collective-permute-start | bytes 1769480 | tf_op jit(solution)/shard_map/ppermute | solution.py:360
  3.4 34.2 %collective-permute-start.1 = (f32[1152,128]{1,0:T(8,128)}, f32[1152,128]{1,0:T(8,128)S(1)}, u32[]{:S(2)}, u32[]{:S(2)}) collective-permute-start(f32[1152,128]{1,0:T(8,128)} %get-tuple-element.54.refs_0_.refs_6_), channel_id=1, source_target_pairs={{0,192},{64,0},{128,64},{192,128},{1,193},{65,1},{129,65},{193,129... | collective-permute-start | bytes 1769480 | tf_op jit(solution)/shard_map/ppermute | solution.py:360
  5.1 32.5 %collective-permute-start = (f32[1152,128]{1,0:T(8,128)}, f32[1152,128]{1,0:T(8,128)S(1)}, u32[]{:S(2)}, u32[]{:S(2)}) collective-permute-start(f32[1152,128]{1,0:T(8,128)} %get-tuple-element.54.refs_0_.refs_6_), channel_id=1, source_target_pairs={{0,64},{64,128},{128,192},{192,0},{1,65},{65,129},{129,193},{193,1... | collective-permute-start | bytes 1769480 | tf_op jit(solution)/shard_map/ppermute | solution.py:360
  6.6 22.0 %all-to-all-start = ((f32[32,8,128]{2,1,0:T(8,128)}), f32[32,8,128]{2,1,0:T(8,128)S(1)}, u32[]{:S(2)}, u32[]{:S(2)}) async-start(f32[32,8,128]{2,1,0:T(8,128)} %get-tuple-element.55), calls=%async_computation | async-start | bytes 262144 | tf_op jit(solution)/shard_map/all_to_all | solution.py:370
  29.7 1.1 %copy-start = (f32[1152,128]{1,0:T(8,128)S(1)}, f32[1152,128]{1,0:T(8,128)}, u32[]{:S(2)}) copy-start(f32[1152,128]{1,0:T(8,128)} %get-tuple-element.54.refs_0_.refs_6_) | copy-start | bytes 1769476
  37.6 2.1 %collective-permute-start.4 = (f32[1152,128]{1,0:T(8,128)S(1)}, f32[1152,128]{1,0:T(8,128)S(1)}, u32[]{:S(2)}, u32[]{:S(2)}) collective-permute-start(f32[1152,128]{1,0:T(8,128)S(1)} %collective-permute-done.refs_0_), channel_id=1, source_target_pairs={{0,16},{16,0},{1,17},{17,1},{2,18},{18,2},{3,19},{19,3},{4,20},{20... | collective-permute-start | bytes 1769480 | tf_op jit(solution)/shard_map/ppermute | solution.py:363
  37.7 2.8 %collective-permute-start.5 = (f32[1152,128]{1,0:T(8,128)S(1)}, f32[1152,128]{1,0:T(8,128)S(1)}, u32[]{:S(2)}, u32[]{:S(2)}) collective-permute-start(f32[1152,128]{1,0:T(8,128)S(1)} %collective-permute-done.1.refs_1_), channel_id=1, source_target_pairs={{0,16},{16,0},{1,17},{17,1},{2,18},{18,2},{3,19},{19,3},{4,20},{20... | collective-permute-start | bytes 1769480 | tf_op jit(solution)/shard_map/ppermute | solution.py:363
  38.2 3.2 %collective-permute-start.6 = (f32[1152,128]{1,0:T(8,128)S(1)}, f32[1152,128]{1,0:T(8,128)S(1)}, u32[]{:S(2)}, u32[]{:S(2)}) collective-permute-start(f32[1152,128]{1,0:T(8,128)S(1)} %collective-permute-done.2.refs_2_), channel_id=1, source_target_pairs={{0,16},{16,0},{1,17},{17,1},{2,18},{18,2},{3,19},{19,3},{4,20},{20... | collective-permute-start | bytes 1769480 | tf_op jit(solution)/shard_map/ppermute | solution.py:363
  48.0 12.7 %collective-permute-start.9 = (f32[4,128,128]{2,1,0:T(8,128)S(1)}, f32[4,128,128]{2,1,0:T(8,128)S(1)}, u32[]{:S(2)}, u32[]{:S(2)}) collective-permute-start(f32[4,128,128]{2,1,0:T(8,128)S(1)} %get-tuple-element.78), channel_id=1, source_target_pairs={{0,40},{32,0},{8,32},{40,8},{1,41},{33,1},{9,33},{41,9},{2,42},{34... | collective-permute-start | bytes 786440 | tf_op jit(solution)/shard_map/ppermute | solution.py:379
  49.8 15.5 %collective-permute-start.7 = (f32[4,128,128]{2,1,0:T(8,128)S(1)}, f32[4,128,128]{2,1,0:T(8,128)S(1)}, u32[]{:S(2)}, u32[]{:S(2)}) collective-permute-start(f32[4,128,128]{2,1,0:T(8,128)S(1)} %get-tuple-element.76), channel_id=1, source_target_pairs={{0,32},{32,8},{8,40},{40,0},{1,33},{33,9},{9,41},{41,1},{2,34},{34... | collective-permute-start | bytes 786440 | tf_op jit(solution)/shard_map/ppermute | solution.py:379
  60.8 14.6 %collective-permute-start.10 = (f32[8,128,128]{2,1,0:T(8,128)S(1)}, f32[8,128,128]{2,1,0:T(8,128)S(1)}, u32[]{:S(2)}, u32[]{:S(2)}) collective-permute-start(f32[8,128,128]{2,1,0:T(8,128)S(1)} %add_dynamic-update-slice_fusion), channel_id=1, source_target_pairs={{0,40},{32,0},{8,32},{40,8},{1,41},{33,1},{9,33},{41,9},{2,42},{34... | collective-permute-start | bytes 1572872 | tf_op jit(solution)/shard_map/ppermute | solution.py:379
  65.4 13.1 %collective-permute-start.8 = (f32[8,128,128]{2,1,0:T(8,128)S(1)}, f32[8,128,128]{2,1,0:T(8,128)S(1)}, u32[]{:S(2)}, u32[]{:S(2)}) collective-permute-start(f32[8,128,128]{2,1,0:T(8,128)S(1)} %add_dynamic-update-slice_fusion.1), channel_id=1, source_target_pairs={{0,32},{32,8},{8,40},{40,0},{1,33},{33,9},{9,41},{41,1},{2,34},{34... | collective-permute-start | bytes 1572872 | tf_op jit(solution)/shard_map/ppermute | solution.py:379
  73.3 29.8 %copy-start.1 = (f32[128,128]{1,0:T(8,128)S(1)}, f32[128,128]{1,0:T(8,128)}, u32[]{:S(2)}) copy-start(f32[128,128]{1,0:T(8,128)} %param.21) | copy-start | bytes 196612

commit v7 on v6

--- a/solution.py
+++ b/solution.py
@@ -17,13 +17,17 @@
 GROUP = NX * NC
 NJ = NY * NZ
 CENTRE = 3.0
-TILE = 16
+TILE = 8
 POS, NRM, AREA = 0, 3, 6
 ROWS, DOT, SQA, SQB, ONE = 16, 8, 9, 10, 11
 KF, KS, KD = 32, 32, 48
 VMEM_LIMIT = 16 << 20
 UNROLL, TAIL = 16, 8
 FLUX = SB * BS
+LISTS = FLUX + SB * TILE
+LANES = NYH * NZ
+TABLE = 40
+COUNT = GROUP * CAP
 
 
 def contraction_terms():
@@ -113,21 +117,21 @@
     incident, pos, angles, area, keep, lists, counts, recv_pos, recv_angles, packed, recv_tile
 ):
     packed[:FLUX, :] = incident[...].astype(jnp.float32)
-    packed[FLUX:, :] = jnp.zeros((SB * TILE, BS), jnp.float32)
     scale = keep[...] * area[...] * (1.0 / np.pi)
     rows = [pos[a : a + 1, :] - CENTRE for a in range(3)]
     rows += [component * scale for component in direction(angles[...])]
     rows += [area[...], jnp.zeros_like(scale)]
     tile = jnp.concatenate(rows, axis=0)
-    slot = lax.broadcasted_iota(jnp.int32, (CAP, NYH * NZ), 0)
+    slot = lax.broadcasted_iota(jnp.int32, (CAP, LANES), 0)
     for k in range(SB):
-        at = FLUX + k * TILE
-        packed[at : at + 8, :] = tile[:, k * BS : (k + 1) * BS]
+        packed[FLUX + k * TILE : FLUX + (k + 1) * TILE, :] = tile[:, k * BS : (k + 1) * BS]
+    for k in range(GROUP):
         for yl in range(NYL):
             slab = ((k // NC) * NYL + yl) * NC + k % NC
             live = slot < counts[slab : slab + 1, :]
             marked = jnp.where(live, lists[slab], -1).astype(jnp.float32)
-            packed[at + 8 + yl * CAP : at + 8 + (yl + 1) * CAP, : NYH * NZ] = marked
+            rows = slice(LISTS + yl * CAP, LISTS + (yl + 1) * CAP)
+            packed[rows, k * LANES : (k + 1) * LANES] = marked
     rows = [recv_pos[a : a + 1, :] - CENTRE for a in range(3)]
     rows += direction(recv_angles[...])
     rows += [jnp.zeros((2, BS), jnp.float32)]
@@ -136,17 +140,35 @@
         recv_tile[j] = tile
 
 
-def src_prep_kernel(count, me, *refs):
+def compact(count, first, packed, table):
+    place = lax.broadcasted_iota(jnp.int32, (COUNT, BS), 0)
+    for yl in range(NYL):
+        entries = jnp.full((COUNT, BS), count * SB, jnp.int32)
+        filled = jnp.zeros((1, BS), jnp.int32)
+        for d in range(count):
+            if d == first:
+                table[yl * TABLE + COUNT : yl * TABLE + COUNT + 1, :] = filled
+            for c in range(CAP):
+                at = LISTS + yl * CAP + c
+                value = packed[d][at : at + 1, :].astype(jnp.int32)
+                live = value >= 0
+                entries = jnp.where(place == jnp.where(live, filled, -1), value + d * SB, entries)
+                filled = filled + live.astype(jnp.int32)
+        table[yl * TABLE : yl * TABLE + COUNT, :] = entries
+        table[yl * TABLE + COUNT + 1 : yl * TABLE + COUNT + 2, :] = filled
+
+
+def src_prep_kernel(count, first, *refs):
     packed = refs[:count]
-    sf, ss, sd, em, lists = refs[count:]
+    sf, ss, sd, em, table = refs[count:]
     mats = selections(1)
+    table[...] = jnp.zeros(table.shape, jnp.int32)
+    compact(count, first, packed, table)
     for d, ref in enumerate(packed):
         for k in range(SB):
             em[d * SB + k] = ref[k * BS : (k + 1) * BS, :].astype(jnp.bfloat16)
-        tiles = [ref[FLUX + k * TILE : FLUX + k * TILE + 8, :] for k in range(SB)]
+        tiles = [ref[FLUX + k * TILE : FLUX + (k + 1) * TILE, :] for k in range(SB)]
         q = split_pieces(jnp.concatenate(tiles, axis=1))
-        list_at = pl.multiple_of(FLUX + me[0] * TILE + 8, 8)
-        lists[d] = ref[pl.ds(list_at, 8), :].astype(jnp.int32)
         for m, out in zip(mats, (sf, ss, sd)):
             values = dot(m, q).astype(jnp.bfloat16)
             for k in range(SB):
@@ -169,79 +191,69 @@
             ).astype(jnp.bfloat16)
 
 
-def sweep_kernel(count, distances, added, sizes, my_y, lists, rf, rs, rd, sf, ss, sd, em, *refs):
-    before, outs = refs[:added], refs[added:-3]
-    out, ids, owner = refs[-3:]
-    blocks = len(distances) * NZ
+def sweep_kernel(most, whole, distances, added, sizes, place, table, rf, rs, rd, sf, ss, sd, em, *refs):
+    before, outs = refs[:added], refs[added:-2]
+    out, codes = refs[-2:]
     null = sf.shape[0] - 1
-    slots = count * CAP // 2
-
-    def block_of(j):
-        ahead = distances[0]
-        for at in range(1, len(distances)):
-            ahead = jnp.where(j >= at * NZ, distances[at], ahead)
-        target = (my_y[0] + ahead) & (NY - 1)
-        return ((target & (NYL - 1)) * NYH + (target >> 1)) * NZ + (j & (NZ - 1))
-
-    for j in range(blocks):
+    my_y, lane = place[0], place[1] * LANES
+
+    for j in range(len(distances) * NZ):
         start = jnp.zeros((BS, BS), jnp.float32)
         if added:
             start = before[0][(distances[j // NZ] - 1) * NZ + j % NZ]
         out[j] = start
 
-    def one_block(j, n):
-        block = block_of(j)
-        row = (block >> 4) * CAP
-        lane = block & (NYH * NZ - 1)
-        for t in range(slots):
-            owner[n // 2 + t] = j
-        for d in range(count):
-            used = []
-            for c in range(CAP):
-                value = lists[d, row + c, lane]
-                ids[n + c] = d * SB + value
-                used.append((value >= 0).astype(jnp.int32))
-            n = n + ((used[0] + used[1]) + (used[2] + used[3]))
-        ids[n] = null
-        return n + n % 2
-
-    n = lax.fori_loop(0, blocks, one_block, 0)
-    for t in range(2 * TAIL):
-        ids[n + t] = null
+    n = jnp.int32(0)
+    for at, distance in enumerate(distances):
+        target = (my_y + distance) & (NY - 1)
+        base = ((target & (NYL - 1)) * NYH + (target >> 1)) * NZ
+
+        def one_block(z, n, at=at, base=base):
+            block = base + z
+            used = table[(block >> 4) * TABLE + COUNT + int(whole), lane + (block & (LANES - 1))]
+            code = (block << 8) | ((z + at * NZ) << 16)
+            for t in range(most * CAP // 2):
+                codes[n + t] = code + t
+            units = (used + 1) >> 1
+            last = jnp.maximum(units - 1, 0)
+            codes[n + last] = (code + last) | ((used & 1) << 24)
+            return n + units
+
+        n = lax.fori_loop(0, NZ, one_block, n)
     for t in range(TAIL):
-        owner[n // 2 + t] = 0
-
-    def front(u):
-        a, b = ids[2 * u], ids[2 * u + 1]
-        j = block_of(owner[u])
-
+        codes[n + t] = 3 << 24
+
+    def decode(u):
+        code = codes[u]
+        block = (code >> 8) & 255
+        row = (block >> 4) * TABLE + 2 * (code & 255)
+        column = lane + (block & (LANES - 1))
+        a = jnp.where(code >= 2 << 24, null, table[row, column])
+        b = jnp.where(code >= 1 << 24, null, table[row + 1, column])
+        return a, b, block, (code >> 16) & 255
+
+    def front(a, b, block, j):
         def pair(ref):
             return jnp.concatenate([ref[a], ref[b]], axis=1)
 
-        facing = jnp.maximum(dot(rf[j], pair(sf)), 0.0)
-        seen = jnp.maximum(dot(rs[j], pair(ss)), 0.0)
-        spread = dot(rd[j], pair(sd))
+        facing = jnp.maximum(dot(rf[block], pair(sf)), 0.0)
+        seen = jnp.maximum(dot(rs[block], pair(ss)), 0.0)
+        spread = dot(rd[block], pair(sd))
         return (facing * seen / (spread * spread)).astype(jnp.bfloat16)
-
-    def back(u, values):
-        a, b = ids[2 * u], ids[2 * u + 1]
-        j = owner[u]
-        out[j] = out[j] + dot(values, jnp.concatenate([em[a], em[b]], axis=0))
 
     def run(first_unit, width, steps):
         def step(i, carry):
-            units = [first_unit + i * width + r for r in range(width)]
-            values = [front(u) for u in units]
-            for u, value in zip(units, values):
-                back(u, value)
+            units = [decode(first_unit + i * width + r) for r in range(width)]
+            values = [front(*unit) for unit in units]
+            for (a, b, block, j), value in zip(units, values):
+                out[j] = out[j] + dot(value, jnp.concatenate([em[a], em[b]], axis=0))
             return carry
 
         lax.fori_loop(0, steps, step, 0)
 
-    units = n // 2
-    long = units // UNROLL
+    long = n // UNROLL
     run(0, UNROLL, long)
-    run(long * UNROLL, TAIL, pl.cdiv(units - long * UNROLL, TAIL))
+    run(long * UNROLL, TAIL, pl.cdiv(n - long * UNROLL, TAIL))
     at = 0
     for ref, size in zip(outs, sizes):
         ref[...] = out[at : at + size]
@@ -258,24 +270,24 @@
     return jax.ShapeDtypeStruct(shape, BF16)
 
 
-def src_prep(me, packed):
+def src_prep(packed, first):
     count = len(packed)
     rows = count * SB + 1
     return pl.pallas_call(
-        functools.partial(src_prep_kernel, count),
+        functools.partial(src_prep_kernel, count, first),
         out_shape=[
             bf16_shape(rows, KF, BS),
             bf16_shape(rows, KS, BS),
             bf16_shape(rows, KD, BS),
             bf16_shape(rows, BS, BS),
-            jax.ShapeDtypeStruct((count, 8, BS), jnp.int32),
+            jax.ShapeDtypeStruct((NYL * TABLE, BS), jnp.int32),
         ],
-        in_specs=[SMEM_SPEC] + [VMEM_SPEC] * count,
+        in_specs=[VMEM_SPEC] * count,
         out_specs=[VMEM_SPEC] * 5,
         name="src_prep",
         compiler_params=PARAMS,
         cost_estimate=pl.CostEstimate(flops=10**6, bytes_accessed=10**6, transcendentals=0),
-    )(me, *packed)
+    )(*packed)
 
 
 def recv_prep(tiles):
@@ -290,31 +302,30 @@
     )(tiles)
 
 
-def sweep(my_y, distances, recv, src, count, *before, sizes=None):
-    *src, lists = src
+def sweep(place, distances, recv, src, count, whole, *before, sizes=None):
+    *src, table = src
     blocks = len(distances) * NZ
     sizes = sizes or (blocks,)
     return pl.pallas_call(
-        functools.partial(sweep_kernel, count, distances, len(before), sizes),
+        functools.partial(sweep_kernel, count, whole, distances, len(before), sizes),
         out_shape=[jax.ShapeDtypeStruct((size, BS, BS), jnp.float32) for size in sizes],
         in_specs=[SMEM_SPEC] * 2 + [VMEM_SPEC] * (7 + len(before)),
         out_specs=[VMEM_SPEC] * len(sizes),
         scratch_shapes=[
             pltpu.VMEM((blocks, BS, BS), jnp.float32),
-            pltpu.SMEM((blocks * count * CAP + 4 * UNROLL,), jnp.int32),
-            pltpu.SMEM((blocks * count * CAP // 2 + count * CAP + 2 * UNROLL,), jnp.int32),
+            pltpu.SMEM((blocks * count * CAP // 2 + count * CAP + UNROLL,), jnp.int32),
         ],
         name="sweep",
         compiler_params=PARAMS,
         cost_estimate=pl.CostEstimate(flops=10**6, bytes_accessed=10**6, transcendentals=0),
-    )(my_y, lists, *recv, *src, *before)
+    )(place, table, *recv, *src, *before)
 
 
 def pack(*operands):
     return pl.pallas_call(
         pack_kernel,
         out_shape=[
-            jax.ShapeDtypeStruct((FLUX + SB * TILE, BS), jnp.float32),
+            jax.ShapeDtypeStruct((LISTS + TILE, BS), jnp.float32),
             jax.ShapeDtypeStruct((NJ, 8, BS), jnp.float32),
         ],
         in_specs=[VMEM_SPEC] * 9,
@@ -362,29 +373,33 @@
     def other_core(block):
         return lax.ppermute(block, "c", [(0, 1), (1, 0)])
 
-    me = (lax.axis_index("x") * NC + lax.axis_index("c")).astype(jnp.int32).reshape(1)
-    my_y = (lax.axis_index("yh") * NYL + lax.axis_index("yl")).astype(jnp.int32).reshape(1)
+    my_y = lax.axis_index("yh") * NYL + lax.axis_index("yl")
+    place = jnp.stack([my_y, lax.axis_index("x") * NC + lax.axis_index("c")]).astype(jnp.int32)
     far = [along_x(mine, distance) for distance in (1, 3, 2)]
     own = other_core(mine)
 
     tiles = lax.all_to_all(recv_tile, ("yl", "yh", "z"), 0, 0, tiled=True)
 
     own, tiles = lax.optimization_barrier((own, tiles))
-    recv = recv_prep(tiles)
-    (begun,) = sweep(my_y, (1, 2, 3), recv, src_prep(me, [mine, own]), 2)
-    *far, begun = lax.optimization_barrier((*far, begun))
-    src = src_prep(me, far + [other_core(block) for block in far] + [mine, own])
+    recv = list(recv_prep(tiles))
+    left, right, recv[0] = lax.optimization_barrier((far[0], far[1], recv[0]))
+    sides = [left, right, other_core(left), other_core(right)]
+    near = list(src_prep([mine, own], 0))
+    sides[2], sides[3], near[0] = lax.optimization_barrier((sides[2], sides[3], near[0]))
+    (begun,) = sweep(place, (1, 2, 3), recv, near, 2, True)
+    opposite, begun = lax.optimization_barrier((far[2], begun))
+    src = src_prep(sides + [opposite, other_core(opposite), mine, own], GROUP - 2)
 
     def along_y(block, distance):
         return lax.ppermute(block, ("yl", "yh"), y_route(distance))
 
     half = NZ // 2
-    parts = sweep(my_y, (2,), recv, src, GROUP - 2, begun, sizes=(half, half))
+    parts = sweep(place, (2,), recv, src, GROUP - 2, False, begun, sizes=(half, half))
     by_left, by_right = along_y(parts[0], 1), along_y(parts[1], 3)
-    ahead, behind = sweep(my_y, (1, 3), recv, src, GROUP - 2, begun, sizes=(NZ, NZ))
+    ahead, behind = sweep(place, (1, 3), recv, src, GROUP - 2, False, begun, sizes=(NZ, NZ))
     ahead = along_y(ahead.at[:half].add(by_left), 1)
     behind = along_y(behind.at[half:].add(by_right), 3)
-    (total,) = sweep(my_y, (0,), recv, src, GROUP)
+    (total,) = sweep(place, (0,), recv, src, GROUP, True)
     total = total + ahead + behind
     pieces = lax.all_to_all(total, "z", 0, 0, tiled=True)
     return direct + jnp.sum(pieces, axis=0)

time: 104 us -> 109 us (1.048); the launches traced: 104 us -> 108 us
  blocking collectives: 24.5 us -> 41.5 us
  starting transfers between devices: 23.8 us -> 16.4 us
  Pallas kernels: 34.6 us -> 29.7 us
  waiting for transfers between devices: 18.8 us -> 15.8 us
  local copies, waits for them, and re-layouts: 1.06 us -> 2.92 us
    all_to_all x0 -> x1, blocking collectives: none -> 22 us  [shards(): tiles = lax.all_to_all(recv_tile, ('yl', 'yh', 'z'), 0, 0, tiled=True)]
    all_to_all x1 -> x0, starting transfers between devices: 11.5 us -> none  [shards(): tiles = lax.all_to_all(recv_tile, ('yl', 'yh', 'z'), 0, 0, tiled=True)]
    all_to_all x1 -> x0, waiting for transfers between devices: 10.5 us -> none  [shards(): tiles = lax.all_to_all(recv_tile, ('yl', 'yh', 'z'), 0, 0, tiled=True)]
    ppermute x3, waiting for transfers between devices: 0.01 us -> 5.53 us  [along_x(): lax.ppermute(block, 'x', [(i, (i + distance) % NX) for i in range(NX)])]
    ppermute x4, starting transfers between devices: 6.97 us -> 12.4 us  [along_y(): return lax.ppermute(block, ('yl', 'yh'), y_route(distance))]
    all_to_all x1, blocking collectives: 24.5 us -> 19.5 us  [shards(): pieces = lax.all_to_all(total, 'z', 0, 0, tiled=True)]
    pallas_call x7, Pallas kernels: 33.5 us -> 28.6 us  [the longest x4 23.5 us: sweep(): pl.pallas_call(functools.partial(sweep_kernel, count, whole, distances, l...]
    ppermute x4, waiting for transfers between devices: 5.2 us -> 8.1 us  [along_y(): return lax.ppermute(block, ('yl', 'yh'), y_route(distance))]
  transfers between devices with their start and end apart: 12 -> 11, of which waited for: 6 -> 4; matrix products, arithmetic and copies ran while one was open for 0% -> 0% of each run, Pallas kernels for 25% -> 20%
where the time goes in v7:
time: 109 us; the launch traced here: 108 us
  blocking collectives  41.5 us (38%)
  Pallas kernels  29.7 us (27%)
  starting transfers between devices  16.4 us (15%)
  waiting for transfers between devices  15.8 us (14%)
  local copies, waits for them, and re-layouts  2.92 us (3%)
    pallas_call x4, Pallas kernels, sweep(): pl.pallas_call(functools.partial(sweep_kernel, count, whole, distances, l...  23.5 us
    all_to_all x1, blocking collectives, shards(): tiles = lax.all_to_all(recv_tile, ('yl', 'yh', 'z'), 0, 0, tiled=True)  22 us
    all_to_all x1, blocking collectives, shards(): pieces = lax.all_to_all(total, 'z', 0, 0, tiled=True)  19.5 us
    ppermute x4, starting transfers between devices, along_y(): return lax.ppermute(block, ('yl', 'yh'), y_route(distance))  12.4 us
    ppermute x4, waiting for transfers between devices, along_y(): return lax.ppermute(block, ('yl', 'yh'), y_route(distance))  8.1 us
    ppermute x3, waiting for transfers between devices, along_x(): lax.ppermute(block, 'x', [(i, (i + distance) % NX) for i in range(NX)])  5.53 us
    ppermute x3, starting transfers between devices, along_x(): lax.ppermute(block, 'x', [(i, (i + distance) % NX) for i in range(NX)])  3.42 us
    pallas_call x2, Pallas kernels, src_prep(): pl.pallas_call(functools.partial(src_prep_kernel, count, first), out_shap...  3.17 us
  transfers between devices with their start and end apart: 11, of which 4 were waited for; matrix products, arithmetic and copies ran while one was open for 0% of the time, Pallas kernels for 20%

profile of v7, /device:TPU:6, one launch (start us, length us, event | category | flops | bytes accessed | tf_op | source)
XLA Modules:
  0.0 107.5 jit_solution(8308054367814098983)
XLA Ops:
  0.0 2.0 %pack.1 = (f32[1096,128]{1,0:T(8,128)}, f32[32,8,128]{2,1,0:T(8,128)}) custom-call(bf16[1024,128]{1,0:T(8,128)(2,1)} %incident.1, f32[3,1024]{1,0:T(4,128)} %pos.1, f32[2,1024]{1,0:T(2,128)} %angles.1, f32[1,1024]{1,0:T(1,128)} %bitcast.10, f32[1,1024]{1,0:T(1,128)} %bitcast.11, s32[16,4,16]{2,1,0:T(4,128)} %bitcast.8, s32[16,16]{1,0:T(8,128)} %bitcast.9, ...), custom_call_target="tpu_custom_call" | custom-call | flops 1000000 | bytes 1000000 | tf_op jit(solution)/shard_map/pack/pallas_call | solution.py:325
  2.0 0.0 collective-permute-start.2
  2.0 0.8 collective-permute-start.1
  2.8 2.4 %collective-permute-start = (f32[1096,128]{1,0:T(8,128)}, f32[1096,128]{1,0:T(8,128)}, u32[]{:S(2)}, u32[]{:S(2)}) collective-permute-start(f32[1096,128]{1,0:T(8,128)} %get-tuple-element.58.refs_0_.refs_6_), channel_id=1, source_target_pairs={{0,64},{64,128},{128,192},{192,0},{1,65},{65,129},{129,193},{193,1... | collective-permute-start | bytes 1683464 | tf_op jit(solution)/shard_map/ppermute | solution.py:371
  5.2 22.0 %all_to_all.10.tiles = f32[32,8,128]{2,1,0:T(8,128)S(1)} all-to-all(f32[32,8,128]{2,1,0:T(8,128)} %get-tuple-element.59), channel_id=1, replica_groups=mesh['x'=4,'yl'=2,'c'=2,'yh'=2,'z'=8] {'yl','yh','z'}, dimensions={0} | all-to-all | bytes 262144 | tf_op jit(solution)/shard_map/all_to_all | solution.py:381
  27.3 0.8 copy-done.1
  28.1 1.1 recv_prep.1
  29.2 0.1 collective-permute-start.3
  29.3 0.5 collective-permute-start.4
  29.8 0.2 collective-permute-start.5
  29.9 0.1 pad_add_fusion.place
  30.0 1.1 copy-done
  31.1 1.1 copy-done.2
  32.1 0.4 src_prep.2
  32.6 8.2 %sweep.4.refs_0_ = f32[24,128,128]{2,1,0:T(8,128)S(1)} custom-call(s32[2]{0:T(128)S(1)} %pad_add_fusion.place, s32[80,128]{1,0:T(8,128)S(1)} %get-tuple-element.68.table, bf16[32,128,32]{2,1,0:T(8,128)(2,1)S(1)} %get-tuple-element.69.rf, bf16[32,128,32]{2,1,0:T(8,128)(2,1)S(1)} %get-tuple-element.70.rs, bf16[32,128,48]{2,1,0:T(8,128)(2,1)S(1)} %get-tuple-element.71.rd, ...), custom_call_target="tpu_custom_call" | custom-call | flops 1000000 | bytes 1000000 | tf_op jit(solution)/shard_map/sweep/pallas_call | solution.py:309
  40.8 5.5 %collective-permute-done.5.refs_4_ = f32[1096,128]{1,0:T(8,128)} collective-permute-done((f32[1096,128]{1,0:T(8,128)}, f32[1096,128]{1,0:T(8,128)}, u32[]{:S(2)}, u32[]{:S(2)}) %collective-permute-start.5) | collective-permute-done | bytes 561184 | tf_op jit(solution)/shard_map/ppermute | solution.py:371
  46.3 2.2 %collective-permute-done.6.refs_5_ = f32[1096,128]{1,0:T(8,128)S(1)} collective-permute-done((f32[1096,128]{1,0:T(8,128)}, f32[1096,128]{1,0:T(8,128)S(1)}, u32[]{:S(2)}, u32[]{:S(2)}) %collective-permute-start.6) | collective-permute-done | bytes 561184 | tf_op jit(solution)/shard_map/ppermute | solution.py:374
  48.5 2.8 %src_prep.3 = (bf16[65,32,128]{2,1,0:T(8,128)(2,1)S(1)}, bf16[65,32,128]{2,1,0:T(8,128)(2,1)S(1)}, bf16[65,48,128]{2,1,0:T(8,128)(2,1)S(1)}, bf16[65,128,128]{2,1,0:T(8,128)(2,1)S(1)}, s32[80,128]{1,0:T(8,128)S(1)}) custom-call(f32[1096,128]{1,0:T(8,128)} %collective-permute-done.refs_0_, f32[1096,128]{1,0:T(8,128)} %collective-permute-done.1.refs_1_, ...), custom_call_target="tpu_custom_call" | custom-call | flops 1000000 | bytes 1000000 | tf_op jit(solution)/shard_map/src_prep/pallas_call | solution.py:276
  51.2 3.5 %sweep.7 = (f32[4,128,128]{2,1,0:T(8,128)S(1)}, f32[4,128,128]{2,1,0:T(8,128)S(1)}) custom-call(s32[2]{0:T(128)S(1)} %pad_add_fusion.place, s32[80,128]{1,0:T(8,128)S(1)} %get-tuple-element.77.table, bf16[32,128,32]{2,1,0:T(8,128)(2,1)S(1)} %get-tuple-element.69.rf, bf16[32,128,32]{2,1,0:T(8,128)(2,1)S(1)} %get-tuple-element.70.rs, ...), custom_call_target="tpu_custom_call" | custom-call | flops 1000000 | bytes 1000000 | tf_op jit(solution)/shard_map/sweep/pallas_call | solution.py:309
  54.8 4.4 %collective-permute-start.9 = (f32[4,128,128]{2,1,0:T(8,128)S(1)}, f32[4,128,128]{2,1,0:T(8,128)S(1)}, u32[]{:S(2)}, u32[]{:S(2)}) collective-permute-start(f32[4,128,128]{2,1,0:T(8,128)S(1)} %get-tuple-element.86), channel_id=1, source_target_pairs={{0,40},{32,0},{8,32},{40,8},{1,41},{33,1},{9,33},{41,9},{2,42},{34... | collective-permute-start | bytes 786440 | tf_op jit(solution)/shard_map/ppermute | solution.py:394
  59.2 6.3 %sweep.6 = (f32[8,128,128]{2,1,0:T(8,128)S(1)}, f32[8,128,128]{2,1,0:T(8,128)S(1)}) custom-call(s32[2]{0:T(128)S(1)} %pad_add_fusion.place, s32[80,128]{1,0:T(8,128)S(1)} %get-tuple-element.77.table, bf16[32,128,32]{2,1,0:T(8,128)(2,1)S(1)} %get-tuple-element.69.rf, bf16[32,128,32]{2,1,0:T(8,128)(2,1)S(1)} %get-tuple-element.70.rs, ...), custom_call_target="tpu_custom_call" | custom-call | flops 1000000 | bytes 1000000 | tf_op jit(solution)/shard_map/sweep/pallas_call | solution.py:309
  65.5 0.1 add_dynamic-update-slice_fusion
  65.6 7.9 %collective-permute-start.10 = (f32[8,128,128]{2,1,0:T(8,128)S(1)}, f32[8,128,128]{2,1,0:T(8,128)S(1)}, u32[]{:S(2)}, u32[]{:S(2)}) collective-permute-start(f32[8,128,128]{2,1,0:T(8,128)S(1)} %add_dynamic-update-slice_fusion), channel_id=1, source_target_pairs={{0,40},{32,0},{8,32},{40,8},{1,41},{33,1},{9,33},{41,9},{2,42},{34... | collective-permute-start | bytes 1572872 | tf_op jit(solution)/shard_map/ppermute | solution.py:394
  73.5 0.1 add_dynamic-update-slice_fusion.1
  73.5 0.1 collective-permute-start.8
  73.6 5.5 %sweep.5 = f32[8,128,128]{2,1,0:T(8,128)S(1)} custom-call(s32[2]{0:T(128)S(1)} %pad_add_fusion.place, s32[80,128]{1,0:T(8,128)S(1)} %get-tuple-element.77.table, bf16[32,128,32]{2,1,0:T(8,128)(2,1)S(1)} %get-tuple-element.69.rf, bf16[32,128,32]{2,1,0:T(8,128)(2,1)S(1)} %get-tuple-element.70.rs, bf16[32,128,48]{2,1,0:T(8,128)(2,1)S(1)} %get-tuple-element.71.rd, ...), custom_call_target="tpu_custom_call" | custom-call | flops 1000000 | bytes 1000000 | tf_op jit(solution)/shard_map/sweep/pallas_call | solution.py:309
  79.1 0.0 copy-start.4
  79.1 4.5 %collective-permute-done.10 = f32[8,128,128]{2,1,0:T(8,128)S(1)} collective-permute-done((f32[8,128,128]{2,1,0:T(8,128)S(1)}, f32[8,128,128]{2,1,0:T(8,128)S(1)}, u32[]{:S(2)}, u32[]{:S(2)}) %collective-permute-start.10) | collective-permute-done | bytes 524320 | tf_op jit(solution)/shard_map/ppermute | solution.py:394
  83.7 3.6 %collective-permute-done.8 = f32[8,128,128]{2,1,0:T(8,128)S(1)} collective-permute-done((f32[8,128,128]{2,1,0:T(8,128)S(1)}, f32[8,128,128]{2,1,0:T(8,128)S(1)}, u32[]{:S(2)}, u32[]{:S(2)}) %collective-permute-start.8) | collective-permute-done | bytes 524320 | tf_op jit(solution)/shard_map/ppermute | solution.py:394
  87.2 0.1 add_add_fusion
  87.3 19.5 %all_to_all.11 = f32[8,128,128]{2,1,0:T(8,128)S(1)} all-to-all(f32[8,128,128]{2,1,0:T(8,128)S(1)} %add_add_fusion), channel_id=1, replica_groups=mesh['x'=4,'yl'=2,'c'=2,'yh'=2,'z'=8] {'z'}, dimensions={0} | all-to-all | bytes 1048576 | tf_op jit(solution)/shard_map/all_to_all | solution.py:404
  106.9 0.6 add.35
  (16 shorter events, 0.1 us)
Async XLA Ops:
  2.0 25.3 %collective-permute-start.2 = (f32[1096,128]{1,0:T(8,128)}, f32[1096,128]{1,0:T(8,128)S(1)}, u32[]{:S(2)}, u32[]{:S(2)}) collective-permute-start(f32[1096,128]{1,0:T(8,128)} %get-tuple-element.58.refs_0_.refs_6_), channel_id=1, source_target_pairs={{0,16},{16,0},{1,17},{17,1},{2,18},{18,2},{3,19},{19,3},{4,20},{20... | collective-permute-start | bytes 1683464 | tf_op jit(solution)/shard_map/ppermute | solution.py:374
  2.0 27.1 %collective-permute-start.1 = (f32[1096,128]{1,0:T(8,128)}, f32[1096,128]{1,0:T(8,128)}, u32[]{:S(2)}, u32[]{:S(2)}) collective-permute-start(f32[1096,128]{1,0:T(8,128)} %get-tuple-element.58.refs_0_.refs_6_), channel_id=1, source_target_pairs={{0,192},{64,0},{128,64},{192,128},{1,193},{65,1},{129,65},{193,129... | collective-permute-start | bytes 1683464 | tf_op jit(solution)/shard_map/ppermute | solution.py:371
  2.8 26.3 %collective-permute-start = (f32[1096,128]{1,0:T(8,128)}, f32[1096,128]{1,0:T(8,128)}, u32[]{:S(2)}, u32[]{:S(2)}) collective-permute-start(f32[1096,128]{1,0:T(8,128)} %get-tuple-element.58.refs_0_.refs_6_), channel_id=1, source_target_pairs={{0,64},{64,128},{128,192},{192,0},{1,65},{65,129},{129,193},{193,1... | collective-permute-start | bytes 1683464 | tf_op jit(solution)/shard_map/ppermute | solution.py:371
  27.3 0.8 copy-start.1
  29.2 3.4 %collective-permute-start.3 = (f32[1096,128]{1,0:T(8,128)}, f32[1096,128]{1,0:T(8,128)}, u32[]{:S(2)}, u32[]{:S(2)}) collective-permute-start(f32[1096,128]{1,0:T(8,128)} %collective-permute-done.refs_0_), channel_id=1, source_target_pairs={{0,16},{16,0},{1,17},{17,1},{2,18},{18,2},{3,19},{19,3},{4,20},{20... | collective-permute-start | bytes 1683464 | tf_op jit(solution)/shard_map/ppermute | solution.py:374
  29.3 3.3 %collective-permute-start.4 = (f32[1096,128]{1,0:T(8,128)}, f32[1096,128]{1,0:T(8,128)}, u32[]{:S(2)}, u32[]{:S(2)}) collective-permute-start(f32[1096,128]{1,0:T(8,128)} %collective-permute-done.1.refs_1_), channel_id=1, source_target_pairs={{0,16},{16,0},{1,17},{17,1},{2,18},{18,2},{3,19},{19,3},{4,20},{20... | collective-permute-start | bytes 1683464 | tf_op jit(solution)/shard_map/ppermute | solution.py:374
  29.8 16.5 %collective-permute-start.5 = (f32[1096,128]{1,0:T(8,128)}, f32[1096,128]{1,0:T(8,128)}, u32[]{:S(2)}, u32[]{:S(2)}) collective-permute-start(f32[1096,128]{1,0:T(8,128)} %get-tuple-element.58.refs_0_.refs_6_), channel_id=1, source_target_pairs={{0,128},{64,192},{128,0},{192,64},{1,129},{65,193},{129,1},{193,65... | collective-permute-start | bytes 1683464 | tf_op jit(solution)/shard_map/ppermute | solution.py:371
  30.0 1.1 copy-start
  31.1 1.1 copy-start.2
  32.5 15.9 %copy-start.3 = (f32[1096,128]{1,0:T(8,128)S(1)}, f32[1096,128]{1,0:T(8,128)}, u32[]{:S(2)}) copy-start(f32[1096,128]{1,0:T(8,128)} %copy-done.1) | copy-start | bytes 1683460
  46.3 2.2 %collective-permute-start.6 = (f32[1096,128]{1,0:T(8,128)}, f32[1096,128]{1,0:T(8,128)S(1)}, u32[]{:S(2)}, u32[]{:S(2)}) collective-permute-start(f32[1096,128]{1,0:T(8,128)} %collective-permute-done.5.refs_4_), channel_id=1, source_target_pairs={{0,16},{16,0},{1,17},{17,1},{2,18},{18,2},{3,19},{19,3},{4,20},{20... | collective-permute-start | bytes 1683464 | tf_op jit(solution)/shard_map/ppermute | solution.py:374
  54.8 10.8 %collective-permute-start.9 = (f32[4,128,128]{2,1,0:T(8,128)S(1)}, f32[4,128,128]{2,1,0:T(8,128)S(1)}, u32[]{:S(2)}, u32[]{:S(2)}) collective-permute-start(f32[4,128,128]{2,1,0:T(8,128)S(1)} %get-tuple-element.86), channel_id=1, source_target_pairs={{0,40},{32,0},{8,32},{40,8},{1,41},{33,1},{9,33},{41,9},{2,42},{34... | collective-permute-start | bytes 786440 | tf_op jit(solution)/shard_map/ppermute | solution.py:394
  59.2 14.2 %collective-permute-start.7 = (f32[4,128,128]{2,1,0:T(8,128)S(1)}, f32[4,128,128]{2,1,0:T(8,128)S(1)}, u32[]{:S(2)}, u32[]{:S(2)}) collective-permute-start(f32[4,128,128]{2,1,0:T(8,128)S(1)} %get-tuple-element.84), channel_id=1, source_target_pairs={{0,32},{32,8},{8,40},{40,0},{1,33},{33,9},{9,41},{41,1},{2,34},{34... | collective-permute-start | bytes 786440 | tf_op jit(solution)/shard_map/ppermute | solution.py:394
  65.6 18.1 %collective-permute-start.10 = (f32[8,128,128]{2,1,0:T(8,128)S(1)}, f32[8,128,128]{2,1,0:T(8,128)S(1)}, u32[]{:S(2)}, u32[]{:S(2)}) collective-permute-start(f32[8,128,128]{2,1,0:T(8,128)S(1)} %add_dynamic-update-slice_fusion), channel_id=1, source_target_pairs={{0,40},{32,0},{8,32},{40,8},{1,41},{33,1},{9,33},{41,9},{2,42},{34... | collective-permute-start | bytes 1572872 | tf_op jit(solution)/shard_map/ppermute | solution.py:394
  73.5 13.7 %collective-permute-start.8 = (f32[8,128,128]{2,1,0:T(8,128)S(1)}, f32[8,128,128]{2,1,0:T(8,128)S(1)}, u32[]{:S(2)}, u32[]{:S(2)}) collective-permute-start(f32[8,128,128]{2,1,0:T(8,128)S(1)} %add_dynamic-update-slice_fusion.1), channel_id=1, source_target_pairs={{0,32},{32,8},{8,40},{40,0},{1,33},{33,9},{9,41},{41,1},{2,34},{34... | collective-permute-start | bytes 1572872 | tf_op jit(solution)/shard_map/ppermute | solution.py:394
  79.1 27.8 %copy-start.4 = (f32[128,128]{1,0:T(8,128)S(1)}, f32[128,128]{1,0:T(8,128)}, u32[]{:S(2)}) copy-start(f32[128,128]{1,0:T(8,128)} %param.21) | copy-start | bytes 196612

commit v8 on v6

--- a/solution.py
+++ b/solution.py
@@ -17,13 +17,15 @@
 GROUP = NX * NC
 NJ = NY * NZ
 CENTRE = 3.0
-TILE = 16
+TILE = 8
 POS, NRM, AREA = 0, 3, 6
 ROWS, DOT, SQA, SQB, ONE = 16, 8, 9, 10, 11
 KF, KS, KD = 32, 32, 48
 VMEM_LIMIT = 16 << 20
-UNROLL, TAIL = 16, 8
+UNROLL, TAIL = 32, 8
 FLUX = SB * BS
+LISTS = FLUX + SB * TILE
+LANES = NYH * NZ
 
 
 def contraction_terms():
@@ -109,25 +111,33 @@
     return [across * jnp.cos(azimuth), across * jnp.sin(azimuth), jnp.cos(polar)]
 
 
-def pack_kernel(
-    incident, pos, angles, area, keep, lists, counts, recv_pos, recv_angles, packed, recv_tile
-):
+def pack_kernel(*refs):
+    given, (packed, recv_tile), held, arrival = refs[:9], refs[9:11], refs[11:20], refs[20]
+    copies = [
+        pltpu.make_async_copy(source, target, arrival.at[at])
+        for at, (source, target) in enumerate(zip(given, held))
+    ]
+    for copy in copies:
+        copy.start()
+    for copy in copies:
+        copy.wait()
+    incident, pos, angles, area, keep, lists, counts, recv_pos, recv_angles = held
     packed[:FLUX, :] = incident[...].astype(jnp.float32)
-    packed[FLUX:, :] = jnp.zeros((SB * TILE, BS), jnp.float32)
     scale = keep[...] * area[...] * (1.0 / np.pi)
     rows = [pos[a : a + 1, :] - CENTRE for a in range(3)]
     rows += [component * scale for component in direction(angles[...])]
     rows += [area[...], jnp.zeros_like(scale)]
     tile = jnp.concatenate(rows, axis=0)
-    slot = lax.broadcasted_iota(jnp.int32, (CAP, NYH * NZ), 0)
+    slot = lax.broadcasted_iota(jnp.int32, (CAP, LANES), 0)
     for k in range(SB):
-        at = FLUX + k * TILE
-        packed[at : at + 8, :] = tile[:, k * BS : (k + 1) * BS]
+        packed[FLUX + k * TILE : FLUX + (k + 1) * TILE, :] = tile[:, k * BS : (k + 1) * BS]
+    for k in range(GROUP):
         for yl in range(NYL):
             slab = ((k // NC) * NYL + yl) * NC + k % NC
             live = slot < counts[slab : slab + 1, :]
             marked = jnp.where(live, lists[slab], -1).astype(jnp.float32)
-            packed[at + 8 + yl * CAP : at + 8 + (yl + 1) * CAP, : NYH * NZ] = marked
+            rows = slice(LISTS + yl * CAP, LISTS + (yl + 1) * CAP)
+            packed[rows, k * LANES : (k + 1) * LANES] = marked
     rows = [recv_pos[a : a + 1, :] - CENTRE for a in range(3)]
     rows += direction(recv_angles[...])
     rows += [jnp.zeros((2, BS), jnp.float32)]
@@ -136,17 +146,16 @@
         recv_tile[j] = tile
 
 
-def src_prep_kernel(count, me, *refs):
+def src_prep_kernel(count, *refs):
     packed = refs[:count]
     sf, ss, sd, em, lists = refs[count:]
     mats = selections(1)
     for d, ref in enumerate(packed):
         for k in range(SB):
             em[d * SB + k] = ref[k * BS : (k + 1) * BS, :].astype(jnp.bfloat16)
-        tiles = [ref[FLUX + k * TILE : FLUX + k * TILE + 8, :] for k in range(SB)]
+        tiles = [ref[FLUX + k * TILE : FLUX + (k + 1) * TILE, :] for k in range(SB)]
         q = split_pieces(jnp.concatenate(tiles, axis=1))
-        list_at = pl.multiple_of(FLUX + me[0] * TILE + 8, 8)
-        lists[d] = ref[pl.ds(list_at, 8), :].astype(jnp.int32)
+        lists[d] = ref[LISTS : LISTS + TILE, :].astype(jnp.int32)
         for m, out in zip(mats, (sf, ss, sd)):
             values = dot(m, q).astype(jnp.bfloat16)
             for k in range(SB):
@@ -169,7 +178,7 @@
             ).astype(jnp.bfloat16)
 
 
-def sweep_kernel(count, distances, added, sizes, my_y, lists, rf, rs, rd, sf, ss, sd, em, *refs):
+def sweep_kernel(count, distances, added, sizes, place, lists, rf, rs, rd, sf, ss, sd, em, *refs):
     before, outs = refs[:added], refs[added:-3]
     out, ids, owner = refs[-3:]
     blocks = len(distances) * NZ
@@ -180,7 +189,7 @@
         ahead = distances[0]
         for at in range(1, len(distances)):
             ahead = jnp.where(j >= at * NZ, distances[at], ahead)
-        target = (my_y[0] + ahead) & (NY - 1)
+        target = (place[0] + ahead) & (NY - 1)
         return ((target & (NYL - 1)) * NYH + (target >> 1)) * NZ + (j & (NZ - 1))
 
     for j in range(blocks):
@@ -192,7 +201,7 @@
     def one_block(j, n):
         block = block_of(j)
         row = (block >> 4) * CAP
-        lane = block & (NYH * NZ - 1)
+        lane = place[1] * LANES + (block & (LANES - 1))
         for t in range(slots):
             owner[n // 2 + t] = j
         for d in range(count):
@@ -258,7 +267,7 @@
     return jax.ShapeDtypeStruct(shape, BF16)
 
 
-def src_prep(me, packed):
+def src_prep(packed):
     count = len(packed)
     rows = count * SB + 1
     return pl.pallas_call(
@@ -270,12 +279,12 @@
             bf16_shape(rows, BS, BS),
             jax.ShapeDtypeStruct((count, 8, BS), jnp.int32),
         ],
-        in_specs=[SMEM_SPEC] + [VMEM_SPEC] * count,
+        in_specs=[VMEM_SPEC] * count,
         out_specs=[VMEM_SPEC] * 5,
         name="src_prep",
         compiler_params=PARAMS,
         cost_estimate=pl.CostEstimate(flops=10**6, bytes_accessed=10**6, transcendentals=0),
-    )(me, *packed)
+    )(*packed)
 
 
 def recv_prep(tiles):
@@ -290,7 +299,7 @@
     )(tiles)
 
 
-def sweep(my_y, distances, recv, src, count, *before, sizes=None):
+def sweep(place, distances, recv, src, count, *before, sizes=None):
     *src, lists = src
     blocks = len(distances) * NZ
     sizes = sizes or (blocks,)
@@ -307,22 +316,24 @@
         name="sweep",
         compiler_params=PARAMS,
         cost_estimate=pl.CostEstimate(flops=10**6, bytes_accessed=10**6, transcendentals=0),
-    )(my_y, lists, *recv, *src, *before)
+    )(place, lists, *recv, *src, *before)
 
 
 def pack(*operands):
     return pl.pallas_call(
         pack_kernel,
         out_shape=[
-            jax.ShapeDtypeStruct((FLUX + SB * TILE, BS), jnp.float32),
+            jax.ShapeDtypeStruct((LISTS + TILE, BS), jnp.float32),
             jax.ShapeDtypeStruct((NJ, 8, BS), jnp.float32),
         ],
-        in_specs=[VMEM_SPEC] * 9,
+        in_specs=[pl.BlockSpec(memory_space=pltpu.HBM)] * 9,
         out_specs=[VMEM_SPEC] * 2,
+        scratch_shapes=[pltpu.VMEM(array.shape, array.dtype) for array in operands]
+        + [pltpu.SemaphoreType.DMA((9,))],
         name="pack",
-        compiler_params=pltpu.CompilerParams(vmem_limit_bytes=60 << 20),
+        compiler_params=PARAMS,
         cost_estimate=pl.CostEstimate(flops=10**6, bytes_accessed=10**6, transcendentals=0),
-    )(*operands)
+    )(*[pltpu.with_memory_space_constraint(array, pltpu.HBM) for array in operands])
 
 
 def y_route(distance):
@@ -362,8 +373,8 @@
     def other_core(block):
         return lax.ppermute(block, "c", [(0, 1), (1, 0)])
 
-    me = (lax.axis_index("x") * NC + lax.axis_index("c")).astype(jnp.int32).reshape(1)
-    my_y = (lax.axis_index("yh") * NYL + lax.axis_index("yl")).astype(jnp.int32).reshape(1)
+    my_y = lax.axis_index("yh") * NYL + lax.axis_index("yl")
+    place = jnp.stack([my_y, lax.axis_index("x") * NC + lax.axis_index("c")]).astype(jnp.int32)
     far = [along_x(mine, distance) for distance in (1, 3, 2)]
     own = other_core(mine)
 
@@ -371,20 +382,20 @@
 
     own, tiles = lax.optimization_barrier((own, tiles))
     recv = recv_prep(tiles)
-    (begun,) = sweep(my_y, (1, 2, 3), recv, src_prep(me, [mine, own]), 2)
+    (begun,) = sweep(place, (1, 2, 3), recv, src_prep([mine, own]), 2)
     *far, begun = lax.optimization_barrier((*far, begun))
-    src = src_prep(me, far + [other_core(block) for block in far] + [mine, own])
+    src = src_prep(far + [other_core(block) for block in far] + [mine, own])
 
     def along_y(block, distance):
         return lax.ppermute(block, ("yl", "yh"), y_route(distance))
 
     half = NZ // 2
-    parts = sweep(my_y, (2,), recv, src, GROUP - 2, begun, sizes=(half, half))
+    parts = sweep(place, (2,), recv, src, GROUP - 2, begun, sizes=(half, half))
     by_left, by_right = along_y(parts[0], 1), along_y(parts[1], 3)
-    ahead, behind = sweep(my_y, (1, 3), recv, src, GROUP - 2, begun, sizes=(NZ, NZ))
+    ahead, behind = sweep(place, (1, 3), recv, src, GROUP - 2, begun, sizes=(NZ, NZ))
     ahead = along_y(ahead.at[:half].add(by_left), 1)
     behind = along_y(behind.at[half:].add(by_right), 3)
-    (total,) = sweep(my_y, (0,), recv, src, GROUP)
+    (total,) = sweep(place, (0,), recv, src, GROUP)
     total = total + ahead + behind
     pieces = lax.all_to_all(total, "z", 0, 0, tiled=True)
     return direct + jnp.sum(pieces, axis=0)

time: 104 us -> 102 us (0.981); the launches traced: 104 us -> 101 us
  waiting for transfers between devices: 18.8 us -> 22.6 us
  blocking collectives: 24.5 us -> 21.9 us
  starting transfers between devices: 23.8 us -> 21.5 us
  Pallas kernels: 34.6 us -> 33.4 us
  local copies, waits for them, and re-layouts: 1.06 us -> 0.01 us
    ppermute x4, waiting for transfers between devices: 5.2 us -> 9.19 us  [along_y(): return lax.ppermute(block, ('yl', 'yh'), y_route(distance))]
    all_to_all x1, blocking collectives: 24.5 us -> 21.9 us  [shards(): pieces = lax.all_to_all(total, 'z', 0, 0, tiled=True)]
    ppermute x4, starting transfers between devices: 6.97 us -> 4.49 us  [along_y(): return lax.ppermute(block, ('yl', 'yh'), y_route(distance))]
    unnamed x4 -> x2, local copies, waits for them, and re-layouts: 1.06 us -> 0.01 us
where the time goes in v8:
time: 102 us; the launch traced here: 101 us
  Pallas kernels  33.4 us (33%)
  waiting for transfers between devices  22.6 us (22%)
  blocking collectives  21.9 us (21%)
  starting transfers between devices  21.5 us (21%)
    pallas_call x4, Pallas kernels, sweep(): pl.pallas_call(functools.partial(sweep_kernel, count, distances, len(befo...  29.3 us
    all_to_all x1, blocking collectives, shards(): pieces = lax.all_to_all(total, 'z', 0, 0, tiled=True)  21.9 us
    all_to_all x1, starting transfers between devices, shards(): tiles = lax.all_to_all(recv_tile, ('yl', 'yh', 'z'), 0, 0, tiled=True)  11.5 us
    all_to_all x1, waiting for transfers between devices, shards(): tiles = lax.all_to_all(recv_tile, ('yl', 'yh', 'z'), 0, 0, tiled=True)  10.4 us
    ppermute x4, waiting for transfers between devices, along_y(): return lax.ppermute(block, ('yl', 'yh'), y_route(distance))  9.19 us
    ppermute x3, starting transfers between devices, along_x(): lax.ppermute(block, 'x', [(i, (i + distance) % NX) for i in range(NX)])  4.73 us
    ppermute x4, starting transfers between devices, along_y(): return lax.ppermute(block, ('yl', 'yh'), y_route(distance))  4.49 us
    ppermute x4, waiting for transfers between devices, other_core(): return lax.ppermute(block, 'c', [(0, 1), (1, 0)])  2.96 us
  transfers between devices with their start and end apart: 12, of which 6 were waited for; matrix products, arithmetic and copies ran while one was open for 0% of the time, Pallas kernels for 25%

profile of v8, /device:TPU:6, one launch (start us, length us, event | category | flops | bytes accessed | tf_op | source)
XLA Modules:
  0.0 100.5 jit_solution(1217995173243760726)
XLA Ops:
  0.0 1.8 %pack.1 = (f32[1096,128]{1,0:T(8,128)S(1)}, f32[32,8,128]{2,1,0:T(8,128)}) custom-call(bf16[1024,128]{1,0:T(8,128)(2,1)} %refs_0_.1, f32[3,1024]{1,0:T(4,128)} %refs_1_.1, f32[2,1024]{1,0:T(2,128)} %refs_2_.1, f32[1,1024]{1,0:T(1,128)} %bitcast.10, f32[1,1024]{1,0:T(1,128)} %bitcast.11, s32[16,4,16]{2,1,0:T(4,128)} %bitcast.8, s32[16,16]{1,0:T(8,128)} %bitcast.9, ...), custom_call_target="tpu_custom_call" | custom-call | flops 1000000 | bytes 1000000 | tf_op jit(solution)/shard_map/pack/pallas_call | solution.py:323
  1.8 0.1 collective-permute-start.3
  1.9 1.5 %collective-permute-start.2 = (f32[1096,128]{1,0:T(8,128)S(1)}, f32[1096,128]{1,0:T(8,128)S(1)}, u32[]{:S(2)}, u32[]{:S(2)}) collective-permute-start(f32[1096,128]{1,0:T(8,128)S(1)} %get-tuple-element.54.refs_0_.refs_6_), channel_id=1, source_target_pairs={{0,128},{64,192},{128,0},{192,64},{1,129},{65,193},{129,1},{193,65... | collective-permute-start | bytes 1683464 | tf_op jit(solution)/shard_map/ppermute | solution.py:371
  3.4 1.7 %collective-permute-start.1 = (f32[1096,128]{1,0:T(8,128)S(1)}, f32[1096,128]{1,0:T(8,128)S(1)}, u32[]{:S(2)}, u32[]{:S(2)}) collective-permute-start(f32[1096,128]{1,0:T(8,128)S(1)} %get-tuple-element.54.refs_0_.refs_6_), channel_id=1, source_target_pairs={{0,192},{64,0},{128,64},{192,128},{1,193},{65,1},{129,65},{193,129... | collective-permute-start | bytes 1683464 | tf_op jit(solution)/shard_map/ppermute | solution.py:371
  5.0 1.6 %collective-permute-start = (f32[1096,128]{1,0:T(8,128)S(1)}, f32[1096,128]{1,0:T(8,128)S(1)}, u32[]{:S(2)}, u32[]{:S(2)}) collective-permute-start(f32[1096,128]{1,0:T(8,128)S(1)} %get-tuple-element.54.refs_0_.refs_6_), channel_id=1, source_target_pairs={{0,64},{64,128},{128,192},{192,0},{1,65},{65,129},{129,193},{193,1... | collective-permute-start | bytes 1683464 | tf_op jit(solution)/shard_map/ppermute | solution.py:371
  6.6 11.5 %all-to-all-start = ((f32[32,8,128]{2,1,0:T(8,128)}), f32[32,8,128]{2,1,0:T(8,128)S(1)}, u32[]{:S(2)}, u32[]{:S(2)}) async-start(f32[32,8,128]{2,1,0:T(8,128)} %get-tuple-element.55), calls=%async_computation | async-start | bytes 262144 | tf_op jit(solution)/shard_map/all_to_all | solution.py:381
  18.1 0.1 pad_add_fusion.place
  18.2 10.4 %all-to-all-done.tiles = f32[32,8,128]{2,1,0:T(8,128)S(1)} async-done(((f32[32,8,128]{2,1,0:T(8,128)}), f32[32,8,128]{2,1,0:T(8,128)S(1)}, u32[]{:S(2)}, u32[]{:S(2)}) %all-to-all-start) | async-done | bytes 131104 | tf_op jit(solution)/shard_map/all_to_all | solution.py:381
  28.6 0.4 src_prep.2
  29.0 1.1 %recv_prep.1 = (bf16[32,128,32]{2,1,0:T(8,128)(2,1)S(1)}, bf16[32,128,32]{2,1,0:T(8,128)(2,1)S(1)}, bf16[32,128,48]{2,1,0:T(8,128)(2,1)S(1)}) custom-call(f32[32,8,128]{2,1,0:T(8,128)S(1)} %all-to-all-done.tiles), custom_call_target="tpu_custom_call" | custom-call | flops 1000000 | bytes 1000000 | tf_op jit(solution)/shard_map/recv_prep/pallas_call | solution.py:291
  30.0 7.2 %sweep.4.refs_0_ = f32[24,128,128]{2,1,0:T(8,128)S(1)} custom-call(s32[2]{0:T(128)S(1)} %pad_add_fusion.place, s32[2,8,128]{2,1,0:T(8,128)S(1)} %get-tuple-element.57.lists, bf16[32,128,32]{2,1,0:T(8,128)(2,1)S(1)} %get-tuple-element.59.rf, bf16[32,128,32]{2,1,0:T(8,128)(2,1)S(1)} %get-tuple-element.60.rs, bf16[32,128,48]{2,1,0:T(8,128)(2,1)S(1)} %get-tuple-element.61.rd, ...), custom_call_target="tpu_custom_call" | custom-call | flops 1000000 | bytes 1000000 | tf_op jit(solution)/shard_map/sweep/pallas_call | solution.py:306
  37.3 0.1 collective-permute-start.4
  37.4 0.5 collective-permute-start.5
  37.9 0.1 collective-permute-start.6
  38.0 1.4 %collective-permute-done.4.refs_3_ = f32[1096,128]{1,0:T(8,128)S(1)} collective-permute-done((f32[1096,128]{1,0:T(8,128)S(1)}, f32[1096,128]{1,0:T(8,128)S(1)}, u32[]{:S(2)}, u32[]{:S(2)}) %collective-permute-start.4) | collective-permute-done | bytes 561184 | tf_op jit(solution)/shard_map/ppermute | solution.py:374
  39.4 0.8 collective-permute-done.5.refs_4_
  40.2 0.8 collective-permute-done.6.refs_5_
  41.0 0.8 src_prep.3
  41.8 5.8 %sweep.7 = (f32[4,128,128]{2,1,0:T(8,128)S(1)}, f32[4,128,128]{2,1,0:T(8,128)S(1)}) custom-call(s32[2]{0:T(128)S(1)} %pad_add_fusion.place, s32[8,8,128]{2,1,0:T(8,128)S(1)} %get-tuple-element.69.lists, bf16[32,128,32]{2,1,0:T(8,128)(2,1)S(1)} %get-tuple-element.59.rf, bf16[32,128,32]{2,1,0:T(8,128)(2,1)S(1)} %get-tuple-element.60.rs, ...), custom_call_target="tpu_custom_call" | custom-call | flops 1000000 | bytes 1000000 | tf_op jit(solution)/shard_map/sweep/pallas_call | solution.py:306
  47.7 0.1 collective-permute-start.9
  47.8 2.0 %collective-permute-start.7 = (f32[4,128,128]{2,1,0:T(8,128)S(1)}, f32[4,128,128]{2,1,0:T(8,128)S(1)}, u32[]{:S(2)}, u32[]{:S(2)}) collective-permute-start(f32[4,128,128]{2,1,0:T(8,128)S(1)} %get-tuple-element.76), channel_id=1, source_target_pairs={{0,32},{32,8},{8,40},{40,0},{1,33},{33,9},{9,41},{41,1},{2,34},{34... | collective-permute-start | bytes 786440 | tf_op jit(solution)/shard_map/ppermute | solution.py:390
  49.8 9.5 %sweep.6 = (f32[8,128,128]{2,1,0:T(8,128)S(1)}, f32[8,128,128]{2,1,0:T(8,128)S(1)}) custom-call(s32[2]{0:T(128)S(1)} %pad_add_fusion.place, s32[8,8,128]{2,1,0:T(8,128)S(1)} %get-tuple-element.69.lists, bf16[32,128,32]{2,1,0:T(8,128)(2,1)S(1)} %get-tuple-element.59.rf, bf16[32,128,32]{2,1,0:T(8,128)(2,1)S(1)} %get-tuple-element.60.rs, ...), custom_call_target="tpu_custom_call" | custom-call | flops 1000000 | bytes 1000000 | tf_op jit(solution)/shard_map/sweep/pallas_call | solution.py:306
  59.3 0.1 add_dynamic-update-slice_fusion
  59.4 2.3 %collective-permute-start.10 = (f32[8,128,128]{2,1,0:T(8,128)S(1)}, f32[8,128,128]{2,1,0:T(8,128)S(1)}, u32[]{:S(2)}, u32[]{:S(2)}) collective-permute-start(f32[8,128,128]{2,1,0:T(8,128)S(1)} %add_dynamic-update-slice_fusion), channel_id=1, source_target_pairs={{0,40},{32,0},{8,32},{40,8},{1,41},{33,1},{9,33},{41,9},{2,42},{34... | collective-permute-start | bytes 1572872 | tf_op jit(solution)/shard_map/ppermute | solution.py:390
  61.7 0.1 add_dynamic-update-slice_fusion.1
  61.8 0.1 collective-permute-start.8
  61.8 6.8 %sweep.5 = f32[8,128,128]{2,1,0:T(8,128)S(1)} custom-call(s32[2]{0:T(128)S(1)} %pad_add_fusion.place, s32[8,8,128]{2,1,0:T(8,128)S(1)} %get-tuple-element.69.lists, bf16[32,128,32]{2,1,0:T(8,128)(2,1)S(1)} %get-tuple-element.59.rf, bf16[32,128,32]{2,1,0:T(8,128)(2,1)S(1)} %get-tuple-element.60.rs, bf16[32,128,48]{2,1,0:T(8,128)(2,1)S(1)} %get-tuple-element.61.rd, ...), custom_call_target="tpu_custom_call" | custom-call | flops 1000000 | bytes 1000000 | tf_op jit(solution)/shard_map/sweep/pallas_call | solution.py:306
  68.6 5.1 %collective-permute-done.10 = f32[8,128,128]{2,1,0:T(8,128)S(1)} collective-permute-done((f32[8,128,128]{2,1,0:T(8,128)S(1)}, f32[8,128,128]{2,1,0:T(8,128)S(1)}, u32[]{:S(2)}, u32[]{:S(2)}) %collective-permute-start.10) | collective-permute-done | bytes 524320 | tf_op jit(solution)/shard_map/ppermute | solution.py:390
  73.7 4.1 %collective-permute-done.8 = f32[8,128,128]{2,1,0:T(8,128)S(1)} collective-permute-done((f32[8,128,128]{2,1,0:T(8,128)S(1)}, f32[8,128,128]{2,1,0:T(8,128)S(1)}, u32[]{:S(2)}, u32[]{:S(2)}) %collective-permute-start.8) | collective-permute-done | bytes 524320 | tf_op jit(solution)/shard_map/ppermute | solution.py:390
  77.8 0.1 add_add_fusion
  77.9 21.9 %all_to_all.10 = f32[8,128,128]{2,1,0:T(8,128)S(1)} all-to-all(f32[8,128,128]{2,1,0:T(8,128)S(1)} %add_add_fusion), channel_id=1, replica_groups=mesh['x'=4,'yl'=2,'c'=2,'yh'=2,'z'=8] {'z'}, dimensions={0} | all-to-all | bytes 1048576 | tf_op jit(solution)/shard_map/all_to_all | solution.py:400
  99.9 0.6 add.35
  (9 shorter events, 0.1 us)
Async XLA Ops:
  1.8 26.8 %collective-permute-start.3 = (f32[1096,128]{1,0:T(8,128)S(1)}, f32[1096,128]{1,0:T(8,128)S(1)}, u32[]{:S(2)}, u32[]{:S(2)}) collective-permute-start(f32[1096,128]{1,0:T(8,128)S(1)} %get-tuple-element.54.refs_0_.refs_6_), channel_id=1, source_target_pairs={{0,16},{16,0},{1,17},{17,1},{2,18},{18,2},{3,19},{19,3},{4,20},{20... | collective-permute-start | bytes 1683464 | tf_op jit(solution)/shard_map/ppermute | solution.py:374
  1.9 35.4 %collective-permute-start.2 = (f32[1096,128]{1,0:T(8,128)S(1)}, f32[1096,128]{1,0:T(8,128)S(1)}, u32[]{:S(2)}, u32[]{:S(2)}) collective-permute-start(f32[1096,128]{1,0:T(8,128)S(1)} %get-tuple-element.54.refs_0_.refs_6_), channel_id=1, source_target_pairs={{0,128},{64,192},{128,0},{192,64},{1,129},{65,193},{129,1},{193,65... | collective-permute-start | bytes 1683464 | tf_op jit(solution)/shard_map/ppermute | solution.py:371
  3.4 33.9 %collective-permute-start.1 = (f32[1096,128]{1,0:T(8,128)S(1)}, f32[1096,128]{1,0:T(8,128)S(1)}, u32[]{:S(2)}, u32[]{:S(2)}) collective-permute-start(f32[1096,128]{1,0:T(8,128)S(1)} %get-tuple-element.54.refs_0_.refs_6_), channel_id=1, source_target_pairs={{0,192},{64,0},{128,64},{192,128},{1,193},{65,1},{129,65},{193,129... | collective-permute-start | bytes 1683464 | tf_op jit(solution)/shard_map/ppermute | solution.py:371
  5.0 32.3 %collective-permute-start = (f32[1096,128]{1,0:T(8,128)S(1)}, f32[1096,128]{1,0:T(8,128)S(1)}, u32[]{:S(2)}, u32[]{:S(2)}) collective-permute-start(f32[1096,128]{1,0:T(8,128)S(1)} %get-tuple-element.54.refs_0_.refs_6_), channel_id=1, source_target_pairs={{0,64},{64,128},{128,192},{192,0},{1,65},{65,129},{129,193},{193,1... | collective-permute-start | bytes 1683464 | tf_op jit(solution)/shard_map/ppermute | solution.py:371
  6.6 22.0 %all-to-all-start = ((f32[32,8,128]{2,1,0:T(8,128)}), f32[32,8,128]{2,1,0:T(8,128)S(1)}, u32[]{:S(2)}, u32[]{:S(2)}) async-start(f32[32,8,128]{2,1,0:T(8,128)} %get-tuple-element.55), calls=%async_computation | async-start | bytes 262144 | tf_op jit(solution)/shard_map/all_to_all | solution.py:381
  37.3 2.0 %collective-permute-start.4 = (f32[1096,128]{1,0:T(8,128)S(1)}, f32[1096,128]{1,0:T(8,128)S(1)}, u32[]{:S(2)}, u32[]{:S(2)}) collective-permute-start(f32[1096,128]{1,0:T(8,128)S(1)} %collective-permute-done.refs_0_), channel_id=1, source_target_pairs={{0,16},{16,0},{1,17},{17,1},{2,18},{18,2},{3,19},{19,3},{4,20},{20... | collective-permute-start | bytes 1683464 | tf_op jit(solution)/shard_map/ppermute | solution.py:374
  37.4 2.8 %collective-permute-start.5 = (f32[1096,128]{1,0:T(8,128)S(1)}, f32[1096,128]{1,0:T(8,128)S(1)}, u32[]{:S(2)}, u32[]{:S(2)}) collective-permute-start(f32[1096,128]{1,0:T(8,128)S(1)} %collective-permute-done.1.refs_1_), channel_id=1, source_target_pairs={{0,16},{16,0},{1,17},{17,1},{2,18},{18,2},{3,19},{19,3},{4,20},{20... | collective-permute-start | bytes 1683464 | tf_op jit(solution)/shard_map/ppermute | solution.py:374
  37.9 3.1 %collective-permute-start.6 = (f32[1096,128]{1,0:T(8,128)S(1)}, f32[1096,128]{1,0:T(8,128)S(1)}, u32[]{:S(2)}, u32[]{:S(2)}) collective-permute-start(f32[1096,128]{1,0:T(8,128)S(1)} %collective-permute-done.2.refs_2_), channel_id=1, source_target_pairs={{0,16},{16,0},{1,17},{17,1},{2,18},{18,2},{3,19},{19,3},{4,20},{20... | collective-permute-start | bytes 1683464 | tf_op jit(solution)/shard_map/ppermute | solution.py:374
  47.7 11.6 %collective-permute-start.9 = (f32[4,128,128]{2,1,0:T(8,128)S(1)}, f32[4,128,128]{2,1,0:T(8,128)S(1)}, u32[]{:S(2)}, u32[]{:S(2)}) collective-permute-start(f32[4,128,128]{2,1,0:T(8,128)S(1)} %get-tuple-element.78), channel_id=1, source_target_pairs={{0,40},{32,0},{8,32},{40,8},{1,41},{33,1},{9,33},{41,9},{2,42},{34... | collective-permute-start | bytes 786440 | tf_op jit(solution)/shard_map/ppermute | solution.py:390
  47.8 13.9 %collective-permute-start.7 = (f32[4,128,128]{2,1,0:T(8,128)S(1)}, f32[4,128,128]{2,1,0:T(8,128)S(1)}, u32[]{:S(2)}, u32[]{:S(2)}) collective-permute-start(f32[4,128,128]{2,1,0:T(8,128)S(1)} %get-tuple-element.76), channel_id=1, source_target_pairs={{0,32},{32,8},{8,40},{40,0},{1,33},{33,9},{9,41},{41,1},{2,34},{34... | collective-permute-start | bytes 786440 | tf_op jit(solution)/shard_map/ppermute | solution.py:390
  59.4 14.3 %collective-permute-start.10 = (f32[8,128,128]{2,1,0:T(8,128)S(1)}, f32[8,128,128]{2,1,0:T(8,128)S(1)}, u32[]{:S(2)}, u32[]{:S(2)}) collective-permute-start(f32[8,128,128]{2,1,0:T(8,128)S(1)} %add_dynamic-update-slice_fusion), channel_id=1, source_target_pairs={{0,40},{32,0},{8,32},{40,8},{1,41},{33,1},{9,33},{41,9},{2,42},{34... | collective-permute-start | bytes 1572872 | tf_op jit(solution)/shard_map/ppermute | solution.py:390
  61.8 16.1 %collective-permute-start.8 = (f32[8,128,128]{2,1,0:T(8,128)S(1)}, f32[8,128,128]{2,1,0:T(8,128)S(1)}, u32[]{:S(2)}, u32[]{:S(2)}) collective-permute-start(f32[8,128,128]{2,1,0:T(8,128)S(1)} %add_dynamic-update-slice_fusion.1), channel_id=1, source_target_pairs={{0,32},{32,8},{8,40},{40,0},{1,33},{33,9},{9,41},{41,1},{2,34},{34... | collective-permute-start | bytes 1572872 | tf_op jit(solution)/shard_map/ppermute | solution.py:390
  68.6 31.2 %copy-start = (f32[128,128]{1,0:T(8,128)S(1)}, f32[128,128]{1,0:T(8,128)}, u32[]{:S(2)}) copy-start(f32[128,128]{1,0:T(8,128)} %param.21) | copy-start | bytes 196612

commit v9 on v8

--- a/solution.py
+++ b/solution.py
@@ -146,7 +146,7 @@
         recv_tile[j] = tile
 
 
-def src_prep_kernel(count, *refs):
+def src_prep_kernel(count, place, *refs):
     packed = refs[:count]
     sf, ss, sd, em, lists = refs[count:]
     mats = selections(1)
@@ -155,7 +155,13 @@
             em[d * SB + k] = ref[k * BS : (k + 1) * BS, :].astype(jnp.bfloat16)
         tiles = [ref[FLUX + k * TILE : FLUX + (k + 1) * TILE, :] for k in range(SB)]
         q = split_pieces(jnp.concatenate(tiles, axis=1))
-        lists[d] = ref[LISTS : LISTS + TILE, :].astype(jnp.int32)
+        tile = ref[LISTS : LISTS + TILE, :]
+        tile = pltpu.roll(tile, 0, 1, stride=LANES, stride_axis=0)
+        tile = pltpu.roll(tile, (GROUP - place[1]) * LANES, 1)
+        row = lax.broadcasted_iota(jnp.int32, tile.shape, 0)
+        lane = lax.broadcasted_iota(jnp.int32, tile.shape, 1)
+        side = jnp.sum(jnp.where((lane >> 4) == row, tile, 0.0), axis=0, keepdims=True)
+        lists[d : d + 1, :] = side.astype(jnp.int32)
         for m, out in zip(mats, (sf, ss, sd)):
             values = dot(m, q).astype(jnp.bfloat16)
             for k in range(SB):
@@ -181,6 +187,8 @@
 def sweep_kernel(count, distances, added, sizes, place, lists, rf, rs, rd, sf, ss, sd, em, *refs):
     before, outs = refs[:added], refs[added:-3]
     out, ids, owner = refs[-3:]
+    if len(sizes) == 1:
+        out = outs[0]
     blocks = len(distances) * NZ
     null = sf.shape[0] - 1
     slots = count * CAP // 2
@@ -200,14 +208,13 @@
 
     def one_block(j, n):
         block = block_of(j)
-        row = (block >> 4) * CAP
-        lane = place[1] * LANES + (block & (LANES - 1))
+        lane = (block >> 4) * CAP * LANES + (block & (LANES - 1))
         for t in range(slots):
             owner[n // 2 + t] = j
         for d in range(count):
             used = []
             for c in range(CAP):
-                value = lists[d, row + c, lane]
+                value = lists[d, lane + c * LANES]
                 ids[n + c] = d * SB + value
                 used.append((value >= 0).astype(jnp.int32))
             n = n + ((used[0] + used[1]) + (used[2] + used[3]))
@@ -251,10 +258,11 @@
     long = units // UNROLL
     run(0, UNROLL, long)
     run(long * UNROLL, TAIL, pl.cdiv(units - long * UNROLL, TAIL))
-    at = 0
-    for ref, size in zip(outs, sizes):
-        ref[...] = out[at : at + size]
-        at += size
+    if len(sizes) > 1:
+        at = 0
+        for ref, size in zip(outs, sizes):
+            ref[...] = out[at : at + size]
+            at += size
 
 
 VMEM_SPEC = pl.BlockSpec(memory_space=pltpu.VMEM)
@@ -267,7 +275,7 @@
     return jax.ShapeDtypeStruct(shape, BF16)
 
 
-def src_prep(packed):
+def src_prep(place, packed):
     count = len(packed)
     rows = count * SB + 1
     return pl.pallas_call(
@@ -277,14 +285,14 @@
             bf16_shape(rows, KS, BS),
             bf16_shape(rows, KD, BS),
             bf16_shape(rows, BS, BS),
-            jax.ShapeDtypeStruct((count, 8, BS), jnp.int32),
+            jax.ShapeDtypeStruct((count, BS), jnp.int32),
         ],
-        in_specs=[VMEM_SPEC] * count,
+        in_specs=[SMEM_SPEC] + [VMEM_SPEC] * count,
         out_specs=[VMEM_SPEC] * 5,
         name="src_prep",
         compiler_params=PARAMS,
         cost_estimate=pl.CostEstimate(flops=10**6, bytes_accessed=10**6, transcendentals=0),
-    )(*packed)
+    )(place, *packed)
 
 
 def recv_prep(tiles):
@@ -309,7 +317,7 @@
         in_specs=[SMEM_SPEC] * 2 + [VMEM_SPEC] * (7 + len(before)),
         out_specs=[VMEM_SPEC] * len(sizes),
         scratch_shapes=[
-            pltpu.VMEM((blocks, BS, BS), jnp.float32),
+            pltpu.VMEM((blocks if len(sizes) > 1 else 1, BS, BS), jnp.float32),
             pltpu.SMEM((blocks * count * CAP + 4 * UNROLL,), jnp.int32),
             pltpu.SMEM((blocks * count * CAP // 2 + count * CAP + 2 * UNROLL,), jnp.int32),
         ],
@@ -382,9 +390,9 @@
 
     own, tiles = lax.optimization_barrier((own, tiles))
     recv = recv_prep(tiles)
-    (begun,) = sweep(place, (1, 2, 3), recv, src_prep([mine, own]), 2)
+    (begun,) = sweep(place, (1, 2, 3), recv, src_prep(place, [mine, own]), 2)
     *far, begun = lax.optimization_barrier((*far, begun))
-    src = src_prep(far + [other_core(block) for block in far] + [mine, own])
+    src = src_prep(place, far + [other_core(block) for block in far] + [mine, own])
 
     def along_y(block, distance):
         return lax.ppermute(block, ("yl", "yh"), y_route(distance))

time: 102 us -> 101 us (level)
  starting transfers between devices: 21.5 us -> 26.9 us
  waiting for transfers between devices: 22.6 us -> 18.1 us
    ppermute x4, starting transfers between devices: 4.49 us -> 9.89 us  [along_y(): return lax.ppermute(block, ('yl', 'yh'), y_route(distance))]
    ppermute x4, waiting for transfers between devices: 9.19 us -> 4.7 us  [along_y(): return lax.ppermute(block, ('yl', 'yh'), y_route(distance))]
    pallas_call x4, Pallas kernels: 29.3 us -> 27.3 us  [sweep(): pl.pallas_call(functools.partial(sweep_kernel, count, distances, len(befo...]
    pallas_call x2, Pallas kernels: 1.2 us -> 2.29 us  [src_prep(): pl.pallas_call(functools.partial(src_prep_kernel, count), out_shape=[bf16...]
  transfers between devices with their start and end apart: 12 -> 12, of which waited for: 6 -> 5; matrix products, arithmetic and copies ran while one was open for 0% -> 0% of each run, Pallas kernels for 25% -> 24%
where the time goes in v9:
time: 101 us; the launch traced here: 99.4 us
  Pallas kernels  32.4 us (32%)
  starting transfers between devices  26.9 us (27%)
  blocking collectives  20.9 us (21%)
  waiting for transfers between devices  18.1 us (18%)
    pallas_call x4, Pallas kernels, sweep(): pl.pallas_call(functools.partial(sweep_kernel, count, distances, len(befo...  27.3 us
    all_to_all x1, blocking collectives, shards(): pieces = lax.all_to_all(total, 'z', 0, 0, tiled=True)  20.9 us
    all_to_all x1, starting transfers between devices, shards(): tiles = lax.all_to_all(recv_tile, ('yl', 'yh', 'z'), 0, 0, tiled=True)  11.5 us
    all_to_all x1, waiting for transfers between devices, shards(): tiles = lax.all_to_all(recv_tile, ('yl', 'yh', 'z'), 0, 0, tiled=True)  10.4 us
    ppermute x4, starting transfers between devices, along_y(): return lax.ppermute(block, ('yl', 'yh'), y_route(distance))  9.89 us
    ppermute x3, starting transfers between devices, along_x(): lax.ppermute(block, 'x', [(i, (i + distance) % NX) for i in range(NX)])  4.73 us
    ppermute x4, waiting for transfers between devices, along_y(): return lax.ppermute(block, ('yl', 'yh'), y_route(distance))  4.7 us
    ppermute x4, waiting for transfers between devices, other_core(): return lax.ppermute(block, 'c', [(0, 1), (1, 0)])  2.96 us
  transfers between devices with their start and end apart: 12, of which 5 were waited for; matrix products, arithmetic and copies ran while one was open for 0% of the time, Pallas kernels for 24%

profile of v9, /device:TPU:6, one launch (start us, length us, event | category | flops | bytes accessed | tf_op | source)
XLA Modules:
  0.0 99.4 jit_solution(7166912634153878616)
XLA Ops:
  0.0 1.8 %pack.1 = (f32[1096,128]{1,0:T(8,128)S(1)}, f32[32,8,128]{2,1,0:T(8,128)}) custom-call(bf16[1024,128]{1,0:T(8,128)(2,1)} %refs_0_.1, f32[3,1024]{1,0:T(4,128)} %refs_1_.1, f32[2,1024]{1,0:T(2,128)} %refs_2_.1, f32[1,1024]{1,0:T(1,128)} %bitcast.10, f32[1,1024]{1,0:T(1,128)} %bitcast.11, s32[16,4,16]{2,1,0:T(4,128)} %bitcast.8, s32[16,16]{1,0:T(8,128)} %bitcast.9, ...), custom_call_target="tpu_custom_call" | custom-call | flops 1000000 | bytes 1000000 | tf_op jit(solution)/shard_map/pack/pallas_call | solution.py:331
  1.8 0.1 collective-permute-start.3
  1.9 1.5 %collective-permute-start.2 = (f32[1096,128]{1,0:T(8,128)S(1)}, f32[1096,128]{1,0:T(8,128)S(1)}, u32[]{:S(2)}, u32[]{:S(2)}) collective-permute-start(f32[1096,128]{1,0:T(8,128)S(1)} %get-tuple-element.54.refs_0_.refs_6_), channel_id=1, source_target_pairs={{0,128},{64,192},{128,0},{192,64},{1,129},{65,193},{129,1},{193,65... | collective-permute-start | bytes 1683464 | tf_op jit(solution)/shard_map/ppermute | solution.py:379
  3.4 1.7 %collective-permute-start.1 = (f32[1096,128]{1,0:T(8,128)S(1)}, f32[1096,128]{1,0:T(8,128)S(1)}, u32[]{:S(2)}, u32[]{:S(2)}) collective-permute-start(f32[1096,128]{1,0:T(8,128)S(1)} %get-tuple-element.54.refs_0_.refs_6_), channel_id=1, source_target_pairs={{0,192},{64,0},{128,64},{192,128},{1,193},{65,1},{129,65},{193,129... | collective-permute-start | bytes 1683464 | tf_op jit(solution)/shard_map/ppermute | solution.py:379
  5.0 1.6 %collective-permute-start = (f32[1096,128]{1,0:T(8,128)S(1)}, f32[1096,128]{1,0:T(8,128)S(1)}, u32[]{:S(2)}, u32[]{:S(2)}) collective-permute-start(f32[1096,128]{1,0:T(8,128)S(1)} %get-tuple-element.54.refs_0_.refs_6_), channel_id=1, source_target_pairs={{0,64},{64,128},{128,192},{192,0},{1,65},{65,129},{129,193},{193,1... | collective-permute-start | bytes 1683464 | tf_op jit(solution)/shard_map/ppermute | solution.py:379
  6.6 11.5 %all-to-all-start = ((f32[32,8,128]{2,1,0:T(8,128)}), f32[32,8,128]{2,1,0:T(8,128)S(1)}, u32[]{:S(2)}, u32[]{:S(2)}) async-start(f32[32,8,128]{2,1,0:T(8,128)} %get-tuple-element.55), calls=%async_computation | async-start | bytes 262144 | tf_op jit(solution)/shard_map/all_to_all | solution.py:389
  18.1 0.1 pad_add_fusion.place
  18.2 10.4 %all-to-all-done.tiles = f32[32,8,128]{2,1,0:T(8,128)S(1)} async-done(((f32[32,8,128]{2,1,0:T(8,128)}), f32[32,8,128]{2,1,0:T(8,128)S(1)}, u32[]{:S(2)}, u32[]{:S(2)}) %all-to-all-start) | async-done | bytes 131104 | tf_op jit(solution)/shard_map/all_to_all | solution.py:389
  28.6 1.1 %recv_prep.1 = (bf16[32,128,32]{2,1,0:T(8,128)(2,1)S(1)}, bf16[32,128,32]{2,1,0:T(8,128)(2,1)S(1)}, bf16[32,128,48]{2,1,0:T(8,128)(2,1)S(1)}) custom-call(f32[32,8,128]{2,1,0:T(8,128)S(1)} %all-to-all-done.tiles), custom_call_target="tpu_custom_call" | custom-call | flops 1000000 | bytes 1000000 | tf_op jit(solution)/shard_map/recv_prep/pallas_call | solution.py:299
  29.7 0.9 src_prep.2
  30.6 4.8 %sweep.4.refs_0_ = f32[24,128,128]{2,1,0:T(8,128)S(1)} custom-call(s32[2]{0:T(128)S(1)} %pad_add_fusion.place, s32[2,128]{1,0:T(2,128)S(1)} %get-tuple-element.57.lists, bf16[32,128,32]{2,1,0:T(8,128)(2,1)S(1)} %get-tuple-element.59.rf, bf16[32,128,32]{2,1,0:T(8,128)(2,1)S(1)} %get-tuple-element.60.rs, bf16[32,128,48]{2,1,0:T(8,128)(2,1)S(1)} %get-tuple-element.61.rd, ...), custom_call_target="tpu_custom_call" | custom-call | flops 1000000 | bytes 1000000 | tf_op jit(solution)/shard_map/sweep/pallas_call | solution.py:314
  35.5 0.1 collective-permute-start.4
  35.6 0.5 collective-permute-start.5
  36.1 0.1 collective-permute-start.6
  36.2 1.4 %collective-permute-done.4.refs_3_ = f32[1096,128]{1,0:T(8,128)S(1)} collective-permute-done((f32[1096,128]{1,0:T(8,128)S(1)}, f32[1096,128]{1,0:T(8,128)S(1)}, u32[]{:S(2)}, u32[]{:S(2)}) %collective-permute-start.4) | collective-permute-done | bytes 561184 | tf_op jit(solution)/shard_map/ppermute | solution.py:382
  37.5 0.8 collective-permute-done.5.refs_4_
  38.3 0.8 collective-permute-done.6.refs_5_
  39.1 1.4 %src_prep.3 = (bf16[65,32,128]{2,1,0:T(8,128)(2,1)S(1)}, bf16[65,32,128]{2,1,0:T(8,128)(2,1)S(1)}, bf16[65,48,128]{2,1,0:T(8,128)(2,1)S(1)}, bf16[65,128,128]{2,1,0:T(8,128)(2,1)S(1)}, s32[8,128]{1,0:T(8,128)S(1)}) custom-call(s32[2]{0:T(128)S(1)} %pad_add_fusion.place, f32[1096,128]{1,0:T(8,128)S(1)} %collective-permute-done.refs_0_, ...), custom_call_target="tpu_custom_call" | custom-call | flops 1000000 | bytes 1000000 | tf_op jit(solution)/shard_map/src_prep/pallas_call | solution.py:281
  40.5 5.4 %sweep.7 = (f32[4,128,128]{2,1,0:T(8,128)S(1)}, f32[4,128,128]{2,1,0:T(8,128)S(1)}) custom-call(s32[2]{0:T(128)S(1)} %pad_add_fusion.place, s32[8,128]{1,0:T(8,128)S(1)} %get-tuple-element.69.lists, bf16[32,128,32]{2,1,0:T(8,128)(2,1)S(1)} %get-tuple-element.59.rf, bf16[32,128,32]{2,1,0:T(8,128)(2,1)S(1)} %get-tuple-element.60.rs, ...), custom_call_target="tpu_custom_call" | custom-call | flops 1000000 | bytes 1000000 | tf_op jit(solution)/shard_map/sweep/pallas_call | solution.py:314
  46.0 0.1 collective-permute-start.9
  46.1 5.3 %collective-permute-start.7 = (f32[4,128,128]{2,1,0:T(8,128)S(1)}, f32[4,128,128]{2,1,0:T(8,128)S(1)}, u32[]{:S(2)}, u32[]{:S(2)}) collective-permute-start(f32[4,128,128]{2,1,0:T(8,128)S(1)} %get-tuple-element.76), channel_id=1, source_target_pairs={{0,32},{32,8},{8,40},{40,0},{1,33},{33,9},{9,41},{41,1},{2,34},{34... | collective-permute-start | bytes 786440 | tf_op jit(solution)/shard_map/ppermute | solution.py:398
  51.4 9.9 %sweep.6 = (f32[8,128,128]{2,1,0:T(8,128)S(1)}, f32[8,128,128]{2,1,0:T(8,128)S(1)}) custom-call(s32[2]{0:T(128)S(1)} %pad_add_fusion.place, s32[8,128]{1,0:T(8,128)S(1)} %get-tuple-element.69.lists, bf16[32,128,32]{2,1,0:T(8,128)(2,1)S(1)} %get-tuple-element.59.rf, bf16[32,128,32]{2,1,0:T(8,128)(2,1)S(1)} %get-tuple-element.60.rs, ...), custom_call_target="tpu_custom_call" | custom-call | flops 1000000 | bytes 1000000 | tf_op jit(solution)/shard_map/sweep/pallas_call | solution.py:314
  61.3 0.1 add_dynamic-update-slice_fusion
  61.4 0.1 collective-permute-start.10
  61.5 0.1 add_dynamic-update-slice_fusion.1
  61.5 4.4 %collective-permute-start.8 = (f32[8,128,128]{2,1,0:T(8,128)S(1)}, f32[8,128,128]{2,1,0:T(8,128)S(1)}, u32[]{:S(2)}, u32[]{:S(2)}) collective-permute-start(f32[8,128,128]{2,1,0:T(8,128)S(1)} %add_dynamic-update-slice_fusion.1), channel_id=1, source_target_pairs={{0,32},{32,8},{8,40},{40,0},{1,33},{33,9},{9,41},{41,1},{2,34},{34... | collective-permute-start | bytes 1572872 | tf_op jit(solution)/shard_map/ppermute | solution.py:398
  66.0 7.1 %sweep.5 = f32[8,128,128]{2,1,0:T(8,128)S(1)} custom-call(s32[2]{0:T(128)S(1)} %pad_add_fusion.place, s32[8,128]{1,0:T(8,128)S(1)} %get-tuple-element.69.lists, bf16[32,128,32]{2,1,0:T(8,128)(2,1)S(1)} %get-tuple-element.59.rf, bf16[32,128,32]{2,1,0:T(8,128)(2,1)S(1)} %get-tuple-element.60.rs, bf16[32,128,48]{2,1,0:T(8,128)(2,1)S(1)} %get-tuple-element.61.rd, ...), custom_call_target="tpu_custom_call" | custom-call | flops 1000000 | bytes 1000000 | tf_op jit(solution)/shard_map/sweep/pallas_call | solution.py:314
  73.0 0.0 copy-start
  73.1 4.7 %collective-permute-done.10 = f32[8,128,128]{2,1,0:T(8,128)S(1)} collective-permute-done((f32[8,128,128]{2,1,0:T(8,128)S(1)}, f32[8,128,128]{2,1,0:T(8,128)S(1)}, u32[]{:S(2)}, u32[]{:S(2)}) %collective-permute-start.10) | collective-permute-done | bytes 524320 | tf_op jit(solution)/shard_map/ppermute | solution.py:398
  77.7 0.1 add_add_fusion
  77.9 20.9 %all_to_all.10 = f32[8,128,128]{2,1,0:T(8,128)S(1)} all-to-all(f32[8,128,128]{2,1,0:T(8,128)S(1)} %add_add_fusion), channel_id=1, replica_groups=mesh['x'=4,'yl'=2,'c'=2,'yh'=2,'z'=8] {'z'}, dimensions={0} | all-to-all | bytes 1048576 | tf_op jit(solution)/shard_map/all_to_all | solution.py:408
  98.8 0.6 add.35
  (9 shorter events, 0.1 us)
Async XLA Ops:
  1.8 26.8 %collective-permute-start.3 = (f32[1096,128]{1,0:T(8,128)S(1)}, f32[1096,128]{1,0:T(8,128)S(1)}, u32[]{:S(2)}, u32[]{:S(2)}) collective-permute-start(f32[1096,128]{1,0:T(8,128)S(1)} %get-tuple-element.54.refs_0_.refs_6_), channel_id=1, source_target_pairs={{0,16},{16,0},{1,17},{17,1},{2,18},{18,2},{3,19},{19,3},{4,20},{20... | collective-permute-start | bytes 1683464 | tf_op jit(solution)/shard_map/ppermute | solution.py:382
  1.9 33.5 %collective-permute-start.2 = (f32[1096,128]{1,0:T(8,128)S(1)}, f32[1096,128]{1,0:T(8,128)S(1)}, u32[]{:S(2)}, u32[]{:S(2)}) collective-permute-start(f32[1096,128]{1,0:T(8,128)S(1)} %get-tuple-element.54.refs_0_.refs_6_), channel_id=1, source_target_pairs={{0,128},{64,192},{128,0},{192,64},{1,129},{65,193},{129,1},{193,65... | collective-permute-start | bytes 1683464 | tf_op jit(solution)/shard_map/ppermute | solution.py:379
  3.4 32.1 %collective-permute-start.1 = (f32[1096,128]{1,0:T(8,128)S(1)}, f32[1096,128]{1,0:T(8,128)S(1)}, u32[]{:S(2)}, u32[]{:S(2)}) collective-permute-start(f32[1096,128]{1,0:T(8,128)S(1)} %get-tuple-element.54.refs_0_.refs_6_), channel_id=1, source_target_pairs={{0,192},{64,0},{128,64},{192,128},{1,193},{65,1},{129,65},{193,129... | collective-permute-start | bytes 1683464 | tf_op jit(solution)/shard_map/ppermute | solution.py:379
  5.0 30.4 %collective-permute-start = (f32[1096,128]{1,0:T(8,128)S(1)}, f32[1096,128]{1,0:T(8,128)S(1)}, u32[]{:S(2)}, u32[]{:S(2)}) collective-permute-start(f32[1096,128]{1,0:T(8,128)S(1)} %get-tuple-element.54.refs_0_.refs_6_), channel_id=1, source_target_pairs={{0,64},{64,128},{128,192},{192,0},{1,65},{65,129},{129,193},{193,1... | collective-permute-start | bytes 1683464 | tf_op jit(solution)/shard_map/ppermute | solution.py:379
  6.6 22.0 %all-to-all-start = ((f32[32,8,128]{2,1,0:T(8,128)}), f32[32,8,128]{2,1,0:T(8,128)S(1)}, u32[]{:S(2)}, u32[]{:S(2)}) async-start(f32[32,8,128]{2,1,0:T(8,128)} %get-tuple-element.55), calls=%async_computation | async-start | bytes 262144 | tf_op jit(solution)/shard_map/all_to_all | solution.py:389
  35.5 2.0 %collective-permute-start.4 = (f32[1096,128]{1,0:T(8,128)S(1)}, f32[1096,128]{1,0:T(8,128)S(1)}, u32[]{:S(2)}, u32[]{:S(2)}) collective-permute-start(f32[1096,128]{1,0:T(8,128)S(1)} %collective-permute-done.refs_0_), channel_id=1, source_target_pairs={{0,16},{16,0},{1,17},{17,1},{2,18},{18,2},{3,19},{19,3},{4,20},{20... | collective-permute-start | bytes 1683464 | tf_op jit(solution)/shard_map/ppermute | solution.py:382
  35.6 2.8 %collective-permute-start.5 = (f32[1096,128]{1,0:T(8,128)S(1)}, f32[1096,128]{1,0:T(8,128)S(1)}, u32[]{:S(2)}, u32[]{:S(2)}) collective-permute-start(f32[1096,128]{1,0:T(8,128)S(1)} %collective-permute-done.1.refs_1_), channel_id=1, source_target_pairs={{0,16},{16,0},{1,17},{17,1},{2,18},{18,2},{3,19},{19,3},{4,20},{20... | collective-permute-start | bytes 1683464 | tf_op jit(solution)/shard_map/ppermute | solution.py:382
  36.1 3.1 %collective-permute-start.6 = (f32[1096,128]{1,0:T(8,128)S(1)}, f32[1096,128]{1,0:T(8,128)S(1)}, u32[]{:S(2)}, u32[]{:S(2)}) collective-permute-start(f32[1096,128]{1,0:T(8,128)S(1)} %collective-permute-done.2.refs_2_), channel_id=1, source_target_pairs={{0,16},{16,0},{1,17},{17,1},{2,18},{18,2},{3,19},{19,3},{4,20},{20... | collective-permute-start | bytes 1683464 | tf_op jit(solution)/shard_map/ppermute | solution.py:382
  46.0 15.3 %collective-permute-start.9 = (f32[4,128,128]{2,1,0:T(8,128)S(1)}, f32[4,128,128]{2,1,0:T(8,128)S(1)}, u32[]{:S(2)}, u32[]{:S(2)}) collective-permute-start(f32[4,128,128]{2,1,0:T(8,128)S(1)} %get-tuple-element.78), channel_id=1, source_target_pairs={{0,40},{32,0},{8,32},{40,8},{1,41},{33,1},{9,33},{41,9},{2,42},{34... | collective-permute-start | bytes 786440 | tf_op jit(solution)/shard_map/ppermute | solution.py:398
  46.1 15.4 %collective-permute-start.7 = (f32[4,128,128]{2,1,0:T(8,128)S(1)}, f32[4,128,128]{2,1,0:T(8,128)S(1)}, u32[]{:S(2)}, u32[]{:S(2)}) collective-permute-start(f32[4,128,128]{2,1,0:T(8,128)S(1)} %get-tuple-element.76), channel_id=1, source_target_pairs={{0,32},{32,8},{8,40},{40,0},{1,33},{33,9},{9,41},{41,1},{2,34},{34... | collective-permute-start | bytes 786440 | tf_op jit(solution)/shard_map/ppermute | solution.py:398
  61.4 16.4 %collective-permute-start.10 = (f32[8,128,128]{2,1,0:T(8,128)S(1)}, f32[8,128,128]{2,1,0:T(8,128)S(1)}, u32[]{:S(2)}, u32[]{:S(2)}) collective-permute-start(f32[8,128,128]{2,1,0:T(8,128)S(1)} %add_dynamic-update-slice_fusion), channel_id=1, source_target_pairs={{0,40},{32,0},{8,32},{40,8},{1,41},{33,1},{9,33},{41,9},{2,42},{34... | collective-permute-start | bytes 1572872 | tf_op jit(solution)/shard_map/ppermute | solution.py:398
  61.5 16.2 %collective-permute-start.8 = (f32[8,128,128]{2,1,0:T(8,128)S(1)}, f32[8,128,128]{2,1,0:T(8,128)S(1)}, u32[]{:S(2)}, u32[]{:S(2)}) collective-permute-start(f32[8,128,128]{2,1,0:T(8,128)S(1)} %add_dynamic-update-slice_fusion.1), channel_id=1, source_target_pairs={{0,32},{32,8},{8,40},{40,0},{1,33},{33,9},{9,41},{41,1},{2,34},{34... | collective-permute-start | bytes 1572872 | tf_op jit(solution)/shard_map/ppermute | solution.py:398
  73.0 25.7 %copy-start = (f32[128,128]{1,0:T(8,128)S(1)}, f32[128,128]{1,0:T(8,128)}, u32[]{:S(2)}) copy-start(f32[128,128]{1,0:T(8,128)} %param.21) | copy-start | bytes 196612

commit v10 on v9

--- a/solution.py
+++ b/solution.py
@@ -136,8 +136,9 @@
             slab = ((k // NC) * NYL + yl) * NC + k % NC
             live = slot < counts[slab : slab + 1, :]
             marked = jnp.where(live, lists[slab], -1).astype(jnp.float32)
-            rows = slice(LISTS + yl * CAP, LISTS + (yl + 1) * CAP)
-            packed[rows, k * LANES : (k + 1) * LANES] = marked
+            for c in range(CAP):
+                at = (yl * CAP + c) * LANES
+                packed[LISTS + k : LISTS + k + 1, at : at + LANES] = marked[c : c + 1, :]
     rows = [recv_pos[a : a + 1, :] - CENTRE for a in range(3)]
     rows += direction(recv_angles[...])
     rows += [jnp.zeros((2, BS), jnp.float32)]
@@ -155,13 +156,7 @@
             em[d * SB + k] = ref[k * BS : (k + 1) * BS, :].astype(jnp.bfloat16)
         tiles = [ref[FLUX + k * TILE : FLUX + (k + 1) * TILE, :] for k in range(SB)]
         q = split_pieces(jnp.concatenate(tiles, axis=1))
-        tile = ref[LISTS : LISTS + TILE, :]
-        tile = pltpu.roll(tile, 0, 1, stride=LANES, stride_axis=0)
-        tile = pltpu.roll(tile, (GROUP - place[1]) * LANES, 1)
-        row = lax.broadcasted_iota(jnp.int32, tile.shape, 0)
-        lane = lax.broadcasted_iota(jnp.int32, tile.shape, 1)
-        side = jnp.sum(jnp.where((lane >> 4) == row, tile, 0.0), axis=0, keepdims=True)
-        lists[d : d + 1, :] = side.astype(jnp.int32)
+        lists[d : d + 1, :] = ref[pl.ds(LISTS + place[1], 1), :].astype(jnp.int32)
         for m, out in zip(mats, (sf, ss, sd)):
             values = dot(m, q).astype(jnp.bfloat16)
             for k in range(SB):

time: 101 us -> 101 us (level); the launches traced: 99.4 us -> 101 us
  starting transfers between devices: 26.9 us -> 21.3 us
  blocking collectives: 20.9 us -> 26.3 us
  Pallas kernels: 32.4 us -> 33.9 us
    ppermute x4, starting transfers between devices: 9.89 us -> 4.26 us  [along_y(): return lax.ppermute(block, ('yl', 'yh'), y_route(distance))]
    all_to_all x1, blocking collectives: 20.9 us -> 26.3 us  [shards(): pieces = lax.all_to_all(total, 'z', 0, 0, tiled=True)]
    pallas_call x4, Pallas kernels: 27.3 us -> 28.7 us  [sweep(): pl.pallas_call(functools.partial(sweep_kernel, count, distances, len(befo...]
  transfers between devices with their start and end apart: 12 -> 12, of which waited for: 5 -> 6; matrix products, arithmetic and copies ran while one was open for 0% -> 0% of each run, Pallas kernels for 24% -> 24%
where the time goes in v10:
time: 101 us
  Pallas kernels  33.9 us (34%)
  blocking collectives  26.3 us (26%)
  starting transfers between devices  21.3 us (21%)
  waiting for transfers between devices  18.9 us (19%)
    pallas_call x4, Pallas kernels, sweep(): pl.pallas_call(functools.partial(sweep_kernel, count, distances, len(befo...  28.7 us
    all_to_all x1, blocking collectives, shards(): pieces = lax.all_to_all(total, 'z', 0, 0, tiled=True)  26.3 us
    all_to_all x1, starting transfers between devices, shards(): tiles = lax.all_to_all(recv_tile, ('yl', 'yh', 'z'), 0, 0, tiled=True)  11.5 us
    all_to_all x1, waiting for transfers between devices, shards(): tiles = lax.all_to_all(recv_tile, ('yl', 'yh', 'z'), 0, 0, tiled=True)  10.4 us
    ppermute x4, waiting for transfers between devices, along_y(): return lax.ppermute(block, ('yl', 'yh'), y_route(distance))  5.54 us
    ppermute x3, starting transfers between devices, along_x(): lax.ppermute(block, 'x', [(i, (i + distance) % NX) for i in range(NX)])  4.73 us
    ppermute x4, starting transfers between devices, along_y(): return lax.ppermute(block, ('yl', 'yh'), y_route(distance))  4.26 us
    ppermute x4, waiting for transfers between devices, other_core(): return lax.ppermute(block, 'c', [(0, 1), (1, 0)])  2.96 us
  transfers between devices with their start and end apart: 12, of which 6 were waited for; matrix products, arithmetic and copies ran while one was open for 0% of the time, Pallas kernels for 24%

profile of v10, /device:TPU:6, one launch (start us, length us, event | category | flops | bytes accessed | tf_op | source)
XLA Modules:
  0.0 101.5 jit_solution(3929031134486827323)
XLA Ops:
  0.0 1.8 %pack.1 = (f32[1096,128]{1,0:T(8,128)S(1)}, f32[32,8,128]{2,1,0:T(8,128)}) custom-call(bf16[1024,128]{1,0:T(8,128)(2,1)} %refs_0_.1, f32[3,1024]{1,0:T(4,128)} %refs_1_.1, f32[2,1024]{1,0:T(2,128)} %refs_2_.1, f32[1,1024]{1,0:T(1,128)} %bitcast.10, f32[1,1024]{1,0:T(1,128)} %bitcast.11, s32[16,4,16]{2,1,0:T(4,128)} %bitcast.8, s32[16,16]{1,0:T(8,128)} %bitcast.9, ...), custom_call_target="tpu_custom_call" | custom-call | flops 1000000 | bytes 1000000 | tf_op jit(solution)/shard_map/pack/pallas_call | solution.py:326
  1.8 0.1 collective-permute-start.3
  1.9 1.5 %collective-permute-start.2 = (f32[1096,128]{1,0:T(8,128)S(1)}, f32[1096,128]{1,0:T(8,128)S(1)}, u32[]{:S(2)}, u32[]{:S(2)}) collective-permute-start(f32[1096,128]{1,0:T(8,128)S(1)} %get-tuple-element.54.refs_0_.refs_6_), channel_id=1, source_target_pairs={{0,128},{64,192},{128,0},{192,64},{1,129},{65,193},{129,1},{193,65... | collective-permute-start | bytes 1683464 | tf_op jit(solution)/shard_map/ppermute | solution.py:374
  3.4 1.7 %collective-permute-start.1 = (f32[1096,128]{1,0:T(8,128)S(1)}, f32[1096,128]{1,0:T(8,128)S(1)}, u32[]{:S(2)}, u32[]{:S(2)}) collective-permute-start(f32[1096,128]{1,0:T(8,128)S(1)} %get-tuple-element.54.refs_0_.refs_6_), channel_id=1, source_target_pairs={{0,192},{64,0},{128,64},{192,128},{1,193},{65,1},{129,65},{193,129... | collective-permute-start | bytes 1683464 | tf_op jit(solution)/shard_map/ppermute | solution.py:374
  5.1 1.6 %collective-permute-start = (f32[1096,128]{1,0:T(8,128)S(1)}, f32[1096,128]{1,0:T(8,128)S(1)}, u32[]{:S(2)}, u32[]{:S(2)}) collective-permute-start(f32[1096,128]{1,0:T(8,128)S(1)} %get-tuple-element.54.refs_0_.refs_6_), channel_id=1, source_target_pairs={{0,64},{64,128},{128,192},{192,0},{1,65},{65,129},{129,193},{193,1... | collective-permute-start | bytes 1683464 | tf_op jit(solution)/shard_map/ppermute | solution.py:374
  6.6 11.5 %all-to-all-start = ((f32[32,8,128]{2,1,0:T(8,128)}), f32[32,8,128]{2,1,0:T(8,128)S(1)}, u32[]{:S(2)}, u32[]{:S(2)}) async-start(f32[32,8,128]{2,1,0:T(8,128)} %get-tuple-element.55), calls=%async_computation | async-start | bytes 262144 | tf_op jit(solution)/shard_map/all_to_all | solution.py:384
  18.2 0.1 pad_add_fusion.place
  18.2 10.4 %all-to-all-done.tiles = f32[32,8,128]{2,1,0:T(8,128)S(1)} async-done(((f32[32,8,128]{2,1,0:T(8,128)}), f32[32,8,128]{2,1,0:T(8,128)S(1)}, u32[]{:S(2)}, u32[]{:S(2)}) %all-to-all-start) | async-done | bytes 131104 | tf_op jit(solution)/shard_map/all_to_all | solution.py:384
  28.6 1.1 %recv_prep.1 = (bf16[32,128,32]{2,1,0:T(8,128)(2,1)S(1)}, bf16[32,128,32]{2,1,0:T(8,128)(2,1)S(1)}, bf16[32,128,48]{2,1,0:T(8,128)(2,1)S(1)}) custom-call(f32[32,8,128]{2,1,0:T(8,128)S(1)} %all-to-all-done.tiles), custom_call_target="tpu_custom_call" | custom-call | flops 1000000 | bytes 1000000 | tf_op jit(solution)/shard_map/recv_prep/pallas_call | solution.py:294
  29.7 0.9 src_prep.2
  30.6 6.3 %sweep.4.refs_0_ = f32[24,128,128]{2,1,0:T(8,128)S(1)} custom-call(s32[2]{0:T(128)S(1)} %pad_add_fusion.place, s32[2,128]{1,0:T(2,128)S(1)} %get-tuple-element.57.lists, bf16[32,128,32]{2,1,0:T(8,128)(2,1)S(1)} %get-tuple-element.59.rf, bf16[32,128,32]{2,1,0:T(8,128)(2,1)S(1)} %get-tuple-element.60.rs, bf16[32,128,48]{2,1,0:T(8,128)(2,1)S(1)} %get-tuple-element.61.rd, ...), custom_call_target="tpu_custom_call" | custom-call | flops 1000000 | bytes 1000000 | tf_op jit(solution)/shard_map/sweep/pallas_call | solution.py:309
  36.9 0.1 collective-permute-start.4
  37.0 0.5 collective-permute-start.5
  37.5 0.1 collective-permute-start.6
  37.6 1.4 %collective-permute-done.4.refs_3_ = f32[1096,128]{1,0:T(8,128)S(1)} collective-permute-done((f32[1096,128]{1,0:T(8,128)S(1)}, f32[1096,128]{1,0:T(8,128)S(1)}, u32[]{:S(2)}, u32[]{:S(2)}) %collective-permute-start.4) | collective-permute-done | bytes 561184 | tf_op jit(solution)/shard_map/ppermute | solution.py:377
  39.0 0.8 collective-permute-done.5.refs_4_
  39.8 0.8 collective-permute-done.6.refs_5_
  40.6 1.4 %src_prep.3 = (bf16[65,32,128]{2,1,0:T(8,128)(2,1)S(1)}, bf16[65,32,128]{2,1,0:T(8,128)(2,1)S(1)}, bf16[65,48,128]{2,1,0:T(8,128)(2,1)S(1)}, bf16[65,128,128]{2,1,0:T(8,128)(2,1)S(1)}, s32[8,128]{1,0:T(8,128)S(1)}) custom-call(s32[2]{0:T(128)S(1)} %pad_add_fusion.place, f32[1096,128]{1,0:T(8,128)S(1)} %collective-permute-done.refs_0_, ...), custom_call_target="tpu_custom_call" | custom-call | flops 1000000 | bytes 1000000 | tf_op jit(solution)/shard_map/src_prep/pallas_call | solution.py:276
  42.0 6.2 %sweep.7 = (f32[4,128,128]{2,1,0:T(8,128)S(1)}, f32[4,128,128]{2,1,0:T(8,128)S(1)}) custom-call(s32[2]{0:T(128)S(1)} %pad_add_fusion.place, s32[8,128]{1,0:T(8,128)S(1)} %get-tuple-element.69.lists, bf16[32,128,32]{2,1,0:T(8,128)(2,1)S(1)} %get-tuple-element.59.rf, bf16[32,128,32]{2,1,0:T(8,128)(2,1)S(1)} %get-tuple-element.60.rs, ...), custom_call_target="tpu_custom_call" | custom-call | flops 1000000 | bytes 1000000 | tf_op jit(solution)/shard_map/sweep/pallas_call | solution.py:309
  48.2 0.1 collective-permute-start.9
  48.2 2.0 %collective-permute-start.7 = (f32[4,128,128]{2,1,0:T(8,128)S(1)}, f32[4,128,128]{2,1,0:T(8,128)S(1)}, u32[]{:S(2)}, u32[]{:S(2)}) collective-permute-start(f32[4,128,128]{2,1,0:T(8,128)S(1)} %get-tuple-element.76), channel_id=1, source_target_pairs={{0,32},{32,8},{8,40},{40,0},{1,33},{33,9},{9,41},{41,1},{2,34},{34... | collective-permute-start | bytes 786440 | tf_op jit(solution)/shard_map/ppermute | solution.py:393
  50.3 9.2 %sweep.6 = (f32[8,128,128]{2,1,0:T(8,128)S(1)}, f32[8,128,128]{2,1,0:T(8,128)S(1)}) custom-call(s32[2]{0:T(128)S(1)} %pad_add_fusion.place, s32[8,128]{1,0:T(8,128)S(1)} %get-tuple-element.69.lists, bf16[32,128,32]{2,1,0:T(8,128)(2,1)S(1)} %get-tuple-element.59.rf, bf16[32,128,32]{2,1,0:T(8,128)(2,1)S(1)} %get-tuple-element.60.rs, ...), custom_call_target="tpu_custom_call" | custom-call | flops 1000000 | bytes 1000000 | tf_op jit(solution)/shard_map/sweep/pallas_call | solution.py:309
  59.5 0.1 add_dynamic-update-slice_fusion
  59.6 0.1 collective-permute-start.10
  59.7 0.1 add_dynamic-update-slice_fusion.1
  59.7 2.1 %collective-permute-start.8 = (f32[8,128,128]{2,1,0:T(8,128)S(1)}, f32[8,128,128]{2,1,0:T(8,128)S(1)}, u32[]{:S(2)}, u32[]{:S(2)}) collective-permute-start(f32[8,128,128]{2,1,0:T(8,128)S(1)} %add_dynamic-update-slice_fusion.1), channel_id=1, source_target_pairs={{0,32},{32,8},{8,40},{40,0},{1,33},{33,9},{9,41},{41,1},{2,34},{34... | collective-permute-start | bytes 1572872 | tf_op jit(solution)/shard_map/ppermute | solution.py:393
  61.8 7.1 %sweep.5 = f32[8,128,128]{2,1,0:T(8,128)S(1)} custom-call(s32[2]{0:T(128)S(1)} %pad_add_fusion.place, s32[8,128]{1,0:T(8,128)S(1)} %get-tuple-element.69.lists, bf16[32,128,32]{2,1,0:T(8,128)(2,1)S(1)} %get-tuple-element.59.rf, bf16[32,128,32]{2,1,0:T(8,128)(2,1)S(1)} %get-tuple-element.60.rs, bf16[32,128,48]{2,1,0:T(8,128)(2,1)S(1)} %get-tuple-element.61.rd, ...), custom_call_target="tpu_custom_call" | custom-call | flops 1000000 | bytes 1000000 | tf_op jit(solution)/shard_map/sweep/pallas_call | solution.py:309
  68.9 4.2 %collective-permute-done.10 = f32[8,128,128]{2,1,0:T(8,128)S(1)} collective-permute-done((f32[8,128,128]{2,1,0:T(8,128)S(1)}, f32[8,128,128]{2,1,0:T(8,128)S(1)}, u32[]{:S(2)}, u32[]{:S(2)}) %collective-permute-start.10) | collective-permute-done | bytes 524320 | tf_op jit(solution)/shard_map/ppermute | solution.py:393
  73.0 1.4 %collective-permute-done.8 = f32[8,128,128]{2,1,0:T(8,128)S(1)} collective-permute-done((f32[8,128,128]{2,1,0:T(8,128)S(1)}, f32[8,128,128]{2,1,0:T(8,128)S(1)}, u32[]{:S(2)}, u32[]{:S(2)}) %collective-permute-start.8) | collective-permute-done | bytes 524320 | tf_op jit(solution)/shard_map/ppermute | solution.py:393
  74.4 0.1 add_add_fusion
  74.5 26.3 %all_to_all.10 = f32[8,128,128]{2,1,0:T(8,128)S(1)} all-to-all(f32[8,128,128]{2,1,0:T(8,128)S(1)} %add_add_fusion), channel_id=1, replica_groups=mesh['x'=4,'yl'=2,'c'=2,'yh'=2,'z'=8] {'z'}, dimensions={0} | all-to-all | bytes 1048576 | tf_op jit(solution)/shard_map/all_to_all | solution.py:403
  100.8 0.6 add.35
  (9 shorter events, 0.1 us)
Async XLA Ops:
  1.8 26.8 %collective-permute-start.3 = (f32[1096,128]{1,0:T(8,128)S(1)}, f32[1096,128]{1,0:T(8,128)S(1)}, u32[]{:S(2)}, u32[]{:S(2)}) collective-permute-start(f32[1096,128]{1,0:T(8,128)S(1)} %get-tuple-element.54.refs_0_.refs_6_), channel_id=1, source_target_pairs={{0,16},{16,0},{1,17},{17,1},{2,18},{18,2},{3,19},{19,3},{4,20},{20... | collective-permute-start | bytes 1683464 | tf_op jit(solution)/shard_map/ppermute | solution.py:377
  1.9 35.0 %collective-permute-start.2 = (f32[1096,128]{1,0:T(8,128)S(1)}, f32[1096,128]{1,0:T(8,128)S(1)}, u32[]{:S(2)}, u32[]{:S(2)}) collective-permute-start(f32[1096,128]{1,0:T(8,128)S(1)} %get-tuple-element.54.refs_0_.refs_6_), channel_id=1, source_target_pairs={{0,128},{64,192},{128,0},{192,64},{1,129},{65,193},{129,1},{193,65... | collective-permute-start | bytes 1683464 | tf_op jit(solution)/shard_map/ppermute | solution.py:374
  3.4 33.5 %collective-permute-start.1 = (f32[1096,128]{1,0:T(8,128)S(1)}, f32[1096,128]{1,0:T(8,128)S(1)}, u32[]{:S(2)}, u32[]{:S(2)}) collective-permute-start(f32[1096,128]{1,0:T(8,128)S(1)} %get-tuple-element.54.refs_0_.refs_6_), channel_id=1, source_target_pairs={{0,192},{64,0},{128,64},{192,128},{1,193},{65,1},{129,65},{193,129... | collective-permute-start | bytes 1683464 | tf_op jit(solution)/shard_map/ppermute | solution.py:374
  5.1 31.8 %collective-permute-start = (f32[1096,128]{1,0:T(8,128)S(1)}, f32[1096,128]{1,0:T(8,128)S(1)}, u32[]{:S(2)}, u32[]{:S(2)}) collective-permute-start(f32[1096,128]{1,0:T(8,128)S(1)} %get-tuple-element.54.refs_0_.refs_6_), channel_id=1, source_target_pairs={{0,64},{64,128},{128,192},{192,0},{1,65},{65,129},{129,193},{193,1... | collective-permute-start | bytes 1683464 | tf_op jit(solution)/shard_map/ppermute | solution.py:374
  6.6 22.0 %all-to-all-start = ((f32[32,8,128]{2,1,0:T(8,128)}), f32[32,8,128]{2,1,0:T(8,128)S(1)}, u32[]{:S(2)}, u32[]{:S(2)}) async-start(f32[32,8,128]{2,1,0:T(8,128)} %get-tuple-element.55), calls=%async_computation | async-start | bytes 262144 | tf_op jit(solution)/shard_map/all_to_all | solution.py:384
  36.9 2.0 %collective-permute-start.4 = (f32[1096,128]{1,0:T(8,128)S(1)}, f32[1096,128]{1,0:T(8,128)S(1)}, u32[]{:S(2)}, u32[]{:S(2)}) collective-permute-start(f32[1096,128]{1,0:T(8,128)S(1)} %collective-permute-done.refs_0_), channel_id=1, source_target_pairs={{0,16},{16,0},{1,17},{17,1},{2,18},{18,2},{3,19},{19,3},{4,20},{20... | collective-permute-start | bytes 1683464 | tf_op jit(solution)/shard_map/ppermute | solution.py:377
  37.0 2.8 %collective-permute-start.5 = (f32[1096,128]{1,0:T(8,128)S(1)}, f32[1096,128]{1,0:T(8,128)S(1)}, u32[]{:S(2)}, u32[]{:S(2)}) collective-permute-start(f32[1096,128]{1,0:T(8,128)S(1)} %collective-permute-done.1.refs_1_), channel_id=1, source_target_pairs={{0,16},{16,0},{1,17},{17,1},{2,18},{18,2},{3,19},{19,3},{4,20},{20... | collective-permute-start | bytes 1683464 | tf_op jit(solution)/shard_map/ppermute | solution.py:377
  37.5 3.1 %collective-permute-start.6 = (f32[1096,128]{1,0:T(8,128)S(1)}, f32[1096,128]{1,0:T(8,128)S(1)}, u32[]{:S(2)}, u32[]{:S(2)}) collective-permute-start(f32[1096,128]{1,0:T(8,128)S(1)} %collective-permute-done.2.refs_2_), channel_id=1, source_target_pairs={{0,16},{16,0},{1,17},{17,1},{2,18},{18,2},{3,19},{19,3},{4,20},{20... | collective-permute-start | bytes 1683464 | tf_op jit(solution)/shard_map/ppermute | solution.py:377
  48.2 11.3 %collective-permute-start.9 = (f32[4,128,128]{2,1,0:T(8,128)S(1)}, f32[4,128,128]{2,1,0:T(8,128)S(1)}, u32[]{:S(2)}, u32[]{:S(2)}) collective-permute-start(f32[4,128,128]{2,1,0:T(8,128)S(1)} %get-tuple-element.78), channel_id=1, source_target_pairs={{0,40},{32,0},{8,32},{40,8},{1,41},{33,1},{9,33},{41,9},{2,42},{34... | collective-permute-start | bytes 786440 | tf_op jit(solution)/shard_map/ppermute | solution.py:393
  48.2 11.4 %collective-permute-start.7 = (f32[4,128,128]{2,1,0:T(8,128)S(1)}, f32[4,128,128]{2,1,0:T(8,128)S(1)}, u32[]{:S(2)}, u32[]{:S(2)}) collective-permute-start(f32[4,128,128]{2,1,0:T(8,128)S(1)} %get-tuple-element.76), channel_id=1, source_target_pairs={{0,32},{32,8},{8,40},{40,0},{1,33},{33,9},{9,41},{41,1},{2,34},{34... | collective-permute-start | bytes 786440 | tf_op jit(solution)/shard_map/ppermute | solution.py:393
  59.6 13.5 %collective-permute-start.10 = (f32[8,128,128]{2,1,0:T(8,128)S(1)}, f32[8,128,128]{2,1,0:T(8,128)S(1)}, u32[]{:S(2)}, u32[]{:S(2)}) collective-permute-start(f32[8,128,128]{2,1,0:T(8,128)S(1)} %add_dynamic-update-slice_fusion), channel_id=1, source_target_pairs={{0,40},{32,0},{8,32},{40,8},{1,41},{33,1},{9,33},{41,9},{2,42},{34... | collective-permute-start | bytes 1572872 | tf_op jit(solution)/shard_map/ppermute | solution.py:393
  59.7 14.7 %collective-permute-start.8 = (f32[8,128,128]{2,1,0:T(8,128)S(1)}, f32[8,128,128]{2,1,0:T(8,128)S(1)}, u32[]{:S(2)}, u32[]{:S(2)}) collective-permute-start(f32[8,128,128]{2,1,0:T(8,128)S(1)} %add_dynamic-update-slice_fusion.1), channel_id=1, source_target_pairs={{0,32},{32,8},{8,40},{40,0},{1,33},{33,9},{9,41},{41,1},{2,34},{34... | collective-permute-start | bytes 1572872 | tf_op jit(solution)/shard_map/ppermute | solution.py:393
  68.9 32.0 %copy-start = (f32[128,128]{1,0:T(8,128)S(1)}, f32[128,128]{1,0:T(8,128)}, u32[]{:S(2)}) copy-start(f32[128,128]{1,0:T(8,128)} %param.21) | copy-start | bytes 196612

commit v11 on v10

--- a/solution.py
+++ b/solution.py
@@ -147,7 +147,15 @@
         recv_tile[j] = tile
 
 
-def src_prep_kernel(count, place, *refs):
+def own_y():
+    return lax.axis_index("yh") * NYL + lax.axis_index("yl")
+
+
+def own_list():
+    return lax.axis_index("x") * NC + lax.axis_index("c")
+
+
+def src_prep_kernel(count, *refs):
     packed = refs[:count]
     sf, ss, sd, em, lists = refs[count:]
     mats = selections(1)
@@ -156,7 +164,7 @@
             em[d * SB + k] = ref[k * BS : (k + 1) * BS, :].astype(jnp.bfloat16)
         tiles = [ref[FLUX + k * TILE : FLUX + (k + 1) * TILE, :] for k in range(SB)]
         q = split_pieces(jnp.concatenate(tiles, axis=1))
-        lists[d : d + 1, :] = ref[pl.ds(LISTS + place[1], 1), :].astype(jnp.int32)
+        lists[d : d + 1, :] = ref[pl.ds(LISTS + own_list(), 1), :].astype(jnp.int32)
         for m, out in zip(mats, (sf, ss, sd)):
             values = dot(m, q).astype(jnp.bfloat16)
             for k in range(SB):
@@ -179,7 +187,7 @@
             ).astype(jnp.bfloat16)
 
 
-def sweep_kernel(count, distances, added, sizes, place, lists, rf, rs, rd, sf, ss, sd, em, *refs):
+def sweep_kernel(count, distances, added, sizes, lists, rf, rs, rd, sf, ss, sd, em, *refs):
     before, outs = refs[:added], refs[added:-3]
     out, ids, owner = refs[-3:]
     if len(sizes) == 1:
@@ -192,7 +200,7 @@
         ahead = distances[0]
         for at in range(1, len(distances)):
             ahead = jnp.where(j >= at * NZ, distances[at], ahead)
-        target = (place[0] + ahead) & (NY - 1)
+        target = (own_y() + ahead) & (NY - 1)
         return ((target & (NYL - 1)) * NYH + (target >> 1)) * NZ + (j & (NZ - 1))
 
     for j in range(blocks):
@@ -270,7 +278,7 @@
     return jax.ShapeDtypeStruct(shape, BF16)
 
 
-def src_prep(place, packed):
+def src_prep(packed):
     count = len(packed)
     rows = count * SB + 1
     return pl.pallas_call(
@@ -282,12 +290,12 @@
             bf16_shape(rows, BS, BS),
             jax.ShapeDtypeStruct((count, BS), jnp.int32),
         ],
-        in_specs=[SMEM_SPEC] + [VMEM_SPEC] * count,
+        in_specs=[VMEM_SPEC] * count,
         out_specs=[VMEM_SPEC] * 5,
         name="src_prep",
         compiler_params=PARAMS,
         cost_estimate=pl.CostEstimate(flops=10**6, bytes_accessed=10**6, transcendentals=0),
-    )(place, *packed)
+    )(*packed)
 
 
 def recv_prep(tiles):
@@ -302,14 +310,14 @@
     )(tiles)
 
 
-def sweep(place, distances, recv, src, count, *before, sizes=None):
+def sweep(distances, recv, src, count, *before, sizes=None):
     *src, lists = src
     blocks = len(distances) * NZ
     sizes = sizes or (blocks,)
     return pl.pallas_call(
         functools.partial(sweep_kernel, count, distances, len(before), sizes),
         out_shape=[jax.ShapeDtypeStruct((size, BS, BS), jnp.float32) for size in sizes],
-        in_specs=[SMEM_SPEC] * 2 + [VMEM_SPEC] * (7 + len(before)),
+        in_specs=[SMEM_SPEC] + [VMEM_SPEC] * (7 + len(before)),
         out_specs=[VMEM_SPEC] * len(sizes),
         scratch_shapes=[
             pltpu.VMEM((blocks if len(sizes) > 1 else 1, BS, BS), jnp.float32),
@@ -319,7 +327,7 @@
         name="sweep",
         compiler_params=PARAMS,
         cost_estimate=pl.CostEstimate(flops=10**6, bytes_accessed=10**6, transcendentals=0),
-    )(place, lists, *recv, *src, *before)
+    )(lists, *recv, *src, *before)
 
 
 def pack(*operands):
@@ -376,8 +384,6 @@
     def other_core(block):
         return lax.ppermute(block, "c", [(0, 1), (1, 0)])
 
-    my_y = lax.axis_index("yh") * NYL + lax.axis_index("yl")
-    place = jnp.stack([my_y, lax.axis_index("x") * NC + lax.axis_index("c")]).astype(jnp.int32)
     far = [along_x(mine, distance) for distance in (1, 3, 2)]
     own = other_core(mine)
 
@@ -385,20 +391,20 @@
 
     own, tiles = lax.optimization_barrier((own, tiles))
     recv = recv_prep(tiles)
-    (begun,) = sweep(place, (1, 2, 3), recv, src_prep(place, [mine, own]), 2)
+    (begun,) = sweep((1, 2, 3), recv, src_prep([mine, own]), 2)
     *far, begun = lax.optimization_barrier((*far, begun))
-    src = src_prep(place, far + [other_core(block) for block in far] + [mine, own])
+    src = src_prep(far + [other_core(block) for block in far] + [mine, own])
 
     def along_y(block, distance):
         return lax.ppermute(block, ("yl", "yh"), y_route(distance))
 
     half = NZ // 2
-    parts = sweep(place, (2,), recv, src, GROUP - 2, begun, sizes=(half, half))
+    parts = sweep((2,), recv, src, GROUP - 2, begun, sizes=(half, half))
     by_left, by_right = along_y(parts[0], 1), along_y(parts[1], 3)
-    ahead, behind = sweep(place, (1, 3), recv, src, GROUP - 2, begun, sizes=(NZ, NZ))
+    ahead, behind = sweep((1, 3), recv, src, GROUP - 2, begun, sizes=(NZ, NZ))
     ahead = along_y(ahead.at[:half].add(by_left), 1)
     behind = along_y(behind.at[half:].add(by_right), 3)
-    (total,) = sweep(place, (0,), recv, src, GROUP)
+    (total,) = sweep((0,), recv, src, GROUP)
     total = total + ahead + behind
     pieces = lax.all_to_all(total, "z", 0, 0, tiled=True)
     return direct + jnp.sum(pieces, axis=0)

time: 101 us -> 100 us (0.990); the launches traced: 101 us -> 98.6 us
  blocking collectives: 26.3 us -> 44.4 us
  starting transfers between devices: 21.3 us -> 9.79 us
  waiting for transfers between devices: 18.9 us -> 11.2 us
  Pallas kernels: 33.9 us -> 32.3 us
    all_to_all x0 -> x1, blocking collectives: none -> 21.8 us  [shards(): tiles = lax.all_to_all(recv_tile, ('yl', 'yh', 'z'), 0, 0, tiled=True)]
    all_to_all x1 -> x0, starting transfers between devices: 11.5 us -> none  [shards(): tiles = lax.all_to_all(recv_tile, ('yl', 'yh', 'z'), 0, 0, tiled=True)]
    all_to_all x1 -> x0, waiting for transfers between devices: 10.4 us -> none  [shards(): tiles = lax.all_to_all(recv_tile, ('yl', 'yh', 'z'), 0, 0, tiled=True)]
    all_to_all x1, blocking collectives: 26.3 us -> 22.6 us  [shards(): pieces = lax.all_to_all(total, 'z', 0, 0, tiled=True)]
    ppermute x4, waiting for transfers between devices: 5.54 us -> 8.19 us  [along_y(): return lax.ppermute(block, ('yl', 'yh'), y_route(distance))]
    pallas_call x2, Pallas kernels: 2.3 us -> 1.21 us  [src_prep(): pl.pallas_call(functools.partial(src_prep_kernel, count), out_shape=[bf16...]
  transfers between devices with their start and end apart: 12 -> 11, of which waited for: 6 -> 5; matrix products, arithmetic and copies ran while one was open for 0% -> 0% of each run, Pallas kernels for 24% -> 25%
where the time goes in v11:
time: 100 us; the launch traced here: 98.6 us
  blocking collectives  44.4 us (44%)
  Pallas kernels  32.3 us (32%)
  waiting for transfers between devices  11.2 us (11%)
  starting transfers between devices  9.79 us (10%)
    pallas_call x4, Pallas kernels, sweep(): pl.pallas_call(functools.partial(sweep_kernel, count, distances, len(befo...  28.7 us
    all_to_all x1, blocking collectives, shards(): pieces = lax.all_to_all(total, 'z', 0, 0, tiled=True)  22.6 us
    all_to_all x1, blocking collectives, shards(): tiles = lax.all_to_all(recv_tile, ('yl', 'yh', 'z'), 0, 0, tiled=True)  21.8 us
    ppermute x4, waiting for transfers between devices, along_y(): return lax.ppermute(block, ('yl', 'yh'), y_route(distance))  8.19 us
    ppermute x3, starting transfers between devices, along_x(): lax.ppermute(block, 'x', [(i, (i + distance) % NX) for i in range(NX)])  4.73 us
    ppermute x4, starting transfers between devices, along_y(): return lax.ppermute(block, ('yl', 'yh'), y_route(distance))  4.28 us
    ppermute x4, waiting for transfers between devices, other_core(): return lax.ppermute(block, 'c', [(0, 1), (1, 0)])  2.96 us
  transfers between devices with their start and end apart: 11, of which 5 were waited for; matrix products, arithmetic and copies ran while one was open for 0% of the time, Pallas kernels for 25%

profile of v11, /device:TPU:6, one launch (start us, length us, event | category | flops | bytes accessed | tf_op | source)
XLA Modules:
  0.0 98.6 jit_solution(12650019793683495724)
XLA Ops:
  0.0 1.2 %pack.1 = (f32[1096,128]{1,0:T(8,128)S(1)}, f32[32,8,128]{2,1,0:T(8,128)S(1)}) custom-call(bf16[1024,128]{1,0:T(8,128)(2,1)} %refs_0_.1, f32[3,1024]{1,0:T(4,128)} %refs_1_.1, f32[2,1024]{1,0:T(2,128)} %refs_2_.1, f32[1,1024]{1,0:T(1,128)} %bitcast.8, f32[1,1024]{1,0:T(1,128)} %bitcast.9, s32[16,4,16]{2,1,0:T(4,128)} %bitcast.6, s32[16,16]{1,0:T(8,128)} %bitcast.7, ...), custom_call_target="tpu_custom_call" | custom-call | flops 1000000 | bytes 1000000 | tf_op jit(solution)/shard_map/pack/pallas_call | solution.py:334
  1.2 0.1 collective-permute-start.3
  1.4 1.5 %collective-permute-start.2 = (f32[1096,128]{1,0:T(8,128)S(1)}, f32[1096,128]{1,0:T(8,128)S(1)}, u32[]{:S(2)}, u32[]{:S(2)}) collective-permute-start(f32[1096,128]{1,0:T(8,128)S(1)} %get-tuple-element.54.refs_0_.refs_6_), channel_id=1, source_target_pairs={{0,128},{64,192},{128,0},{192,64},{1,129},{65,193},{129,1},{193,65... | collective-permute-start | bytes 1683464 | tf_op jit(solution)/shard_map/ppermute | solution.py:382
  2.8 1.7 %collective-permute-start.1 = (f32[1096,128]{1,0:T(8,128)S(1)}, f32[1096,128]{1,0:T(8,128)S(1)}, u32[]{:S(2)}, u32[]{:S(2)}) collective-permute-start(f32[1096,128]{1,0:T(8,128)S(1)} %get-tuple-element.54.refs_0_.refs_6_), channel_id=1, source_target_pairs={{0,192},{64,0},{128,64},{192,128},{1,193},{65,1},{129,65},{193,129... | collective-permute-start | bytes 1683464 | tf_op jit(solution)/shard_map/ppermute | solution.py:382
  4.5 1.6 %collective-permute-start = (f32[1096,128]{1,0:T(8,128)S(1)}, f32[1096,128]{1,0:T(8,128)S(1)}, u32[]{:S(2)}, u32[]{:S(2)}) collective-permute-start(f32[1096,128]{1,0:T(8,128)S(1)} %get-tuple-element.54.refs_0_.refs_6_), channel_id=1, source_target_pairs={{0,64},{64,128},{128,192},{192,0},{1,65},{65,129},{129,193},{193,1... | collective-permute-start | bytes 1683464 | tf_op jit(solution)/shard_map/ppermute | solution.py:382
  6.1 21.8 %all_to_all.10.tiles = f32[32,8,128]{2,1,0:T(8,128)S(1)} all-to-all(f32[32,8,128]{2,1,0:T(8,128)S(1)} %get-tuple-element.55), channel_id=1, replica_groups=mesh['x'=4,'yl'=2,'c'=2,'yh'=2,'z'=8] {'yl','yh','z'}, dimensions={0} | all-to-all | bytes 262144 | tf_op jit(solution)/shard_map/all_to_all | solution.py:390
  27.8 0.0 collective-permute-done.3.refs_1_.refs_7_
  27.8 0.4 src_prep.2
  28.2 1.1 %recv_prep.1 = (bf16[32,128,32]{2,1,0:T(8,128)(2,1)S(1)}, bf16[32,128,32]{2,1,0:T(8,128)(2,1)S(1)}, bf16[32,128,48]{2,1,0:T(8,128)(2,1)S(1)}) custom-call(f32[32,8,128]{2,1,0:T(8,128)S(1)} %all_to_all.10.tiles), custom_call_target="tpu_custom_call" | custom-call | flops 1000000 | bytes 1000000 | tf_op jit(solution)/shard_map/recv_prep/pallas_call | solution.py:302
  29.3 7.4 %sweep.4.refs_0_ = f32[24,128,128]{2,1,0:T(8,128)S(1)} custom-call(s32[2,128]{1,0:T(2,128)S(1)} %get-tuple-element.57.lists, bf16[32,128,32]{2,1,0:T(8,128)(2,1)S(1)} %get-tuple-element.59.rf, bf16[32,128,32]{2,1,0:T(8,128)(2,1)S(1)} %get-tuple-element.60.rs, bf16[32,128,48]{2,1,0:T(8,128)(2,1)S(1)} %get-tuple-element.61.rd, ...), custom_call_target="tpu_custom_call" | custom-call | flops 1000000 | bytes 1000000 | tf_op jit(solution)/shard_map/sweep/pallas_call | solution.py:317
  36.7 0.1 collective-permute-start.4
  36.8 0.5 collective-permute-start.5
  37.3 0.1 collective-permute-start.6
  37.4 1.4 %collective-permute-done.4.refs_3_ = f32[1096,128]{1,0:T(8,128)S(1)} collective-permute-done((f32[1096,128]{1,0:T(8,128)S(1)}, f32[1096,128]{1,0:T(8,128)S(1)}, u32[]{:S(2)}, u32[]{:S(2)}) %collective-permute-start.4) | collective-permute-done | bytes 561184 | tf_op jit(solution)/shard_map/ppermute | solution.py:385
  38.8 0.8 collective-permute-done.5.refs_4_
  39.6 0.8 collective-permute-done.6.refs_5_
  40.4 0.8 src_prep.3
  41.3 5.5 %sweep.7 = (f32[4,128,128]{2,1,0:T(8,128)S(1)}, f32[4,128,128]{2,1,0:T(8,128)S(1)}) custom-call(s32[8,128]{1,0:T(8,128)S(1)} %get-tuple-element.69.lists, bf16[32,128,32]{2,1,0:T(8,128)(2,1)S(1)} %get-tuple-element.59.rf, bf16[32,128,32]{2,1,0:T(8,128)(2,1)S(1)} %get-tuple-element.60.rs, bf16[32,128,48]{2,1,0:T(8,128)(2,1)S(1)} %get-tuple-element.61.rd, ...), custom_call_target="tpu_custom_call" | custom-call | flops 1000000 | bytes 1000000 | tf_op jit(solution)/shard_map/sweep/pallas_call | solution.py:317
  46.7 0.1 collective-permute-start.9
  46.8 2.0 %collective-permute-start.7 = (f32[4,128,128]{2,1,0:T(8,128)S(1)}, f32[4,128,128]{2,1,0:T(8,128)S(1)}, u32[]{:S(2)}, u32[]{:S(2)}) collective-permute-start(f32[4,128,128]{2,1,0:T(8,128)S(1)} %get-tuple-element.76), channel_id=1, source_target_pairs={{0,32},{32,8},{8,40},{40,0},{1,33},{33,9},{9,41},{41,1},{2,34},{34... | collective-permute-start | bytes 786440 | tf_op jit(solution)/shard_map/ppermute | solution.py:399
  48.8 8.5 %sweep.6 = (f32[8,128,128]{2,1,0:T(8,128)S(1)}, f32[8,128,128]{2,1,0:T(8,128)S(1)}) custom-call(s32[8,128]{1,0:T(8,128)S(1)} %get-tuple-element.69.lists, bf16[32,128,32]{2,1,0:T(8,128)(2,1)S(1)} %get-tuple-element.59.rf, bf16[32,128,32]{2,1,0:T(8,128)(2,1)S(1)} %get-tuple-element.60.rs, bf16[32,128,48]{2,1,0:T(8,128)(2,1)S(1)} %get-tuple-element.61.rd, ...), custom_call_target="tpu_custom_call" | custom-call | flops 1000000 | bytes 1000000 | tf_op jit(solution)/shard_map/sweep/pallas_call | solution.py:317
  57.4 0.1 add_dynamic-update-slice_fusion
  57.4 2.1 %collective-permute-start.10 = (f32[8,128,128]{2,1,0:T(8,128)S(1)}, f32[8,128,128]{2,1,0:T(8,128)S(1)}, u32[]{:S(2)}, u32[]{:S(2)}) collective-permute-start(f32[8,128,128]{2,1,0:T(8,128)S(1)} %add_dynamic-update-slice_fusion), channel_id=1, source_target_pairs={{0,40},{32,0},{8,32},{40,8},{1,41},{33,1},{9,33},{41,9},{2,42},{34... | collective-permute-start | bytes 1572872 | tf_op jit(solution)/shard_map/ppermute | solution.py:399
  59.5 0.1 add_dynamic-update-slice_fusion.1
  59.6 0.1 collective-permute-start.8
  59.7 7.3 %sweep.5 = f32[8,128,128]{2,1,0:T(8,128)S(1)} custom-call(s32[8,128]{1,0:T(8,128)S(1)} %get-tuple-element.69.lists, bf16[32,128,32]{2,1,0:T(8,128)(2,1)S(1)} %get-tuple-element.59.rf, bf16[32,128,32]{2,1,0:T(8,128)(2,1)S(1)} %get-tuple-element.60.rs, bf16[32,128,48]{2,1,0:T(8,128)(2,1)S(1)} %get-tuple-element.61.rd, ...), custom_call_target="tpu_custom_call" | custom-call | flops 1000000 | bytes 1000000 | tf_op jit(solution)/shard_map/sweep/pallas_call | solution.py:317
  67.0 0.0 copy-start
  67.0 5.2 %collective-permute-done.10 = f32[8,128,128]{2,1,0:T(8,128)S(1)} collective-permute-done((f32[8,128,128]{2,1,0:T(8,128)S(1)}, f32[8,128,128]{2,1,0:T(8,128)S(1)}, u32[]{:S(2)}, u32[]{:S(2)}) %collective-permute-start.10) | collective-permute-done | bytes 524320 | tf_op jit(solution)/shard_map/ppermute | solution.py:399
  72.2 3.0 %collective-permute-done.8 = f32[8,128,128]{2,1,0:T(8,128)S(1)} collective-permute-done((f32[8,128,128]{2,1,0:T(8,128)S(1)}, f32[8,128,128]{2,1,0:T(8,128)S(1)}, u32[]{:S(2)}, u32[]{:S(2)}) %collective-permute-start.8) | collective-permute-done | bytes 524320 | tf_op jit(solution)/shard_map/ppermute | solution.py:399
  75.2 0.1 add_add_fusion
  75.3 22.6 %all_to_all.11 = f32[8,128,128]{2,1,0:T(8,128)S(1)} all-to-all(f32[8,128,128]{2,1,0:T(8,128)S(1)} %add_add_fusion), channel_id=1, replica_groups=mesh['x'=4,'yl'=2,'c'=2,'yh'=2,'z'=8] {'z'}, dimensions={0} | all-to-all | bytes 1048576 | tf_op jit(solution)/shard_map/all_to_all | solution.py:409
  98.0 0.6 add.27
  (7 shorter events, 0.0 us)
Async XLA Ops:
  1.2 26.6 %collective-permute-start.3 = (f32[1096,128]{1,0:T(8,128)S(1)}, f32[1096,128]{1,0:T(8,128)S(1)}, u32[]{:S(2)}, u32[]{:S(2)}) collective-permute-start(f32[1096,128]{1,0:T(8,128)S(1)} %get-tuple-element.54.refs_0_.refs_6_), channel_id=1, source_target_pairs={{0,16},{16,0},{1,17},{17,1},{2,18},{18,2},{3,19},{19,3},{4,20},{20... | collective-permute-start | bytes 1683464 | tf_op jit(solution)/shard_map/ppermute | solution.py:385
  1.4 35.4 %collective-permute-start.2 = (f32[1096,128]{1,0:T(8,128)S(1)}, f32[1096,128]{1,0:T(8,128)S(1)}, u32[]{:S(2)}, u32[]{:S(2)}) collective-permute-start(f32[1096,128]{1,0:T(8,128)S(1)} %get-tuple-element.54.refs_0_.refs_6_), channel_id=1, source_target_pairs={{0,128},{64,192},{128,0},{192,64},{1,129},{65,193},{129,1},{193,65... | collective-permute-start | bytes 1683464 | tf_op jit(solution)/shard_map/ppermute | solution.py:382
  2.8 33.9 %collective-permute-start.1 = (f32[1096,128]{1,0:T(8,128)S(1)}, f32[1096,128]{1,0:T(8,128)S(1)}, u32[]{:S(2)}, u32[]{:S(2)}) collective-permute-start(f32[1096,128]{1,0:T(8,128)S(1)} %get-tuple-element.54.refs_0_.refs_6_), channel_id=1, source_target_pairs={{0,192},{64,0},{128,64},{192,128},{1,193},{65,1},{129,65},{193,129... | collective-permute-start | bytes 1683464 | tf_op jit(solution)/shard_map/ppermute | solution.py:382
  4.5 32.2 %collective-permute-start = (f32[1096,128]{1,0:T(8,128)S(1)}, f32[1096,128]{1,0:T(8,128)S(1)}, u32[]{:S(2)}, u32[]{:S(2)}) collective-permute-start(f32[1096,128]{1,0:T(8,128)S(1)} %get-tuple-element.54.refs_0_.refs_6_), channel_id=1, source_target_pairs={{0,64},{64,128},{128,192},{192,0},{1,65},{65,129},{129,193},{193,1... | collective-permute-start | bytes 1683464 | tf_op jit(solution)/shard_map/ppermute | solution.py:382
  36.7 2.0 %collective-permute-start.4 = (f32[1096,128]{1,0:T(8,128)S(1)}, f32[1096,128]{1,0:T(8,128)S(1)}, u32[]{:S(2)}, u32[]{:S(2)}) collective-permute-start(f32[1096,128]{1,0:T(8,128)S(1)} %collective-permute-done.refs_0_), channel_id=1, source_target_pairs={{0,16},{16,0},{1,17},{17,1},{2,18},{18,2},{3,19},{19,3},{4,20},{20... | collective-permute-start | bytes 1683464 | tf_op jit(solution)/shard_map/ppermute | solution.py:385
  36.8 2.8 %collective-permute-start.5 = (f32[1096,128]{1,0:T(8,128)S(1)}, f32[1096,128]{1,0:T(8,128)S(1)}, u32[]{:S(2)}, u32[]{:S(2)}) collective-permute-start(f32[1096,128]{1,0:T(8,128)S(1)} %collective-permute-done.1.refs_1_), channel_id=1, source_target_pairs={{0,16},{16,0},{1,17},{17,1},{2,18},{18,2},{3,19},{19,3},{4,20},{20... | collective-permute-start | bytes 1683464 | tf_op jit(solution)/shard_map/ppermute | solution.py:385
  37.3 3.1 %collective-permute-start.6 = (f32[1096,128]{1,0:T(8,128)S(1)}, f32[1096,128]{1,0:T(8,128)S(1)}, u32[]{:S(2)}, u32[]{:S(2)}) collective-permute-start(f32[1096,128]{1,0:T(8,128)S(1)} %collective-permute-done.2.refs_2_), channel_id=1, source_target_pairs={{0,16},{16,0},{1,17},{17,1},{2,18},{18,2},{3,19},{19,3},{4,20},{20... | collective-permute-start | bytes 1683464 | tf_op jit(solution)/shard_map/ppermute | solution.py:385
  46.7 10.6 %collective-permute-start.9 = (f32[4,128,128]{2,1,0:T(8,128)S(1)}, f32[4,128,128]{2,1,0:T(8,128)S(1)}, u32[]{:S(2)}, u32[]{:S(2)}) collective-permute-start(f32[4,128,128]{2,1,0:T(8,128)S(1)} %get-tuple-element.78), channel_id=1, source_target_pairs={{0,40},{32,0},{8,32},{40,8},{1,41},{33,1},{9,33},{41,9},{2,42},{34... | collective-permute-start | bytes 786440 | tf_op jit(solution)/shard_map/ppermute | solution.py:399
  46.8 12.7 %collective-permute-start.7 = (f32[4,128,128]{2,1,0:T(8,128)S(1)}, f32[4,128,128]{2,1,0:T(8,128)S(1)}, u32[]{:S(2)}, u32[]{:S(2)}) collective-permute-start(f32[4,128,128]{2,1,0:T(8,128)S(1)} %get-tuple-element.76), channel_id=1, source_target_pairs={{0,32},{32,8},{8,40},{40,0},{1,33},{33,9},{9,41},{41,1},{2,34},{34... | collective-permute-start | bytes 786440 | tf_op jit(solution)/shard_map/ppermute | solution.py:399
  57.4 14.8 %collective-permute-start.10 = (f32[8,128,128]{2,1,0:T(8,128)S(1)}, f32[8,128,128]{2,1,0:T(8,128)S(1)}, u32[]{:S(2)}, u32[]{:S(2)}) collective-permute-start(f32[8,128,128]{2,1,0:T(8,128)S(1)} %add_dynamic-update-slice_fusion), channel_id=1, source_target_pairs={{0,40},{32,0},{8,32},{40,8},{1,41},{33,1},{9,33},{41,9},{2,42},{34... | collective-permute-start | bytes 1572872 | tf_op jit(solution)/shard_map/ppermute | solution.py:399
  59.6 15.6 %collective-permute-start.8 = (f32[8,128,128]{2,1,0:T(8,128)S(1)}, f32[8,128,128]{2,1,0:T(8,128)S(1)}, u32[]{:S(2)}, u32[]{:S(2)}) collective-permute-start(f32[8,128,128]{2,1,0:T(8,128)S(1)} %add_dynamic-update-slice_fusion.1), channel_id=1, source_target_pairs={{0,32},{32,8},{8,40},{40,0},{1,33},{33,9},{9,41},{41,1},{2,34},{34... | collective-permute-start | bytes 1572872 | tf_op jit(solution)/shard_map/ppermute | solution.py:399
  67.0 31.0 %copy-start = (f32[128,128]{1,0:T(8,128)S(1)}, f32[128,128]{1,0:T(8,128)}, u32[]{:S(2)}) copy-start(f32[128,128]{1,0:T(8,128)} %param.21) | copy-start | bytes 196612
